TPU v7x, 32 devices: a whole 2x2x4 slice. The times are simulated.
32 devices in a mesh: subtree: 8 (over z, core), front: 4 (over y, x).
Axes of the slice: x: 2, y: 2, z: 4, core: 2. Of those that a mesh axis runs over, the one named last changes fastest.
Arguments:
- leaf_rhs: float32 [8, 2048, 256], P('subtree', 'front'), may hold values from -6 to 6
- mid_rhs: float32 [2, 4096, 256], P(None, 'front'), may hold values from -6 to 6
- root_rhs: float32 [10240, 256], P('front'), may hold values from -6 to 6
- leaf_lower: float32 [8, 2048, 2048], P('subtree', None, 'front'), may hold values from -0.125 to 0.125
- leaf_below: float32 [8, 2048, 2048], P('subtree', None, 'front'), may hold values from -0.125 to 0.125
- leaf_right: float32 [8, 2048, 2048], P('subtree', None, 'front'), may hold values from -0.125 to 0.125
- leaf_upper: float32 [8, 2048, 2048], P('subtree', None, 'front'), may hold values from -0.125 to 0.125
- mid_lower: float32 [2, 4096, 4096], P(None, 'subtree', 'front'), may hold values from -0.09375 to 0.09375
- mid_below: float32 [2, 4096, 4096], P(None, 'front', 'subtree'), may hold values from -0.09375 to 0.09375
- mid_right: float32 [2, 4096, 4096], P(None, 'subtree', 'front'), may hold values from -0.09375 to 0.09375
- mid_upper: float32 [2, 4096, 4096], P(None, 'front', 'subtree'), may hold values from -0.09375 to 0.09375
- root_lower: float32 [10240, 10240], P('subtree', 'front'), may hold values from -0.0625 to 0.0625
- root_upper: float32 [10240, 10240], P('front', 'subtree'), may hold values from -0.0625 to 0.0625
- leaf_parent: int32 [8], replicated, may hold values from 0 to 1, as said below
- leaf_sizes: int32 [8], replicated, may hold values from 1024 to 2048, as said below
- leaf_map: int32 [8, 16], replicated, may hold values from 0 to 63, as said below
- mid_map: int32 [2, 32], replicated, may hold values from 0 to 79, as said below
Outputs:
- leaf_sol: float32 [8, 2048, 256], P('subtree', 'front')
- mid_sol: float32 [2, 4096, 256], P(None, 'front')
- root_sol: float32 [10240, 256], P('front')
Inputs may be any that keep to these rules, and one draw needn't show every extreme that they name: `leaf_parent`: every level-1 front is the parent of at least one lowest-level front. `leaf_sizes`: a multiple of 128; some front has all 2048 rows live. `leaf_map`: a front's blocks go to distinct parent blocks; update block b of a lowest-level front, with c = b // 4, goes to c * 8 + i or to that plus 4096 / 128, for some i with 0 <= i < 8. `mid_map`: a front's blocks go to distinct root blocks; update block b of a level-1 front, with c = b // 8, goes to c * 20 + i for some i with 0 <= i < 20.
All inputs are finite; a program needn't handle non-finite values.
Results may differ from a plain program's by a relative error of at most 0.00013.
Values sent between devices are 32-bit elements; how exact they have to be, the bound alone decides.
No kernel may reach another device: no remote copies, remote signals or barrier semaphores. Data moves between devices by JAX's collectives and lax.ppermute only.
A program may use at most 128 MiB of HBM per device.

v0:
```python
import jax
import jax.numpy as jnp
from jax import lax
from jax.sharding import PartitionSpec as P

MID_PIV = 4096
BLOCK = 128


def leaf_product(matrix, vector):
    return lax.psum_scatter(
        jnp.dot(
            matrix, vector, preferred_element_type=jnp.float32, precision=lax.Precision.HIGHEST
        ),
        "front",
        scatter_dimension=0,
        tiled=True,
    )


def across_front(partial_value):
    return lax.psum(partial_value, "front")


def across_subtree(partial_value):
    return lax.psum(partial_value, "subtree")


def batched(matrix, vector):
    return jnp.einsum(
        "fab,fbr->far",
        matrix,
        vector,
        preferred_element_type=jnp.float32,
        precision=lax.Precision.HIGHEST,
    )


def leaf_select(parents, blocks, fronts, column, width):
    front_ids = jnp.arange(fronts, dtype=jnp.int32)[:, None, None, None, None]
    halves = jnp.arange(2, dtype=jnp.int32)[None, :, None, None, None]
    slots = jnp.arange(width, dtype=jnp.int32)[None, None, :, None, None]
    target = halves * (MID_PIV // BLOCK) + column * width + slots
    match_parent = parents[None, None, None, :, None] == front_ids
    match_block = blocks[None, None, None, :, :] == target
    return (match_parent & match_block).astype(jnp.float32)


def on_device(
    leaf_rhs,
    mid_rhs,
    root_rhs,
    leaf_lower,
    leaf_below,
    leaf_right,
    leaf_upper,
    mid_lower,
    mid_below,
    mid_right,
    mid_upper,
    root_lower,
    root_upper,
    leaf_parent,
    leaf_sizes,
    leaf_map,
    mid_map,
):
    group = lax.axis_index("subtree")
    column = lax.axis_index("front")
    local_rows = leaf_rhs.shape[1]
    scenarios = leaf_rhs.shape[2]
    leaf_width = local_rows // BLOCK
    fronts = mid_rhs.shape[0]
    mid_width = mid_rhs.shape[1] // BLOCK
    root_width = root_rhs.shape[0] // BLOCK
    own_size = lax.dynamic_slice_in_dim(leaf_sizes, group, 1)
    positions = column * local_rows + jnp.arange(local_rows, dtype=jnp.int32)
    live = (positions < own_size[0]).astype(jnp.float32)[:, None]
    leaf_fwd = live * leaf_product(leaf_lower[0], live * leaf_rhs[0])
    leaf_contrib = -leaf_product(leaf_below[0], leaf_fwd)
    own_parent = lax.dynamic_slice_in_dim(leaf_parent, group, 1)
    own_blocks = lax.dynamic_slice(leaf_map, (group, column * leaf_width), (1, leaf_width))
    own_select = leaf_select(own_parent, own_blocks, fronts, column, mid_width)
    column_blocks = lax.dynamic_slice_in_dim(leaf_map, column * leaf_width, leaf_width, 1)
    selection = leaf_select(leaf_parent, column_blocks, fronts, column, mid_width)
    piece = lax.all_gather(leaf_contrib[None], "subtree", axis=0, tiled=True)
    shaped = piece.reshape(piece.shape[0], leaf_width, BLOCK, scenarios)
    assembled = jnp.einsum(
        "phqgk,gkbr->phqbr",
        selection,
        shaped,
        preferred_element_type=jnp.float32,
        precision=lax.Precision.HIGHEST,
    )
    mid_pivot = mid_rhs + assembled[:, 0].reshape(fronts, mid_width * BLOCK, scenarios)
    mid_update = assembled[:, 1].reshape(fronts, mid_width * BLOCK, scenarios)
    mid_fwd = across_front(batched(mid_lower, mid_pivot))
    mid_contrib = mid_update - across_subtree(batched(mid_below, mid_fwd))
    column_map = lax.dynamic_slice_in_dim(mid_map, column * mid_width, mid_width, 1)
    slots = jnp.arange(root_width, dtype=jnp.int32)[:, None, None]
    root_select = (column_map[None, :, :] == column * root_width + slots).astype(jnp.float32)
    root_added = jnp.einsum(
        "qpk,pkbr->qbr",
        root_select,
        mid_contrib.reshape(fronts, mid_width, BLOCK, scenarios),
        preferred_element_type=jnp.float32,
        precision=lax.Precision.HIGHEST,
    )
    root_start = root_rhs + root_added.reshape(root_width * BLOCK, scenarios)
    root_fwd = across_front(
        jnp.dot(
            root_lower,
            root_start,
            preferred_element_type=jnp.float32,
            precision=lax.Precision.HIGHEST,
        )
    )
    root_sol = across_subtree(
        jnp.dot(
            root_upper,
            root_fwd,
            preferred_element_type=jnp.float32,
            precision=lax.Precision.HIGHEST,
        )
    )
    mid_ext = jnp.einsum(
        "qpk,qbr->pkbr",
        root_select,
        root_sol.reshape(root_width, BLOCK, scenarios),
        preferred_element_type=jnp.float32,
        precision=lax.Precision.HIGHEST,
    )
    mid_ext = mid_ext.reshape(fronts, mid_width * BLOCK, scenarios)
    mid_back = mid_fwd - across_front(batched(mid_right, mid_ext))
    mid_sol = across_subtree(batched(mid_upper, mid_back))
    whole_column = jnp.stack(
        [
            mid_sol.reshape(fronts, mid_width, BLOCK, scenarios),
            mid_ext.reshape(fronts, mid_width, BLOCK, scenarios),
        ],
        axis=1,
    )
    leaf_ext = jnp.einsum(
        "phqgk,phqbr->gkbr",
        own_select,
        whole_column,
        preferred_element_type=jnp.float32,
        precision=lax.Precision.HIGHEST,
    )
    leaf_ext = leaf_ext.reshape(local_rows, scenarios)
    leaf_back = live * (leaf_fwd - leaf_product(leaf_right[0], leaf_ext))
    leaf_sol = live * leaf_product(leaf_upper[0], leaf_back)
    return (leaf_sol[None], mid_sol, root_sol)


def solution(mesh):
    return jax.shard_map(
        on_device,
        mesh=mesh,
        in_specs=(
            P("subtree", "front", None),
            P(None, "front", None),
            P("front", None),
            P("subtree", None, "front"),
            P("subtree", None, "front"),
            P("subtree", None, "front"),
            P("subtree", None, "front"),
            P(None, "subtree", "front"),
            P(None, "front", "subtree"),
            P(None, "subtree", "front"),
            P(None, "front", "subtree"),
            P("subtree", "front"),
            P("front", "subtree"),
            P(),
            P(),
            P(),
            P(),
        ),
        out_specs=(P("subtree", "front", None), P(None, "front", None), P("front", None)),
        check_vma=False,
    )
```

profile of v0, /device:TPU:0, one launch (start us, length us, event | category | flops | bytes accessed | tf_op | source)
XLA Modules:
  0.0 725.4 jit_solution(1965828273986753131)
XLA Ops:
  9.1 10.6 %fusion.15 = f32[2048,256]{0,1:T(8,128)} fusion(f32[1,2048,512]{2,1,0:T(8,128)} %param.20, f32[1,512,256]{2,1,0:T(8,128)} %param.17, f32[512]{0:T(512)S(1)} %fusion.57), kind=kOutput, calls=%fused_computation.16 | convolution fusion | flops 3221356544 | bytes 6817792 | tf_op jit(solution)/shard_map/dot_general | solution.py:12
  19.8 38.0 %reduce-scatter.5.cloned.1.call-done = f32[512,256]{0,1:T(8,128)} async-done(((f32[2048,256]{0,1:T(8,128)}), f32[512,256]{0,1:T(8,128)}) %reduce-scatter.5.cloned.1.call-update) | async-done | bytes 524304 | tf_op jit(solution)/shard_map/reduce_scatter | solution.py:11
  57.8 7.3 %fusion.18 = f32[2048,256]{0,1:T(8,128)} fusion(f32[1,2048,512]{2,1,0:T(8,128)} %param.21, f32[512,256]{0,1:T(8,128)} %reduce-scatter.5.cloned.1.call-done, f32[512]{0:T(512)S(1)} %fusion.57), kind=kOutput, calls=%fused_computation.17 | convolution fusion | flops 3221356544 | bytes 6817792 | tf_op jit(solution)/shard_map/dot_general | solution.py:12
  65.2 35.3 %reduce-scatter.7.cloned.1.call-done = f32[512,256]{0,1:T(8,128)} async-done(((f32[2048,256]{0,1:T(8,128)}), f32[512,256]{0,1:T(8,128)}) %reduce-scatter.7.cloned.1.call-update) | async-done | bytes 524304 | tf_op jit(solution)/shard_map/reduce_scatter | solution.py:11
  103.0 46.6 %all-gather.3.cloned.1.call-done = f32[4096,256]{0,1:T(8,128)} async-done(((f32[512,256]{0,1:T(8,128)}), f32[4096,256]{0,1:T(8,128)}) %all-gather.3.cloned.1.call-update) | async-done | bytes 4194320 | tf_op jit(solution)/shard_map/all_gather | solution.py:86
  149.5 6.0 reshape.127
  155.6 6.6 copy.48
  162.2 6.1 convolution_bitcast_fusion.2
  171.2 8.0 %fusion.29 = f32[2,512,256]{1,2,0:T(8,128)} fusion(f32[2,512,1024]{2,1,0:T(8,128)S(1)} %copy-done.2, f32[2,1024,256]{2,1,0:T(8,128)S(1)} %copy-done.6, f32[2,1024,256]{2,1,0:T(8,128)S(1)} %bitcast.122), kind=kOutput, calls=%fused_computation.28 | convolution fusion | flops 3221749760 | bytes 9437184 | tf_op jit(solution)/shard_map/fab,fbr->far/dot_general | solution.py:30
  179.6 51.0 %all-reduce.7.cloned.1.call-done = f32[2,512,256]{1,2,0:T(8,128)} async-done(((f32[2,512,256]{1,2,0:T(8,128)}), f32[2,512,256]{1,2,0:T(8,128)}) %all-reduce.7.cloned.1.call-update) | async-done | bytes 1048592 | tf_op jit(solution)/shard_map/psum | solution.py:22
  230.6 7.5 %convolution_bitcast_fusion.5 = f32[2,1024,256]{1,2,0:T(8,128)} fusion(f32[2,512,256]{1,2,0:T(8,128)} %all-reduce.7.cloned.1.call-done, f32[2,1024,512]{2,1,0:T(8,128)} %param.25), kind=kOutput, calls=%fused_computation.27 | convolution fusion | flops 3221225472 | bytes 7340032 | tf_op jit(solution)/shard_map/fab,fbr->far/dot_general | solution.py:30
  242.1 61.2 %all-reduce.9.cloned.1.call-done = f32[2,1024,256]{1,2,0:T(8,128)} async-done(((f32[2,1024,256]{1,2,0:T(8,128)}), f32[2,1024,256]{1,2,0:T(8,128)}) %all-reduce.9.cloned.1.call-update) | async-done | bytes 2097168 | tf_op jit(solution)/shard_map/psum | solution.py:26
  313.2 25.9 %convolution_bitcast_fusion.1 = f32[1280,256]{0,1:T(8,128)} fusion(f32[2560,256]{1,0:T(8,128)S(1)} %bitcast_add_fusion, f32[1280,2560]{1,0:T(8,128)} %param.28), kind=kOutput, calls=%fused_computation.20 | convolution fusion | flops 10066329600 | bytes 17039360 | tf_op jit(solution)/shard_map/dot_general | solution.py:111
  339.2 56.1 %all-reduce.11.cloned.1.call-done = f32[1280,256]{0,1:T(8,128)} async-done(((f32[1280,256]{0,1:T(8,128)}), f32[1280,256]{0,1:T(8,128)}) %all-reduce.11.cloned.1.call-update) | async-done | bytes 1310736 | tf_op jit(solution)/shard_map/psum | solution.py:22
  395.2 15.9 %convolution_bitcast_fusion = f32[2560,256]{0,1:T(8,128)} fusion(f32[1280,256]{0,1:T(8,128)} %all-reduce.11.cloned.1.call-done, f32[2560,1280]{1,0:T(8,128)} %param.29), kind=kOutput, calls=%fused_computation.12 | convolution fusion | flops 10066329600 | bytes 17039360 | tf_op jit(solution)/shard_map/dot_general | solution.py:119
  411.2 69.2 %all-reduce.13.cloned.1.call-done = f32[2560,256]{0,1:T(8,128)} async-done(((f32[2560,256]{0,1:T(8,128)}), f32[2560,256]{0,1:T(8,128)}) %all-reduce.13.cloned.1.call-update) | async-done | bytes 2621456 | tf_op jit(solution)/shard_map/psum | solution.py:26
  490.1 8.0 %convolution_bitcast_fusion.6 = f32[2,512,256]{1,2,0:T(8,128)} fusion(f32[2,1024,256]{2,1,0:T(8,128)S(1)} %bitcast.118, f32[2,512,1024]{2,1,0:T(8,128)S(1)} %copy-done.1), kind=kOutput, calls=%fused_computation.29 | convolution fusion | flops 3221225472 | bytes 7340032 | tf_op jit(solution)/shard_map/fab,fbr->far/dot_general | solution.py:30
  498.4 51.5 %all-reduce.15.cloned.1.call-done = f32[2,512,256]{1,2,0:T(8,128)} async-done(((f32[2,512,256]{1,2,0:T(8,128)}), f32[2,512,256]{1,2,0:T(8,128)}) %all-reduce.15.cloned.1.call-update) | async-done | bytes 1048592 | tf_op jit(solution)/shard_map/psum | solution.py:22
  549.9 7.5 %convolution_bitcast_fusion.4 = f32[2,1024,256]{1,2,0:T(8,128)} fusion(f32[2,1024,512]{2,1,0:T(8,128)} %param.27, f32[2,512,256]{1,2,0:T(8,128)S(1)} %copy-done.4, f32[2,512,256]{1,2,0:T(8,128)} %all-reduce.15.cloned.1.call-done), kind=kOutput, calls=%fused_computation.26 | convolution fusion | flops 3221487616 | bytes 8388608 | tf_op jit(solution)/shard_map/fab,fbr->far/dot_general | solution.py:30
  558.8 63.8 %all-reduce.17.cloned.1.call-done = f32[2,1024,256]{1,2,0:T(8,128)} async-done(((f32[2,1024,256]{1,2,0:T(8,128)}), f32[2,1024,256]{1,2,0:T(8,128)}) %all-reduce.17.cloned.1.call-update) | async-done | bytes 2097168 | tf_op jit(solution)/shard_map/psum | solution.py:26
  630.5 8.4 %fusion.21 = f32[2048,256]{0,1:T(8,128)} fusion(f32[512,256]{1,0:T(8,128)S(1)} %bitcast.123, f32[1,2048,512]{2,1,0:T(8,128)S(1)} %copy-done.3), kind=kOutput, calls=%fused_computation.18 | convolution fusion | flops 3221225472 | bytes 6815744 | tf_op jit(solution)/shard_map/dot_general | solution.py:12
  639.1 34.7 %reduce-scatter.9.cloned.1.call-done = f32[512,256]{0,1:T(8,128)} async-done(((f32[2048,256]{0,1:T(8,128)}), f32[512,256]{0,1:T(8,128)}) %reduce-scatter.9.cloned.1.call-update) | async-done | bytes 524304 | tf_op jit(solution)/shard_map/reduce_scatter | solution.py:11
  673.8 7.4 %fusion.24 = f32[2048,256]{0,1:T(8,128)} fusion(f32[1,2048,512]{2,1,0:T(8,128)} %param.23, f32[512,256]{0,1:T(8,128)} %reduce-scatter.9.cloned.1.call-done, f32[512,256]{0,1:T(8,128)S(1)} %copy-done.7, f32[512]{0:T(512)S(1)} %fusion.57), kind=kOutput, calls=%fused_computation.19 | convolution fusion | flops 3221618688 | bytes 7342080 | tf_op jit(solution)/shard_map/dot_general | solution.py:12
  681.2 35.3 %reduce-scatter.11.cloned.1.call-done = f32[512,256]{0,1:T(8,128)} async-done(((f32[2048,256]{0,1:T(8,128)}), f32[512,256]{0,1:T(8,128)}) %reduce-scatter.11.cloned.1.call-update) | async-done | bytes 524304 | tf_op jit(solution)/shard_map/reduce_scatter | solution.py:11
  (76 shorter events, 43.5 us)
Async XLA Ops:
  7.2 95.5 %copy-start = (s32[8,16]{1,0:T(8,128)S(1)}, s32[8,16]{1,0:T(8,128)}, u32[]{:S(2)}) copy-start(s32[8,16]{1,0:T(8,128)} %param.32) | copy-start | bytes 1540
  7.2 50.6 %reduce-scatter.5.cloned.1.call-start = ((), (), s32[]{:S(2)}) async-start(), calls=%async_computation.4 | async-start | bytes 2621440 | tf_op jit(solution)/shard_map/reduce_scatter | solution.py:11
  19.7 80.7 %reduce-scatter.7.cloned.1.call-start = ((), (), s32[]{:S(2)}) async-start(), calls=%async_computation.5 | async-start | bytes 2621440 | tf_op jit(solution)/shard_map/reduce_scatter | solution.py:11
  65.1 37.7 %copy-start.9 = (s32[8]{0:T(128)S(1)}, s32[8]{0:T(128)}, u32[]{:S(2)}) copy-start(s32[8]{0:T(128)} %param.30) | copy-start | bytes 100
  65.1 84.4 %all-gather.3.cloned.1.call-start = ((), (), s32[]{:S(2)}) async-start(), calls=%async_computation.14 | async-start | bytes 4718592 | tf_op jit(solution)/shard_map/all_gather | solution.py:86
  102.4 128.2 %all-reduce.7.cloned.1.call-start = ((), (), s32[]{:S(2)}) async-start(), calls=%async_computation.6 | async-start | bytes 2097152 | tf_op jit(solution)/shard_map/psum | solution.py:22
  168.3 1.6 copy-start.6
  168.6 2.5 copy-start.2
  179.2 59.0 %copy-start.8 = (s32[2,32]{1,0:T(2,128)S(1)}, s32[2,32]{1,0:T(2,128)}, u32[]{:S(2)}) copy-start(s32[2,32]{1,0:T(2,128)} %param.33) | copy-start | bytes 772
  179.2 124.1 %all-reduce.9.cloned.1.call-start = ((), (), s32[]{:S(2)}) async-start(), calls=%async_computation.7 | async-start | bytes 4194304 | tf_op jit(solution)/shard_map/psum | solution.py:26
  238.1 157.1 %all-reduce.11.cloned.1.call-start = ((), (), s32[]{:S(2)}) async-start(), calls=%async_computation.8 | async-start | bytes 2621440 | tf_op jit(solution)/shard_map/psum | solution.py:22
  311.1 1.7 copy-start.5
  339.1 141.2 %all-reduce.13.cloned.1.call-start = ((), (), s32[]{:S(2)}) async-start(), calls=%async_computation.9 | async-start | bytes 5242880 | tf_op jit(solution)/shard_map/psum | solution.py:26
  411.1 138.8 %all-reduce.15.cloned.1.call-start = ((), (), s32[]{:S(2)}) async-start(), calls=%async_computation.10 | async-start | bytes 2097152 | tf_op jit(solution)/shard_map/psum | solution.py:22
  487.9 2.2 copy-start.1
  490.1 59.8 %copy-start.4 = (f32[2,512,256]{1,2,0:T(8,128)S(1)}, f32[2,512,256]{1,2,0:T(8,128)}, u32[]{:S(2)}) copy-start(f32[2,512,256]{1,2,0:T(8,128)} %all-reduce.7.cloned.1.call-done) | copy-start | bytes 3145732
  498.2 124.4 %all-reduce.17.cloned.1.call-start = ((), (), s32[]{:S(2)}) async-start(), calls=%async_computation.11 | async-start | bytes 4194304 | tf_op jit(solution)/shard_map/psum | solution.py:26
  557.4 116.4 %reduce-scatter.9.cloned.1.call-start = ((), (), s32[]{:S(2)}) async-start(), calls=%async_computation.12 | async-start | bytes 2621440 | tf_op jit(solution)/shard_map/reduce_scatter | solution.py:11
  628.3 2.2 copy-start.3
  630.5 43.3 %copy-start.7 = (f32[512,256]{0,1:T(8,128)S(1)}, f32[512,256]{0,1:T(8,128)}, u32[]{:S(2)}) copy-start(f32[512,256]{0,1:T(8,128)} %reduce-scatter.5.cloned.1.call-done) | copy-start | bytes 1572868
  638.9 77.7 %reduce-scatter.11.cloned.1.call-start = ((), (), s32[]{:S(2)}) async-start(), calls=%async_computation.13 | async-start | bytes 2621440 | tf_op jit(solution)/shard_map/reduce_scatter | solution.py:11
Sparse Core Ops, SparseCore 0:
  19.8 37.9 reduce-scatter.4
  65.2 35.1 reduce-scatter.6
  102.6 46.8 all-gather.2
  179.3 51.2 all-reduce.6
  238.2 65.0 all-reduce.8
  339.2 55.9 all-reduce.10
  411.3 69.0 all-reduce.12
  498.3 51.5 all-reduce.14
  557.5 65.0 all-reduce.16
  639.0 34.7 reduce-scatter.8
  681.3 35.1 reduce-scatter.10
where the time goes:
time: 734 us; the launch traced here: 725 us
  waiting for transfers between devices  543 us (74%)
  matrix products  122 us (17%)
  local copies, waits for them, and re-layouts  38.1 us (5%)
  between operations  14.3 us (2%)
    psum x3, waiting for transfers between devices, across_subtree(): return lax.psum(partial_value, 'subtree')  194 us
    psum x3, waiting for transfers between devices, across_front(): return lax.psum(partial_value, 'front')  159 us
    reduce_scatter x4, waiting for transfers between devices, leaf_product(): lax.psum_scatter(jnp.dot(matrix, vector, preferred_element_type=jnp.float...  143 us
    all_gather x1, waiting for transfers between devices, on_device(): piece = lax.all_gather(leaf_contrib[None], 'subtree', axis=0, tiled=True)  46.6 us
    dot_general x4, matrix products, leaf_product(): jnp.dot(matrix, vector, preferred_element_type=jnp.float32, precision=lax...  33.6 us
    dot_general x4, matrix products, batched(): jnp.einsum('fab,fbr->far', matrix, vector, preferred_element_type=jnp.flo...  31 us
    dot_general x1, matrix products, on_device(): jnp.dot(root_lower, root_start, preferred_element_type=jnp.float32, preci...  25.9 us
    dot_general x1, matrix products, on_device(): jnp.dot(root_upper, root_fwd, preferred_element_type=jnp.float32, precisi...  15.9 us
  transfers between devices with their start and end apart: 11, of which 11 were waited for; matrix products, arithmetic and copies ran while one was open for 1% of the time, Pallas kernels for 0%

commit v1 on v0

v1 whole, which is shorter than its diff:
```python
import functools

import jax
import jax.numpy as jnp
from jax import lax
from jax.experimental import pallas as pl
from jax.experimental.pallas import tpu as pltpu
from jax.sharding import PartitionSpec as P

F32 = jnp.float32
BF16 = jnp.bfloat16
CHAINS = 1
BLOCK_BYTES = 1 << 21
VMEM_LIMIT = 40 << 20


def partner(x, axis, mask, n):
    return lax.ppermute(x, axis, [(i, i ^ mask) for i in range(n)])


def halving_order(masks):
    if not masks:
        return [0]
    rest = halving_order(masks[1:])
    return [masks[0] ^ c for c in rest] + rest


def pick_rows(rows, depth):
    best = 8
    for d in range(8, rows + 1, 8):
        if rows % d == 0 and d * depth * 4 <= BLOCK_BYTES:
            best = d
    return best


def put(x2, slot, start, value):
    n = value.shape[1]
    rows = pl.ds(start, value.shape[0])
    high = value.astype(BF16)
    x2[slot, rows, pl.ds(0, n)] = high
    x2[slot, rows, pl.ds(n, n)] = (value - high.astype(F32)).astype(BF16)


def product(a, x2):
    n = x2.shape[1] // 2
    high = a.astype(BF16)
    low = (a - high.astype(F32)).astype(BF16)
    both = jnp.dot(high, x2, preferred_element_type=F32)
    return (both[:, :n] + both[:, n:]) + jnp.dot(low, x2[:, :n], preferred_element_type=F32)


def matmul(
    name,
    meta,
    matrix,
    rows,
    width,
    index,
    ins,
    outs,
    slots=1,
    slot_of=None,
    prologue=None,
    extra=(),
    x2=None,
    keep_x2=False,
    scratch=(),
    finish=None,
    sign=1.0,
    in_specs=None,
):
    depth = matrix.shape[2]
    total = sum(outs)
    steps = total // rows
    per = steps // len(outs)
    n_in, n_out, n_extra = len(ins), len(outs), len(extra)
    x2_shape = (slots, depth, 2 * width)
    given = x2 is not None

    def whole(a):
        nd = len(a)
        return pl.BlockSpec(a, lambda i, m, nd=nd: (0,) * nd)

    def kernel(meta_ref, a_ref, *refs):
        i = pl.program_id(0)
        in_refs, refs = refs[:n_in], refs[n_in:]
        if given:
            x2_ref, refs = refs[0], refs[1:]
        out_refs, refs = refs[:n_out], refs[n_out:]
        extra_refs, refs = refs[:n_extra], refs[n_extra:]
        if not given:
            x2_ref, refs = refs[0], refs[1:]

            @pl.when(i == 0)
            def _():
                prologue(meta_ref, in_refs, extra_refs, x2_ref, refs)

        slot = 0 if slot_of is None else slot_of(i)
        acc = product(a_ref[0], x2_ref[slot])
        if sign != 1.0:
            acc = -acc
        for j in range(n_out):

            @pl.when(i // per == j)
            def _():
                start = pl.multiple_of((i - j * per) * rows, rows)
                out_refs[j][pl.ds(start, rows), :] = acc

        if finish is not None:

            @pl.when(i == steps - 1)
            def _():
                finish(meta_ref, in_refs, out_refs)

    out_shape = [jax.ShapeDtypeStruct((r, width), F32) for r in outs]
    out_shape += [jax.ShapeDtypeStruct(e, F32) for e in extra]
    out_specs = [whole(o.shape) for o in out_shape]
    scratch_shapes = list(scratch)
    args = [matrix, *ins]
    specs = [pl.BlockSpec((1, rows, depth), lambda i, m: (*index(i, m), 0))]
    specs += in_specs if in_specs is not None else [whole(a.shape) for a in ins]
    if given:
        args.append(x2)
        specs.append(whole(x2_shape))
    elif keep_x2:
        out_shape.append(jax.ShapeDtypeStruct(x2_shape, BF16))
        out_specs.append(whole(x2_shape))
    else:
        scratch_shapes = [pltpu.VMEM(x2_shape, BF16)] + scratch_shapes
    return pl.pallas_call(
        kernel,
        out_shape=out_shape,
        grid_spec=pltpu.PrefetchScalarGridSpec(
            num_scalar_prefetch=1,
            grid=(steps,),
            in_specs=specs,
            out_specs=out_specs,
            scratch_shapes=scratch_shapes,
        ),
        compiler_params=pltpu.CompilerParams(
            dimension_semantics=("arbitrary",), vmem_limit_bytes=VMEM_LIMIT
        ),
        cost_estimate=pl.CostEstimate(
            flops=6 * total * depth * width,
            bytes_accessed=4 * total * depth,
            transcendentals=0,
        ),
        name=name,
    )(meta, *args)


def solve(
    n_sub,
    n_front,
    tables,
    leaf_rhs,
    mid_rhs,
    root_rhs,
    leaf_lower,
    leaf_below,
    leaf_right,
    leaf_upper,
    mid_lower,
    mid_below,
    mid_right,
    mid_upper,
    root_lower,
    root_upper,
):
    meta0, meta, at = tables
    width = leaf_rhs.shape[1]
    local = leaf_rhs.shape[0]
    fronts, mid_rows = mid_rhs.shape[0], mid_rhs.shape[1]
    root_rows = root_rhs.shape[0]
    block, sub, per_stream = at["block"], at["sub"], at["per_stream"]
    half_leaf = local // 2
    half_fronts = fronts // 2
    mid_width = mid_rows // block
    f_bits = n_front.bit_length() - 1
    z_bits = n_sub.bit_length() - 2
    f_masks = [1 << j for j in range(f_bits)]
    f_masks = [f_masks, f_masks[::-1]]
    z_masks = [2 * ((2 << j) - 1) for j in range(z_bits)]
    z_masks = [z_masks, z_masks[::-1]]
    over_front = lambda x, m: partner(x, "front", m, n_front)
    over_sub = lambda x, m: partner(x, "subtree", m, n_sub)

    def scatter_sum(send, keep, masks):
        for j, m in enumerate(masks):
            got = over_front(send, m)
            if j + 1 == len(masks):
                return keep, got
            h = keep.shape[0] // 2
            send, keep = keep[:h] + got[:h], keep[h:] + got[h:]

    def sum_front(value, masks):
        for m in masks[:-1]:
            value = value + over_front(value, m)
        return value, over_front(value, masks[-1])

    def sum_subtree(send, keep):
        got = over_sub(send, 1)
        h = keep.shape[0] // 2
        mine, other = [], []
        for t in range(2):
            value = keep[t * h : (t + 1) * h] + got[t * h : (t + 1) * h]
            for m in z_masks[t]:
                value = value + over_sub(value, m)
            mine.append(value)
            other.append(over_sub(value, 1))
        return mine, other

    def leaf_phase(name, meta_, matrix, ins, prologue, extra=()):
        half = n_front // 2
        rows = half_leaf
        first = lambda base: (lambda i, m: (0, m[base + i]))
        outs = [half * rows] * 2
        res = matmul(
            name + "_send", meta_, matrix, rows, width, first(at["order"]), ins, outs,
            prologue=prologue, extra=extra, keep_x2=True,
        )
        sends, extras, x2 = res[:2], res[2:-1], res[-1]
        keeps = matmul(
            name + "_keep", meta_, matrix, rows, width, first(at["order"] + n_front), [], outs, x2=x2
        )
        terms = []
        for t in range(2):
            terms += scatter_sum(sends[t], keeps[t], f_masks[t])
        return terms, extras

    def live_rows(m, t, value):
        ids = lax.broadcasted_iota(jnp.int32, value.shape, 0) + t * half_leaf
        return jnp.where(ids < m[at["live"]], value, 0.0)

    def pro(m, ins, extra, x2, _):
        for t in range(2):
            put(x2, 0, t * half_leaf, live_rows(m, t, ins[0][pl.ds(t * half_leaf, half_leaf), :]))

    terms, _ = leaf_phase("leaf_lower", meta0, leaf_lower, [leaf_rhs], pro)

    def pro(m, ins, extra, x2, _):
        for t in range(2):
            fwd = live_rows(m, t, ins[2 * t][...] + ins[2 * t + 1][...])
            extra[0][pl.ds(t * half_leaf, half_leaf), :] = fwd
            put(x2, 0, t * half_leaf, fwd)

    terms, (leaf_fwd,) = leaf_phase("leaf_below", meta0, leaf_below, terms, pro, [(local, width)])
    contrib = [-(terms[2 * t] + terms[2 * t + 1]) for t in range(2)]

    pieces, offsets = [], []
    for t in range(2):
        bufs, offs = [contrib[t]], [0]
        for m in z_masks[t]:
            bufs, offs = bufs + [over_sub(b, m) for b in bufs], offs + [o ^ m for o in offs]
        pieces += bufs
        offsets += [(t, o) for o in offs]

    def assemble(m, *refs):
        ins, out = refs[:-1], refs[-1]
        out[...] = jnp.zeros_like(out)
        for ref, (t, off) in zip(ins, offsets):
            leaf = m[at["self"]] ^ off
            for j in range(per_stream):
                row = m[at["pivot"] + leaf * 2 * per_stream + t * per_stream + j]

                @pl.when(row >= 0)
                def _():
                    rows = pl.ds(pl.multiple_of(row, sub), sub)
                    out[rows, :] += ref[pl.ds(j * sub, sub), :]

    pivot_mine = pl.pallas_call(
        assemble,
        out_shape=jax.ShapeDtypeStruct((fronts * mid_rows, width), F32),
        grid_spec=pltpu.PrefetchScalarGridSpec(
            num_scalar_prefetch=1,
            grid=(1,),
            in_specs=[pl.BlockSpec(p.shape, lambda i, m: (0, 0)) for p in pieces],
            out_specs=pl.BlockSpec((fronts * mid_rows, width), lambda i, m: (0, 0)),
        ),
        compiler_params=pltpu.CompilerParams(vmem_limit_bytes=VMEM_LIMIT),
        name="pivot_rows",
    )(meta, *pieces)
    pivot_other = over_sub(pivot_mine, 1)
    mid_flat = mid_rhs.reshape(fronts * mid_rows, width)

    def front_products(name, matrix, prologue_of, ins_of, specs_of=None, extra_of=None):
        out_rows = matrix.shape[1]
        rows = pick_rows(out_rows, matrix.shape[2])
        steps = out_rows // rows
        results = []
        extras = None
        for t in range(2):
            res = matmul(
                f"{name}_{t}", meta, matrix, rows, width,
                lambda i, m, t=t: (t * half_fronts + i // steps, i % steps),
                ins_of(t, extras), [half_fronts * out_rows],
                slots=half_fronts, slot_of=lambda i: i // steps, prologue=prologue_of(t),
                in_specs=specs_of(t) if specs_of else None,
                extra=extra_of(t) if extra_of else (),
            )
            if len(res) > 1:
                extras = res[1]
            results.append(sum_front(res[0], f_masks[t]))
        return results, extras

    def pro_of(t):
        def pro(m, ins, extra, x2, _):
            for q in range(half_fronts):
                rows = pl.ds(q * mid_rows, mid_rows)
                put(x2, q, 0, ins[0][rows, :] + (ins[1][rows, :] + ins[2][rows, :]))

        return pro

    part = (half_fronts * mid_rows, width)
    mid_fwd, _ = front_products(
        "mid_lower", mid_lower, pro_of, lambda t, e: [mid_flat, pivot_mine, pivot_other],
        specs_of=lambda t: [pl.BlockSpec(part, lambda i, m: (t, 0))] * 3,
    )

    def core_products(name, matrix, prologue_of, ins, finish_of=None, sign=1.0):
        out_rows = matrix.shape[1]
        rows = pick_rows(out_rows, matrix.shape[2])
        steps = out_rows // rows
        results = []
        for flip in (1, 0):
            results += matmul(
                f"{name}_{flip}", meta, matrix, rows, width,
                lambda i, m, flip=flip: ((m[at["core"]] ^ flip) * half_fronts + i // steps, i % steps),
                ins, [half_fronts * out_rows],
                slots=half_fronts, slot_of=lambda i: i // steps, prologue=prologue_of(flip),
                finish=finish_of(flip) if finish_of else None, sign=sign,
            )
        return sum_subtree(*results)

    own_rows = mid_lower.shape[1]

    def pro_of(flip):
        def pro(m, ins, extra, x2, _):
            for t in range(2):

                @pl.when((m[at["core"]] ^ flip) == t)
                def _():
                    for q in range(half_fronts):
                        rows = pl.ds(q * own_rows, own_rows)
                        put(x2, q, 0, ins[2 * t][rows, :] + ins[2 * t + 1][rows, :])

        return pro

    def finish_of(flip):
        def finish(m, ins, outs):
            first = (m[at["core"]] ^ flip) * (half_fronts * mid_rows)
            for u in range(2 * per_stream):
                row = m[at["update"] + u] - first

                @pl.when((row >= 0) & (row < half_fronts * mid_rows))
                def _():
                    rows = pl.ds(pl.multiple_of(row, sub), sub)
                    src = ins[4 + u // per_stream]
                    outs[0][rows, :] += src[pl.ds((u % per_stream) * sub, sub), :]

        return finish

    fwd_terms = [*mid_fwd[0], *mid_fwd[1]]
    mine, other = core_products(
        "mid_below", mid_below, pro_of, fwd_terms + contrib, finish_of, sign=-1.0
    )

    mid_half = half_fronts * mid_rows // 2

    def root_pro(m, ins, extra, x2, scr):
        total = scr[0]
        total[...] = ins[0][...]
        for w in range(2):
            half = m[at["core"]] ^ w
            for t in range(2):
                src = ins[1 + 2 * w + t]
                for k in range(mid_half // block):
                    row = t * mid_half + k * block
                    front = half * half_fronts + row // mid_rows
                    slot = m[at["root"] + front * mid_width + (row % mid_rows) // block]
                    rows = pl.ds(pl.multiple_of(slot * block, block), block)
                    total[rows, :] += src[pl.ds(k * block, block), :]
        put(x2, 0, 0, total[...])

    out_rows = root_lower.shape[0] // 2
    rows = pick_rows(out_rows, root_lower.shape[1])
    steps = out_rows // rows
    matrix = root_lower[None]
    h0, x2 = matmul(
        "root_lower_0", meta, matrix, rows, width, lambda i, m: (0, i),
        [root_rhs, *mine, *other], [out_rows], prologue=root_pro, keep_x2=True,
        scratch=[pltpu.VMEM((root_rows, width), F32)],
    )
    root_fwd = list(sum_front(h0, f_masks[0]))
    (h1,) = matmul(
        "root_lower_1", meta, matrix, rows, width, lambda i, m: (0, steps + i), [], [out_rows], x2=x2
    )
    root_fwd += sum_front(h1, f_masks[1])

    def pro(m, ins, extra, x2, _):
        for t in range(2):
            put(x2, 0, t * out_rows, ins[2 * t][...] + ins[2 * t + 1][...])

    half_root = root_rows // 2
    rows = pick_rows(half_root, root_upper.shape[1])
    steps_up = half_root // rows
    matrix = root_upper[None]
    row_of = lambda flip: (lambda i, m: (0, (m[at["core"]] ^ flip) * steps_up + i))
    send, x2 = matmul(
        "root_upper_1", meta, matrix, rows, width, row_of(1), root_fwd, [half_root],
        prologue=pro, keep_x2=True,
    )
    (keep,) = matmul(
        "root_upper_0", meta, matrix, rows, width, row_of(0), [], [half_root], x2=x2
    )
    mine, other = sum_subtree(send, keep)

    def place(m, ins, out):
        h = ins[0].shape[0]
        for w in range(2):
            for t in range(2):
                start = (m[at["core"]] ^ w) * (2 * h) + t * h
                out[pl.ds(pl.multiple_of(start, h), h), :] = ins[2 * w + t][...]

    def pro_of(t):
        def pro(m, ins, extra, x2, _):
            if t == 0:
                place(m, ins, extra[0])
                root = extra[0]
            else:
                root = ins[0]
            for q in range(half_fronts):
                for k in range(mid_width):
                    slot = m[at["root"] + (t * half_fronts + q) * mid_width + k]
                    rows = pl.ds(pl.multiple_of(slot * block, block), block)
                    put(x2, q, k * block, root[rows, :])

        return pro

    mid_ext, root_sol = front_products(
        "mid_right", mid_right, pro_of, lambda t, e: [*mine, *other] if t == 0 else [e],
        extra_of=lambda t: [(root_rows, width)] if t == 0 else [],
    )
    ext_terms = [*mid_ext[0], *mid_ext[1]]

    def pro_of(flip):
        def pro(m, ins, extra, x2, _):
            for t in range(2):

                @pl.when((m[at["core"]] ^ flip) == t)
                def _():
                    for q in range(half_fronts):
                        rows = pl.ds(q * own_rows, own_rows)
                        a, b, c, d = (ins[j][rows, :] for j in (2 * t, 2 * t + 1, 4 + 2 * t, 5 + 2 * t))
                        put(x2, q, 0, (a + b) - (c + d))

        return pro

    mine, other = core_products("mid_upper", mid_upper, pro_of, fwd_terms + ext_terms)

    def pro(m, ins, extra, x2, _):
        place(m, ins, extra[0])
        for u in range(2 * per_stream):
            rows = pl.ds(pl.multiple_of(m[at["ext_row"] + u], sub), sub)

            @pl.when(m[at["ext_root"] + u] == 0)
            def _():
                put(x2, 0, u * sub, extra[0][rows, :])

            @pl.when(m[at["ext_root"] + u] != 0)
            def _():
                put(x2, 0, u * sub, ins[4][rows, :])

    terms, (mid_sol,) = leaf_phase(
        "leaf_right", meta, leaf_right, [*mine, *other, root_sol], pro,
        [(fronts * mid_rows, width)],
    )

    def pro(m, ins, extra, x2, _):
        for t in range(2):
            back = ins[0][pl.ds(t * half_leaf, half_leaf), :] - (ins[1 + 2 * t][...] + ins[2 + 2 * t][...])
            put(x2, 0, t * half_leaf, live_rows(m, t, back))

    terms, _ = leaf_phase("leaf_upper", meta0, leaf_upper, [leaf_fwd, *terms], pro)
    leaf_sol = jnp.concatenate([terms[0] + terms[1], terms[2] + terms[3]], axis=0)
    ids = jnp.arange(local, dtype=jnp.int32)[:, None]
    leaf_sol = jnp.where(ids < meta0[at["live"]], leaf_sol, 0.0)
    return leaf_sol, mid_sol.reshape(mid_rhs.shape), root_sol


def on_device(
    n_sub,
    n_front,
    leaf_rhs,
    mid_rhs,
    root_rhs,
    leaf_lower,
    leaf_below,
    leaf_right,
    leaf_upper,
    mid_lower,
    mid_below,
    mid_right,
    mid_upper,
    root_lower,
    root_upper,
    leaf_parent,
    leaf_sizes,
    leaf_map,
    mid_map,
):
    group = lax.axis_index("subtree").astype(jnp.int32)
    column = lax.axis_index("front").astype(jnp.int32)
    local = leaf_rhs.shape[1]
    scenarios = leaf_rhs.shape[2]
    block = local * n_front // leaf_map.shape[1]
    mid_rows = mid_rhs.shape[1]
    mid_width = mid_rows // block
    root_width = root_rhs.shape[0] // block
    leaf_width = local // block
    sub = min(block, local // 2)
    per_stream = (local // 2) // sub
    leaves = leaf_map.shape[0]
    f_bits = n_front.bit_length() - 1
    masks = [1 << j for j in range(f_bits)]
    orders = [halving_order(masks), halving_order(masks[::-1])]
    half = n_front // 2
    table = [(o, t) for t in range(2) for o in orders[t][:half]]
    table += [(o, t) for t in range(2) for o in orders[t][half:]]
    order = (column ^ jnp.array([o for o, _ in table], jnp.int32)) * 2
    order = order + jnp.array([t for _, t in table], jnp.int32)
    own_size = lax.dynamic_slice_in_dim(leaf_sizes, group, 1)
    head = jnp.stack([column, group, group & 1, own_size[0] - column * local])
    meta0 = jnp.concatenate([head, order])

    columns = lax.dynamic_slice_in_dim(leaf_map, column * leaf_width, leaf_width, 1)
    starts = [u * sub for u in range(2 * per_stream)]
    blocks = jnp.stack([columns[:, r // block] for r in starts], axis=1)
    inner = jnp.array([r % block for r in starts], jnp.int32)[None]
    halves = n_front * mid_width
    is_update = blocks >= halves
    slot = blocks - jnp.where(is_update, halves, 0) - column * mid_width
    target = leaf_parent[:, None] * mid_rows + slot * block + inner
    pivot = jnp.where(is_update, -1, target)
    update = jnp.where(is_update, target, -(1 << 24))
    root = lax.dynamic_slice_in_dim(mid_map, column * mid_width, mid_width, 1) - column * root_width
    row = lambda a: lax.dynamic_slice_in_dim(a, group, 1, 0)[0]
    own_update, own_slot = row(is_update), row(slot)
    own_parent = row(leaf_parent)
    root_slot = root.reshape(-1)[jnp.clip(own_parent * mid_width + own_slot, 0, root.size - 1)]
    ext_row = jnp.where(own_update, root_slot * block + inner[0], row(target))
    parts = [
        ("pivot", pivot.reshape(-1)),
        ("update", row(update)),
        ("root", root.reshape(-1)),
        ("ext_root", own_update.astype(jnp.int32)),
        ("ext_row", ext_row),
    ]
    at = {"self": 1, "core": 2, "live": 3, "order": 4}
    at |= {"block": block, "sub": sub, "per_stream": per_stream}
    size = meta0.shape[0]
    for key, value in parts:
        at[key] = size
        size += value.shape[0]
    meta = jnp.concatenate([meta0] + [v.astype(jnp.int32) for _, v in parts])

    width = scenarios // CHAINS
    results = []
    for k in range(CHAINS):
        cols = slice(k * width, (k + 1) * width)
        results.append(
            solve(
                n_sub, n_front, (meta0, meta, at),
                leaf_rhs[0][:, cols], mid_rhs[:, :, cols], root_rhs[:, cols],
                leaf_lower, leaf_below, leaf_right, leaf_upper,
                mid_lower, mid_below, mid_right, mid_upper, root_lower, root_upper,
            )
        )
    outs = [jnp.concatenate(r, axis=-1) if CHAINS > 1 else r[0] for r in zip(*results)]
    return outs[0][None], outs[1], outs[2]


def solution(mesh):
    return jax.shard_map(
        functools.partial(on_device, mesh.shape["subtree"], mesh.shape["front"]),
        mesh=mesh,
        in_specs=(
            P("subtree", "front", None),
            P(None, "front", None),
            P("front", None),
            P("subtree", None, "front"),
            P("subtree", None, "front"),
            P("subtree", None, "front"),
            P("subtree", None, "front"),
            P(None, "subtree", "front"),
            P(None, "front", "subtree"),
            P(None, "subtree", "front"),
            P(None, "front", "subtree"),
            P("subtree", "front"),
            P("front", "subtree"),
            P(),
            P(),
            P(),
            P(),
        ),
        out_specs=(P("subtree", "front", None), P(None, "front", None), P("front", None)),
        check_vma=False,
    )
```

time: 734 us -> 454 us (0.62); the launches traced: 725 us -> 453 us
  waiting for transfers between devices: 543 us -> 278 us
  matrix products: 122 us -> 0 us
  starting transfers between devices: 1.46 us -> 95.5 us
  Pallas kernels: 0 us -> 62.9 us
  local copies, waits for them, and re-layouts: 38.1 us -> 10 us
  between operations: 14.3 us -> 2.41 us
    psum x6 -> x0, waiting for transfers between devices: 353 us -> none  [the longest x3 194 us: across_subtree(): return lax.psum(partial_value, 'subtree')]
    ppermute x0 -> x56, waiting for transfers between devices: none -> 278 us  [partner(): return lax.ppermute(x, axis, [(i, i ^ mask) for i in range(n)])]
    reduce_scatter x4 -> x0, waiting for transfers between devices: 143 us -> none  [leaf_product(): lax.psum_scatter(jnp.dot(matrix, vector, preferred_element_type=jnp.float...]
    dot_general x14 -> x0, matrix products: 122 us -> none  [the longest x4 33.6 us: leaf_product(): jnp.dot(matrix, vector, preferred_element_type=jnp.float32, precision=lax...]
    ppermute x0 -> x56, starting transfers between devices: none -> 95.5 us  [partner(): return lax.ppermute(x, axis, [(i, i ^ mask) for i in range(n)])]
    pallas_call x0 -> x21, Pallas kernels: none -> 62.9 us  [the longest x20 60.7 us: matmul(): pl.pallas_call(kernel, out_shape=out_shape, grid_spec=pltpu.PrefetchScala...]
    all_gather x1 -> x0, waiting for transfers between devices: 46.6 us -> none  [on_device(): piece = lax.all_gather(leaf_contrib[None], 'subtree', axis=0, tiled=True)]
    reshape x3 -> x2, local copies, waits for them, and re-layouts: 14.7 us -> 0.16 us  [the longest x1 0.08 us: on_device(): root.reshape(-1)]
  transfers between devices with their start and end apart: 11 -> 56, of which waited for: 11 -> 46; matrix products, arithmetic and copies ran while one was open for 1% -> 1% of each run, Pallas kernels for 0% -> 4%
where the time goes in v1:
time: 454 us; the launch traced here: 453 us
  waiting for transfers between devices  278 us (61%)
  starting transfers between devices  95.5 us (21%)
  Pallas kernels  62.9 us (14%)
  local copies, waits for them, and re-layouts  10 us (2%)
    ppermute x56, waiting for transfers between devices, partner(): return lax.ppermute(x, axis, [(i, i ^ mask) for i in range(n)])  278 us
    ppermute x56, starting transfers between devices, partner(): return lax.ppermute(x, axis, [(i, i ^ mask) for i in range(n)])  95.5 us
    pallas_call x20, Pallas kernels, matmul(): pl.pallas_call(kernel, out_shape=out_shape, grid_spec=pltpu.PrefetchScala...  60.7 us
  transfers between devices with their start and end apart: 56, of which 46 were waited for; matrix products, arithmetic and copies ran while one was open for 1% of the time, Pallas kernels for 4%

profile of v1, /device:TPU:0, one launch (start us, length us, event | category | flops | bytes accessed | tf_op | source)
XLA Modules:
  0.0 453.4 jit_solution(13427761768119864303)
XLA Ops:
  15.5 8.3 %collective-permute-done = f32[512,256]{1,0:T(8,128)S(1)} collective-permute-done((f32[512,256]{1,0:T(8,128)S(1)}, f32[512,256]{1,0:T(8,128)S(1)}, u32[]{:S(2)}, u32[]{:S(2)}) %collective-permute-start) | collective-permute-done | bytes 524320 | tf_op jit(solution)/shard_map/ppermute | solution.py:18
  41.5 7.4 %collective-permute-done.9 = f32[512,256]{1,0:T(8,128)S(1)} collective-permute-done((f32[512,256]{1,0:T(8,128)S(1)}, f32[512,256]{1,0:T(8,128)S(1)}, u32[]{:S(2)}, u32[]{:S(2)}) %collective-permute-start.9) | collective-permute-done | bytes 524320 | tf_op jit(solution)/shard_map/ppermute | solution.py:18
  104.1 9.4 %collective-permute-done.15 = f32[512,256]{1,0:T(8,128)S(1)} collective-permute-done((f32[512,256]{1,0:T(8,128)S(1)}, f32[512,256]{1,0:T(8,128)S(1)}, u32[]{:S(2)}, u32[]{:S(2)}) %collective-permute-start.15) | collective-permute-done | bytes 524320 | tf_op jit(solution)/shard_map/ppermute | solution.py:18
  117.4 9.8 %collective-permute-done.16.refs_1_ = f32[512,256]{1,0:T(8,128)S(1)} collective-permute-done((f32[512,256]{1,0:T(8,128)S(1)}, f32[512,256]{1,0:T(8,128)S(1)}, u32[]{:S(2)}, u32[]{:S(2)}) %collective-permute-start.16) | collective-permute-done | bytes 524320 | tf_op jit(solution)/shard_map/ppermute | solution.py:18
  137.4 13.2 %collective-permute-done.22 = f32[512,256]{1,0:T(8,128)S(1)} collective-permute-done((f32[512,256]{1,0:T(8,128)S(1)}, f32[512,256]{1,0:T(8,128)S(1)}, u32[]{:S(2)}, u32[]{:S(2)}) %collective-permute-start.22) | collective-permute-done | bytes 524320 | tf_op jit(solution)/shard_map/ppermute | solution.py:18
  150.7 7.5 %collective-permute-start.23 = (f32[512,256]{1,0:T(8,128)S(1)}, f32[512,256]{1,0:T(8,128)S(1)}, u32[]{:S(2)}, u32[]{:S(2)}) collective-permute-start(f32[512,256]{1,0:T(8,128)S(1)} %add.220), channel_id=1, source_target_pairs={{0,8},{4,12},{8,0},{12,4},{16,24},{20,28},{24,16},{28,20},{1,9},{5... | collective-permute-start | bytes 1572872 | tf_op jit(solution)/shard_map/ppermute | solution.py:18
  163.9 9.2 %collective-permute-done.23 = f32[512,256]{1,0:T(8,128)S(1)} collective-permute-done((f32[512,256]{1,0:T(8,128)S(1)}, f32[512,256]{1,0:T(8,128)S(1)}, u32[]{:S(2)}, u32[]{:S(2)}) %collective-permute-start.23) | collective-permute-done | bytes 524320 | tf_op jit(solution)/shard_map/ppermute | solution.py:18
  173.2 10.3 %collective-permute-done.21 = f32[512,256]{1,0:T(8,128)S(1)} collective-permute-done((f32[512,256]{1,0:T(8,128)S(1)}, f32[512,256]{1,0:T(8,128)S(1)}, u32[]{:S(2)}, u32[]{:S(2)}) %collective-permute-start.21) | collective-permute-done | bytes 524320 | tf_op jit(solution)/shard_map/ppermute | solution.py:18
  185.6 7.5 %root_lower_0.1 = (f32[640,256]{1,0:T(8,128)S(1)}, bf16[1,2560,512]{2,1,0:T(8,128)(2,1)S(1)}) custom-call(s32[72]{0:T(128)S(1)} %concatenate.22.m.meta_ref, f32[1,1280,2560]{2,1,0:T(8,128)} %bitcast.31, f32[2560,256]{1,0:T(8,128)S(1)} %copy-done.10, f32[512,256]{1,0:T(8,128)S(1)} %add.218.refs_1_, f32[512,256]{1,0:T(8,128)S(1)} %add.221.refs_2_, ...), custom_call_target="tpu_custom_call" | custom-call | flops 2516582400 | bytes 6553600 | tf_op jit(solution)/shard_map/root_lower_0/pallas_call | solution.py:130
  193.1 6.5 %root_lower_1.1 = f32[640,256]{1,0:T(8,128)S(1)} custom-call(s32[72]{0:T(128)S(1)} %concatenate.22.m.meta_ref, f32[1,1280,2560]{2,1,0:T(8,128)} %bitcast.32, bf16[1,2560,512]{2,1,0:T(8,128)(2,1)S(1)} %get-tuple-element.43.refs_0_), custom_call_target="tpu_custom_call" | custom-call | flops 2516582400 | bytes 6553600 | tf_op jit(solution)/shard_map/root_lower_1/pallas_call | solution.py:130
  201.7 14.7 %collective-permute-done.28 = f32[640,256]{1,0:T(8,128)S(1)} collective-permute-done((f32[640,256]{1,0:T(8,128)S(1)}, f32[640,256]{1,0:T(8,128)S(1)}, u32[]{:S(2)}, u32[]{:S(2)}) %collective-permute-start.28) | collective-permute-done | bytes 655392 | tf_op jit(solution)/shard_map/ppermute | solution.py:18
  218.8 13.7 %collective-permute-done.29.refs_3_ = f32[640,256]{1,0:T(8,128)S(1)} collective-permute-done((f32[640,256]{1,0:T(8,128)S(1)}, f32[640,256]{1,0:T(8,128)S(1)}, u32[]{:S(2)}, u32[]{:S(2)}) %collective-permute-start.29) | collective-permute-done | bytes 655392 | tf_op jit(solution)/shard_map/ppermute | solution.py:18
  250.2 15.6 %collective-permute-done.33 = f32[640,256]{1,0:T(8,128)S(1)} collective-permute-done((f32[640,256]{1,0:T(8,128)S(1)}, f32[640,256]{1,0:T(8,128)S(1)}, u32[]{:S(2)}, u32[]{:S(2)}) %collective-permute-start.33) | collective-permute-done | bytes 655392 | tf_op jit(solution)/shard_map/ppermute | solution.py:18
  265.9 14.2 %collective-permute-start.34 = (f32[640,256]{1,0:T(8,128)S(1)}, f32[640,256]{1,0:T(8,128)S(1)}, u32[]{:S(2)}, u32[]{:S(2)}) collective-permute-start(f32[640,256]{1,0:T(8,128)S(1)} %add.228), channel_id=1, source_target_pairs={{0,8},{4,12},{8,0},{12,4},{16,24},{20,28},{24,16},{28,20},{1,9},{5... | collective-permute-start | bytes 1966088 | tf_op jit(solution)/shard_map/ppermute | solution.py:18
  282.6 12.6 %collective-permute-done.34 = f32[640,256]{1,0:T(8,128)S(1)} collective-permute-done((f32[640,256]{1,0:T(8,128)S(1)}, f32[640,256]{1,0:T(8,128)S(1)}, u32[]{:S(2)}, u32[]{:S(2)}) %collective-permute-start.34) | collective-permute-done | bytes 655392 | tf_op jit(solution)/shard_map/ppermute | solution.py:18
  295.4 15.5 %collective-permute-done.32 = f32[640,256]{1,0:T(8,128)S(1)} collective-permute-done((f32[640,256]{1,0:T(8,128)S(1)}, f32[640,256]{1,0:T(8,128)S(1)}, u32[]{:S(2)}, u32[]{:S(2)}) %collective-permute-start.32) | collective-permute-done | bytes 655392 | tf_op jit(solution)/shard_map/ppermute | solution.py:18
  321.9 11.5 %collective-permute-done.39 = f32[512,256]{1,0:T(8,128)S(1)} collective-permute-done((f32[512,256]{1,0:T(8,128)S(1)}, f32[512,256]{1,0:T(8,128)S(1)}, u32[]{:S(2)}, u32[]{:S(2)}) %collective-permute-start.39) | collective-permute-done | bytes 524320 | tf_op jit(solution)/shard_map/ppermute | solution.py:18
  336.1 10.5 %collective-permute-done.40.refs_7_ = f32[512,256]{1,0:T(8,128)S(1)} collective-permute-done((f32[512,256]{1,0:T(8,128)S(1)}, f32[512,256]{1,0:T(8,128)S(1)}, u32[]{:S(2)}, u32[]{:S(2)}) %collective-permute-start.40) | collective-permute-done | bytes 524320 | tf_op jit(solution)/shard_map/ppermute | solution.py:18
  353.9 14.9 %collective-permute-done.44 = f32[512,256]{1,0:T(8,128)S(1)} collective-permute-done((f32[512,256]{1,0:T(8,128)S(1)}, f32[512,256]{1,0:T(8,128)S(1)}, u32[]{:S(2)}, u32[]{:S(2)}) %collective-permute-start.44) | collective-permute-done | bytes 524320 | tf_op jit(solution)/shard_map/ppermute | solution.py:18
  368.9 9.3 %collective-permute-start.45 = (f32[512,256]{1,0:T(8,128)S(1)}, f32[512,256]{1,0:T(8,128)S(1)}, u32[]{:S(2)}, u32[]{:S(2)}) collective-permute-start(f32[512,256]{1,0:T(8,128)S(1)} %add.236), channel_id=1, source_target_pairs={{0,8},{4,12},{8,0},{12,4},{16,24},{20,28},{24,16},{28,20},{1,9},{5... | collective-permute-start | bytes 1572872 | tf_op jit(solution)/shard_map/ppermute | solution.py:18
  381.1 9.7 %collective-permute-done.45 = f32[512,256]{1,0:T(8,128)S(1)} collective-permute-done((f32[512,256]{1,0:T(8,128)S(1)}, f32[512,256]{1,0:T(8,128)S(1)}, u32[]{:S(2)}, u32[]{:S(2)}) %collective-permute-start.45) | collective-permute-done | bytes 524320 | tf_op jit(solution)/shard_map/ppermute | solution.py:18
  391.0 11.0 %collective-permute-done.43 = f32[512,256]{1,0:T(8,128)S(1)} collective-permute-done((f32[512,256]{1,0:T(8,128)S(1)}, f32[512,256]{1,0:T(8,128)S(1)}, u32[]{:S(2)}, u32[]{:S(2)}) %collective-permute-start.43) | collective-permute-done | bytes 524320 | tf_op jit(solution)/shard_map/ppermute | solution.py:18
  412.0 9.8 %collective-permute-done.48 = f32[512,256]{1,0:T(8,128)S(1)} collective-permute-done((f32[512,256]{1,0:T(8,128)S(1)}, f32[512,256]{1,0:T(8,128)S(1)}, u32[]{:S(2)}, u32[]{:S(2)}) %collective-permute-start.48) | collective-permute-done | bytes 524320 | tf_op jit(solution)/shard_map/ppermute | solution.py:18
  436.8 8.2 %collective-permute-done.52 = f32[512,256]{1,0:T(8,128)S(1)} collective-permute-done((f32[512,256]{1,0:T(8,128)S(1)}, f32[512,256]{1,0:T(8,128)S(1)}, u32[]{:S(2)}, u32[]{:S(2)}) %collective-permute-start.52) | collective-permute-done | bytes 524320 | tf_op jit(solution)/shard_map/ppermute | solution.py:18
  (191 shorter events, 190.7 us)
Async XLA Ops:
  8.8 15.0 %collective-permute-start = (f32[512,256]{1,0:T(8,128)S(1)}, f32[512,256]{1,0:T(8,128)S(1)}, u32[]{:S(2)}, u32[]{:S(2)}) collective-permute-start(f32[512,256]{1,0:T(8,128)S(1)} %get-tuple-element.33), channel_id=1, source_target_pairs={{0,1},{1,0},{2,3},{3,2},{4,5},{5,4},{6,7},{7,6},{8,9},{9,8},{10,11... | collective-permute-start | bytes 1572872 | tf_op jit(solution)/shard_map/ppermute | solution.py:18
  59.3 20.5 %collective-permute-start.12 = (f32[256,256]{1,0:T(8,128)S(1)}, f32[256,256]{1,0:T(8,128)}, u32[]{:S(2)}, u32[]{:S(2)}) collective-permute-start(f32[256,256]{1,0:T(8,128)S(1)} %fusion.5.refs_4_.refs_5_), channel_id=1, source_target_pairs={{0,8},{4,12},{8,0},{12,4},{16,24},{20,28},{24,16},{28,20},{1,9},{5... | collective-permute-start | bytes 786440 | tf_op jit(solution)/shard_map/ppermute | solution.py:18
  61.4 22.2 %collective-permute-start.7 = (f32[256,256]{1,0:T(8,128)S(1)}, f32[256,256]{1,0:T(8,128)}, u32[]{:S(2)}, u32[]{:S(2)}) collective-permute-start(f32[256,256]{1,0:T(8,128)S(1)} %fusion.7.refs_0_.refs_4_), channel_id=1, source_target_pairs={{0,24},{4,28},{8,16},{12,20},{16,8},{20,12},{24,0},{28,4},{1,25},{... | collective-permute-start | bytes 786440 | tf_op jit(solution)/shard_map/ppermute | solution.py:18
  66.5 22.0 %collective-permute-start.13 = (f32[256,256]{1,0:T(8,128)S(1)}, f32[256,256]{1,0:T(8,128)}, u32[]{:S(2)}, u32[]{:S(2)}) collective-permute-start(f32[256,256]{1,0:T(8,128)S(1)} %collective-permute-done.11.refs_5_), channel_id=1, source_target_pairs={{0,8},{4,12},{8,0},{12,4},{16,24},{20,28},{24,16},{28,20},{1,9},{5... | collective-permute-start | bytes 786440 | tf_op jit(solution)/shard_map/ppermute | solution.py:18
  71.5 19.8 %collective-permute-start.8 = (f32[256,256]{1,0:T(8,128)}, f32[256,256]{1,0:T(8,128)}, u32[]{:S(2)}, u32[]{:S(2)}) collective-permute-start(f32[256,256]{1,0:T(8,128)} %collective-permute-done.6.refs_1_), channel_id=1, source_target_pairs={{0,24},{4,28},{8,16},{12,20},{16,8},{20,12},{24,0},{28,4},{1,25},{... | collective-permute-start | bytes 786440 | tf_op jit(solution)/shard_map/ppermute | solution.py:18
  101.8 14.8 %collective-permute-start.17 = (f32[512,256]{1,0:T(8,128)S(1)}, f32[512,256]{1,0:T(8,128)S(1)}, u32[]{:S(2)}, u32[]{:S(2)}) collective-permute-start(f32[512,256]{1,0:T(8,128)S(1)} %mid_lower_1.1), channel_id=1, source_target_pairs={{0,2},{1,3},{2,0},{3,1},{4,6},{5,7},{6,4},{7,5},{8,10},{9,11},{10,... | collective-permute-start | bytes 1572872 | tf_op jit(solution)/shard_map/ppermute | solution.py:18
  133.8 16.7 %collective-permute-start.22 = (f32[512,256]{1,0:T(8,128)S(1)}, f32[512,256]{1,0:T(8,128)S(1)}, u32[]{:S(2)}, u32[]{:S(2)}) collective-permute-start(f32[512,256]{1,0:T(8,128)S(1)} %get-tuple-element.67), channel_id=1, source_target_pairs={{0,24},{4,28},{8,16},{12,20},{16,8},{20,12},{24,0},{28,4},{1,25},{... | collective-permute-start | bytes 1572872 | tf_op jit(solution)/shard_map/ppermute | solution.py:18
  137.4 23.7 %collective-permute-start.20 = (f32[512,256]{1,0:T(8,128)S(1)}, f32[512,256]{1,0:T(8,128)S(1)}, u32[]{:S(2)}, u32[]{:S(2)}) collective-permute-start(f32[512,256]{1,0:T(8,128)S(1)} %get-tuple-element.68), channel_id=1, source_target_pairs={{0,8},{4,12},{8,0},{12,4},{16,24},{20,28},{24,16},{28,20},{1,9},{5... | collective-permute-start | bytes 1572872 | tf_op jit(solution)/shard_map/ppermute | solution.py:18
  150.7 22.4 %collective-permute-start.23 = (f32[512,256]{1,0:T(8,128)S(1)}, f32[512,256]{1,0:T(8,128)S(1)}, u32[]{:S(2)}, u32[]{:S(2)}) collective-permute-start(f32[512,256]{1,0:T(8,128)S(1)} %add.220), channel_id=1, source_target_pairs={{0,8},{4,12},{8,0},{12,4},{16,24},{20,28},{24,16},{28,20},{1,9},{5... | collective-permute-start | bytes 1572872 | tf_op jit(solution)/shard_map/ppermute | solution.py:18
  161.2 22.4 %collective-permute-start.21 = (f32[512,256]{1,0:T(8,128)S(1)}, f32[512,256]{1,0:T(8,128)S(1)}, u32[]{:S(2)}, u32[]{:S(2)}) collective-permute-start(f32[512,256]{1,0:T(8,128)S(1)} %add.217), channel_id=1, source_target_pairs={{0,24},{4,28},{8,16},{12,20},{16,8},{20,12},{24,0},{28,4},{1,25},{... | collective-permute-start | bytes 1572872 | tf_op jit(solution)/shard_map/ppermute | solution.py:18
  199.6 16.8 %collective-permute-start.28 = (f32[640,256]{1,0:T(8,128)S(1)}, f32[640,256]{1,0:T(8,128)S(1)}, u32[]{:S(2)}, u32[]{:S(2)}) collective-permute-start(f32[640,256]{1,0:T(8,128)S(1)} %root_lower_1.1), channel_id=1, source_target_pairs={{0,2},{1,3},{2,0},{3,1},{4,6},{5,7},{6,4},{7,5},{8,10},{9,11},{10,... | collective-permute-start | bytes 1966088 | tf_op jit(solution)/shard_map/ppermute | solution.py:18
  201.1 16.5 %collective-permute-start.26 = (f32[640,256]{1,0:T(8,128)S(1)}, f32[640,256]{1,0:T(8,128)S(1)}, u32[]{:S(2)}, u32[]{:S(2)}) collective-permute-start(f32[640,256]{1,0:T(8,128)S(1)} %get-tuple-element.42), channel_id=1, source_target_pairs={{0,1},{1,0},{2,3},{3,2},{4,5},{5,4},{6,7},{7,6},{8,9},{9,8},{10,11... | collective-permute-start | bytes 1966088 | tf_op jit(solution)/shard_map/ppermute | solution.py:18
  216.5 16.0 %collective-permute-start.29 = (f32[640,256]{1,0:T(8,128)S(1)}, f32[640,256]{1,0:T(8,128)S(1)}, u32[]{:S(2)}, u32[]{:S(2)}) collective-permute-start(f32[640,256]{1,0:T(8,128)S(1)} %add.223.refs_2_), channel_id=1, source_target_pairs={{0,1},{1,0},{2,3},{3,2},{4,5},{5,4},{6,7},{7,6},{8,9},{9,8},{10,11... | collective-permute-start | bytes 1966088 | tf_op jit(solution)/shard_map/ppermute | solution.py:18
  217.7 15.7 %collective-permute-start.27 = (f32[640,256]{1,0:T(8,128)S(1)}, f32[640,256]{1,0:T(8,128)S(1)}, u32[]{:S(2)}, u32[]{:S(2)}) collective-permute-start(f32[640,256]{1,0:T(8,128)S(1)} %add.222.refs_0_), channel_id=1, source_target_pairs={{0,2},{1,3},{2,0},{3,1},{4,6},{5,7},{6,4},{7,5},{8,10},{9,11},{10,... | collective-permute-start | bytes 1966088 | tf_op jit(solution)/shard_map/ppermute | solution.py:18
  246.3 19.5 %collective-permute-start.33 = (f32[640,256]{1,0:T(8,128)S(1)}, f32[640,256]{1,0:T(8,128)S(1)}, u32[]{:S(2)}, u32[]{:S(2)}) collective-permute-start(f32[640,256]{1,0:T(8,128)S(1)} %get-tuple-element.63), channel_id=1, source_target_pairs={{0,24},{4,28},{8,16},{12,20},{16,8},{20,12},{24,0},{28,4},{1,25},{... | collective-permute-start | bytes 1966088 | tf_op jit(solution)/shard_map/ppermute | solution.py:18
  249.8 30.3 %collective-permute-start.31 = (f32[640,256]{1,0:T(8,128)S(1)}, f32[640,256]{1,0:T(8,128)S(1)}, u32[]{:S(2)}, u32[]{:S(2)}) collective-permute-start(f32[640,256]{1,0:T(8,128)S(1)} %get-tuple-element.64), channel_id=1, source_target_pairs={{0,8},{4,12},{8,0},{12,4},{16,24},{20,28},{24,16},{28,20},{1,9},{5... | collective-permute-start | bytes 1966088 | tf_op jit(solution)/shard_map/ppermute | solution.py:18
  265.9 29.3 %collective-permute-start.34 = (f32[640,256]{1,0:T(8,128)S(1)}, f32[640,256]{1,0:T(8,128)S(1)}, u32[]{:S(2)}, u32[]{:S(2)}) collective-permute-start(f32[640,256]{1,0:T(8,128)S(1)} %add.228), channel_id=1, source_target_pairs={{0,8},{4,12},{8,0},{12,4},{16,24},{20,28},{24,16},{28,20},{1,9},{5... | collective-permute-start | bytes 1966088 | tf_op jit(solution)/shard_map/ppermute | solution.py:18
  280.2 30.7 %collective-permute-start.32 = (f32[640,256]{1,0:T(8,128)S(1)}, f32[640,256]{1,0:T(8,128)S(1)}, u32[]{:S(2)}, u32[]{:S(2)}) collective-permute-start(f32[640,256]{1,0:T(8,128)S(1)} %add.225), channel_id=1, source_target_pairs={{0,24},{4,28},{8,16},{12,20},{16,8},{20,12},{24,0},{28,4},{1,25},{... | collective-permute-start | bytes 1966088 | tf_op jit(solution)/shard_map/ppermute | solution.py:18
  295.3 15.7 %collective-permute-start.36 = (f32[640,256]{1,0:T(8,128)S(1)}, f32[640,256]{1,0:T(8,128)S(1)}, u32[]{:S(2)}, u32[]{:S(2)}) collective-permute-start(f32[640,256]{1,0:T(8,128)S(1)} %add.229.refs_1_), channel_id=1, source_target_pairs={{0,4},{4,0},{8,12},{12,8},{16,20},{20,16},{24,28},{28,24},{1,5},{5... | collective-permute-start | bytes 1966088 | tf_op jit(solution)/shard_map/ppermute | solution.py:18
  352.1 16.7 %collective-permute-start.44 = (f32[512,256]{1,0:T(8,128)S(1)}, f32[512,256]{1,0:T(8,128)S(1)}, u32[]{:S(2)}, u32[]{:S(2)}) collective-permute-start(f32[512,256]{1,0:T(8,128)S(1)} %get-tuple-element.65), channel_id=1, source_target_pairs={{0,24},{4,28},{8,16},{12,20},{16,8},{20,12},{24,0},{28,4},{1,25},{... | collective-permute-start | bytes 1572872 | tf_op jit(solution)/shard_map/ppermute | solution.py:18
  353.9 25.3 %collective-permute-start.42 = (f32[512,256]{1,0:T(8,128)S(1)}, f32[512,256]{1,0:T(8,128)S(1)}, u32[]{:S(2)}, u32[]{:S(2)}) collective-permute-start(f32[512,256]{1,0:T(8,128)S(1)} %get-tuple-element.66), channel_id=1, source_target_pairs={{0,8},{4,12},{8,0},{12,4},{16,24},{20,28},{24,16},{28,20},{1,9},{5... | collective-permute-start | bytes 1572872 | tf_op jit(solution)/shard_map/ppermute | solution.py:18
  368.9 22.0 %collective-permute-start.45 = (f32[512,256]{1,0:T(8,128)S(1)}, f32[512,256]{1,0:T(8,128)S(1)}, u32[]{:S(2)}, u32[]{:S(2)}) collective-permute-start(f32[512,256]{1,0:T(8,128)S(1)} %add.236), channel_id=1, source_target_pairs={{0,8},{4,12},{8,0},{12,4},{16,24},{20,28},{24,16},{28,20},{1,9},{5... | collective-permute-start | bytes 1572872 | tf_op jit(solution)/shard_map/ppermute | solution.py:18
  379.3 22.7 %collective-permute-start.43 = (f32[512,256]{1,0:T(8,128)S(1)}, f32[512,256]{1,0:T(8,128)S(1)}, u32[]{:S(2)}, u32[]{:S(2)}) collective-permute-start(f32[512,256]{1,0:T(8,128)S(1)} %add.233), channel_id=1, source_target_pairs={{0,24},{4,28},{8,16},{12,20},{16,8},{20,12},{24,0},{28,4},{1,25},{... | collective-permute-start | bytes 1572872 | tf_op jit(solution)/shard_map/ppermute | solution.py:18
  408.8 14.5 %collective-permute-start.50 = (f32[512,256]{1,0:T(8,128)S(1)}, f32[512,256]{1,0:T(8,128)S(1)}, u32[]{:S(2)}, u32[]{:S(2)}) collective-permute-start(f32[512,256]{1,0:T(8,128)S(1)} %get-tuple-element.52), channel_id=1, source_target_pairs={{0,2},{1,3},{2,0},{3,1},{4,6},{5,7},{6,4},{7,5},{8,10},{9,11},{10,... | collective-permute-start | bytes 1572872 | tf_op jit(solution)/shard_map/ppermute | solution.py:18
  (47 other events, 593.0 us)

commit v2 on v1

--- a/solution.py
+++ b/solution.py
@@ -10,7 +10,9 @@
 F32 = jnp.float32
 BF16 = jnp.bfloat16
 CHAINS = 1
-BLOCK_BYTES = 1 << 21
+Z_STREAMS = 2
+BLOCK_BYTES = 13 << 18
+CUTS = 2
 VMEM_LIMIT = 40 << 20
 
 
@@ -25,11 +27,13 @@
     return [masks[0] ^ c for c in rest] + rest
 
 
-def pick_rows(rows, depth):
-    best = 8
-    for d in range(8, rows + 1, 8):
-        if rows % d == 0 and d * depth * 4 <= BLOCK_BYTES:
+def pick_depth(rows, depth):
+    best = depth
+    for d in range(128, depth, 128):
+        if depth % d == 0 and (rows * d * 4 <= BLOCK_BYTES or d == 128):
             best = d
+    if rows * depth * 4 <= BLOCK_BYTES:
+        best = depth
     return best
 
 
@@ -54,13 +58,12 @@
     meta,
     matrix,
     rows,
+    groups,
     width,
     index,
     ins,
-    outs,
+    prologue=None,
     slots=1,
-    slot_of=None,
-    prologue=None,
     extra=(),
     x2=None,
     keep_x2=False,
@@ -68,56 +71,87 @@
     finish=None,
     sign=1.0,
     in_specs=None,
+    blocks=1,
+    cuts=1,
+    order=None,
 ):
     depth = matrix.shape[2]
-    total = sum(outs)
-    steps = total // rows
-    per = steps // len(outs)
-    n_in, n_out, n_extra = len(ins), len(outs), len(extra)
+    chunk = pick_depth(rows * blocks, depth)
+    steps = depth // chunk
+    outs = groups * blocks * cuts if order is None else 1
+    piece = rows // cuts
+    n_in, n_extra = len(ins), len(extra)
     x2_shape = (slots, depth, 2 * width)
     given = x2 is not None
 
     def whole(a):
         nd = len(a)
-        return pl.BlockSpec(a, lambda i, m, nd=nd: (0,) * nd)
-
-    def kernel(meta_ref, a_ref, *refs):
-        i = pl.program_id(0)
+        return pl.BlockSpec(a, lambda g, k, m, nd=nd: (0,) * nd)
+
+    def kernel(meta_ref, *refs):
+        g, k = pl.program_id(0), pl.program_id(1)
+        a_refs, refs = refs[:blocks], refs[blocks:]
         in_refs, refs = refs[:n_in], refs[n_in:]
         if given:
             x2_ref, refs = refs[0], refs[1:]
-        out_refs, refs = refs[:n_out], refs[n_out:]
+        out_refs, refs = refs[:outs], refs[outs:]
         extra_refs, refs = refs[:n_extra], refs[n_extra:]
         if not given:
             x2_ref, refs = refs[0], refs[1:]
 
-            @pl.when(i == 0)
+            @pl.when((g == 0) & (k == 0))
             def _():
                 prologue(meta_ref, in_refs, extra_refs, x2_ref, refs)
 
-        slot = 0 if slot_of is None else slot_of(i)
-        acc = product(a_ref[0], x2_ref[slot])
+        slot = 0 if slots == 1 else g
+        part = x2_ref[slot, pl.ds(pl.multiple_of(k * chunk, chunk), chunk), :]
+        whole_a = [a[0] for a in a_refs]
+        acc = product(whole_a[0] if blocks == 1 else jnp.concatenate(whole_a, axis=0), part)
         if sign != 1.0:
             acc = -acc
-        for j in range(n_out):
-
-            @pl.when(i // per == j)
-            def _():
-                start = pl.multiple_of((i - j * per) * rows, rows)
-                out_refs[j][pl.ds(start, rows), :] = acc
+        def write(ref, to, value, first):
+            ref[to, :] = value if first else ref[to, :] + value
+
+        def store(first):
+            if order is not None:
+                for start, size, to in order(meta_ref, g):
+                    to = pl.ds(pl.multiple_of(to, size), size)
+                    write(out_refs[0], to, acc[start : start + size], first)
+                return
+            for own in range(groups):
+
+                def body():
+                    for c in range(blocks * cuts):
+                        value = acc[c * piece : (c + 1) * piece]
+                        write(out_refs[own * blocks * cuts + c], pl.ds(0, piece), value, first)
+
+                if groups == 1:
+                    body()
+                else:
+                    pl.when(g == own)(body)
+
+        if steps == 1:
+            store(True)
+        else:
+            pl.when(k == 0)(lambda: store(True))
+            pl.when(k != 0)(lambda: store(False))
 
         if finish is not None:
 
-            @pl.when(i == steps - 1)
+            @pl.when((g == groups - 1) & (k == steps - 1))
             def _():
                 finish(meta_ref, in_refs, out_refs)
 
-    out_shape = [jax.ShapeDtypeStruct((r, width), F32) for r in outs]
+    out_rows = piece if order is None else groups * rows
+    out_shape = [jax.ShapeDtypeStruct((out_rows, width), F32)] * outs
     out_shape += [jax.ShapeDtypeStruct(e, F32) for e in extra]
     out_specs = [whole(o.shape) for o in out_shape]
     scratch_shapes = list(scratch)
-    args = [matrix, *ins]
-    specs = [pl.BlockSpec((1, rows, depth), lambda i, m: (*index(i, m), 0))]
+    args = [matrix] * blocks + list(ins)
+    specs = [
+        pl.BlockSpec((1, rows, chunk), lambda g, k, m, q=q: (*index(q if groups == 1 else g, m), k))
+        for q in range(blocks)
+    ]
     specs += in_specs if in_specs is not None else [whole(a.shape) for a in ins]
     if given:
         args.append(x2)
@@ -132,17 +166,17 @@
         out_shape=out_shape,
         grid_spec=pltpu.PrefetchScalarGridSpec(
             num_scalar_prefetch=1,
-            grid=(steps,),
+            grid=(groups, steps),
             in_specs=specs,
             out_specs=out_specs,
             scratch_shapes=scratch_shapes,
         ),
         compiler_params=pltpu.CompilerParams(
-            dimension_semantics=("arbitrary",), vmem_limit_bytes=VMEM_LIMIT
+            dimension_semantics=("arbitrary", "arbitrary"), vmem_limit_bytes=VMEM_LIMIT
         ),
         cost_estimate=pl.CostEstimate(
-            flops=6 * total * depth * width,
-            bytes_accessed=4 * total * depth,
+            flops=6 * groups * blocks * rows * depth * width,
+            bytes_accessed=4 * groups * blocks * rows * depth,
             transcendentals=0,
         ),
         name=name,
@@ -180,52 +214,91 @@
     z_bits = n_sub.bit_length() - 2
     f_masks = [1 << j for j in range(f_bits)]
     f_masks = [f_masks, f_masks[::-1]]
-    z_masks = [2 * ((2 << j) - 1) for j in range(z_bits)]
-    z_masks = [z_masks, z_masks[::-1]]
+    z_masks = [2 << j for j in range(z_bits)]
     over_front = lambda x, m: partner(x, "front", m, n_front)
     over_sub = lambda x, m: partner(x, "subtree", m, n_sub)
 
-    def scatter_sum(send, keep, masks):
-        for j, m in enumerate(masks):
-            got = over_front(send, m)
-            if j + 1 == len(masks):
-                return keep, got
-            h = keep.shape[0] // 2
-            send, keep = keep[:h] + got[:h], keep[h:] + got[h:]
-
-    def sum_front(value, masks):
-        for m in masks[:-1]:
-            value = value + over_front(value, m)
-        return value, over_front(value, masks[-1])
+    def scatter_sum(blocks, masks):
+        terms = [[b] for b in blocks]
+        for m in masks:
+            h = len(terms) // 2
+            got = [over_front(sum(b), m) for b in terms[:h]]
+            terms = [keep + [g] for keep, g in zip(terms[h:], got)]
+        return terms[0]
+
+    def sum_front(values, masks):
+        terms = []
+        for value in values:
+            for m in masks[:-1]:
+                value = value + over_front(value, m)
+            terms += [value, over_front(value, masks[-1])]
+        return terms
+
+    top = z_bits - 1
+    n_pieces = Z_STREAMS << top
 
     def sum_subtree(send, keep):
         got = over_sub(send, 1)
-        h = keep.shape[0] // 2
+        h = keep.shape[0] // Z_STREAMS
         mine, other = [], []
-        for t in range(2):
-            value = keep[t * h : (t + 1) * h] + got[t * h : (t + 1) * h]
-            for m in z_masks[t]:
-                value = value + over_sub(value, m)
-            mine.append(value)
-            other.append(over_sub(value, 1))
+        for t in range(Z_STREAMS):
+            parts = [keep[t * h : (t + 1) * h], got[t * h : (t + 1) * h]]
+            for j in range(top):
+                n = parts[0].shape[0] // 2
+                leave = sum(x[:n] for x in parts)
+                parts = [sum(x[n:] for x in parts), over_sub(leave, z_masks[j])]
+            value = sum(parts)
+            value = value + over_sub(value, z_masks[top])
+            pieces = [value]
+            for j in reversed(range(top)):
+                pieces += [over_sub(p, z_masks[j]) for p in pieces]
+            mine += pieces
+            other += [over_sub(p, 1) for p in pieces]
         return mine, other
 
+    def leave_first(groups, rows):
+        per = n_pieces // groups
+        size = rows // per
+
+        def order(m, g):
+            return [(p * size, size, ((g * per + p) ^ m[at["flip"]]) * size) for p in range(per)]
+
+        return order
+
+    piece_bits = [0]
+    for j in reversed(range(top)):
+        piece_bits += [o | (1 << j) for o in piece_bits]
+
+    def piece_starts(m, half_rows):
+        stream = half_rows // Z_STREAMS
+        for w in range(2):
+            for t in range(Z_STREAMS):
+                for n, off in enumerate(piece_bits):
+                    z = (m[at["self"]] // 2) ^ off
+                    start = (m[at["core"]] ^ w) * half_rows + t * stream
+                    for j in range(top):
+                        start = start + ((z >> j) & 1) * (stream >> (j + 1))
+                    yield (w * Z_STREAMS + t) * len(piece_bits) + n, start
+
     def leaf_phase(name, meta_, matrix, ins, prologue, extra=()):
-        half = n_front // 2
-        rows = half_leaf
-        first = lambda base: (lambda i, m: (0, m[base + i]))
-        outs = [half * rows] * 2
-        res = matmul(
-            name + "_send", meta_, matrix, rows, width, first(at["order"]), ins, outs,
-            prologue=prologue, extra=extra, keep_x2=True,
-        )
-        sends, extras, x2 = res[:2], res[2:-1], res[-1]
-        keeps = matmul(
-            name + "_keep", meta_, matrix, rows, width, first(at["order"] + n_front), [], outs, x2=x2
-        )
-        terms = []
-        for t in range(2):
-            terms += scatter_sum(sends[t], keeps[t], f_masks[t])
+        early = max(n_front // 4, 1)
+        spots = [[t * n_front + n for n in range(n_front)] for t in range(2)]
+        calls = [spots[0][:early] + spots[1][:early], spots[0][early:] + spots[1][early:]]
+        made, extras, x2 = {}, (), None
+        for call, chosen in enumerate(calls):
+
+            def pick(q, m, chosen=chosen):
+                return 0, m[at["order"] + chosen[q]]
+
+            res = matmul(
+                f"{name}_{call}", meta_, matrix, half_leaf, 1, width, pick,
+                ins if call == 0 else [], prologue=prologue, blocks=len(chosen),
+                extra=extra if call == 0 else (), keep_x2=call == 0, x2=x2,
+            )
+            made.update(zip(chosen, res))
+            if call == 0:
+                extras, x2 = res[len(chosen) : -1], res[-1]
+        terms = [scatter_sum([made[n] for n in spots[t]], f_masks[t]) for t in range(2)]
         return terms, extras
 
     def live_rows(m, t, value):
@@ -238,19 +311,24 @@
 
     terms, _ = leaf_phase("leaf_lower", meta0, leaf_lower, [leaf_rhs], pro)
 
+    n_terms = f_bits + 1
+
+    def total_of(refs, t, skip=0):
+        return sum(r[...] for r in refs[skip + t * n_terms : skip + (t + 1) * n_terms])
+
     def pro(m, ins, extra, x2, _):
         for t in range(2):
-            fwd = live_rows(m, t, ins[2 * t][...] + ins[2 * t + 1][...])
+            fwd = live_rows(m, t, total_of(ins, t))
             extra[0][pl.ds(t * half_leaf, half_leaf), :] = fwd
             put(x2, 0, t * half_leaf, fwd)
 
-    terms, (leaf_fwd,) = leaf_phase("leaf_below", meta0, leaf_below, terms, pro, [(local, width)])
-    contrib = [-(terms[2 * t] + terms[2 * t + 1]) for t in range(2)]
+    terms, (leaf_fwd,) = leaf_phase("leaf_below", meta0, leaf_below, terms[0] + terms[1], pro, [(local, width)])
+    contrib = [-sum(terms[t]) for t in range(2)]
 
     pieces, offsets = [], []
     for t in range(2):
         bufs, offs = [contrib[t]], [0]
-        for m in z_masks[t]:
+        for m in reversed(z_masks):
             bufs, offs = bufs + [over_sub(b, m) for b in bufs], offs + [o ^ m for o in offs]
         pieces += bufs
         offsets += [(t, o) for o in offs]
@@ -284,23 +362,20 @@
     mid_flat = mid_rhs.reshape(fronts * mid_rows, width)
 
     def front_products(name, matrix, prologue_of, ins_of, specs_of=None, extra_of=None):
-        out_rows = matrix.shape[1]
-        rows = pick_rows(out_rows, matrix.shape[2])
-        steps = out_rows // rows
         results = []
         extras = None
         for t in range(2):
             res = matmul(
-                f"{name}_{t}", meta, matrix, rows, width,
-                lambda i, m, t=t: (t * half_fronts + i // steps, i % steps),
-                ins_of(t, extras), [half_fronts * out_rows],
-                slots=half_fronts, slot_of=lambda i: i // steps, prologue=prologue_of(t),
+                f"{name}_{t}", meta, matrix, matrix.shape[1], half_fronts, width,
+                lambda g, m, t=t: (t * half_fronts + g, 0), ins_of(t, extras),
+                prologue=prologue_of(t), slots=half_fronts,
                 in_specs=specs_of(t) if specs_of else None,
-                extra=extra_of(t) if extra_of else (),
+                extra=extra_of(t) if extra_of else (), cuts=CUTS,
             )
-            if len(res) > 1:
-                extras = res[1]
-            results.append(sum_front(res[0], f_masks[t]))
+            n_parts = half_fronts * CUTS
+            if len(res) > n_parts:
+                extras = res[n_parts]
+            results.append(sum_front(res[:n_parts], f_masks[t]))
         return results, extras
 
     def pro_of(t):
@@ -314,25 +389,23 @@
     part = (half_fronts * mid_rows, width)
     mid_fwd, _ = front_products(
         "mid_lower", mid_lower, pro_of, lambda t, e: [mid_flat, pivot_mine, pivot_other],
-        specs_of=lambda t: [pl.BlockSpec(part, lambda i, m: (t, 0))] * 3,
+        specs_of=lambda t: [pl.BlockSpec(part, lambda g, k, m: (t, 0))] * 3,
     )
 
     def core_products(name, matrix, prologue_of, ins, finish_of=None, sign=1.0):
-        out_rows = matrix.shape[1]
-        rows = pick_rows(out_rows, matrix.shape[2])
-        steps = out_rows // rows
         results = []
         for flip in (1, 0):
             results += matmul(
-                f"{name}_{flip}", meta, matrix, rows, width,
-                lambda i, m, flip=flip: ((m[at["core"]] ^ flip) * half_fronts + i // steps, i % steps),
-                ins, [half_fronts * out_rows],
-                slots=half_fronts, slot_of=lambda i: i // steps, prologue=prologue_of(flip),
-                finish=finish_of(flip) if finish_of else None, sign=sign,
+                f"{name}_{flip}", meta, matrix, matrix.shape[1], half_fronts, width,
+                lambda g, m, flip=flip: ((m[at["core"]] ^ flip) * half_fronts + g, 0), ins,
+                prologue=prologue_of(flip), slots=half_fronts, sign=sign,
+                finish=finish_of(flip) if finish_of else None,
+                order=leave_first(half_fronts, matrix.shape[1]),
             )
         return sum_subtree(*results)
 
     own_rows = mid_lower.shape[1]
+    n_parts = half_fronts * CUTS
 
     def pro_of(flip):
         def pro(m, ins, extra, x2, _):
@@ -340,9 +413,9 @@
 
                 @pl.when((m[at["core"]] ^ flip) == t)
                 def _():
-                    for q in range(half_fronts):
-                        rows = pl.ds(q * own_rows, own_rows)
-                        put(x2, q, 0, ins[2 * t][rows, :] + ins[2 * t + 1][rows, :])
+                    for n in range(n_parts):
+                        value = ins[2 * (t * n_parts + n)][...] + ins[2 * (t * n_parts + n) + 1][...]
+                        put(x2, n // CUTS, n % CUTS * (own_rows // CUTS), value)
 
         return pro
 
@@ -354,8 +427,10 @@
 
                 @pl.when((row >= 0) & (row < half_fronts * mid_rows))
                 def _():
-                    rows = pl.ds(pl.multiple_of(row, sub), sub)
-                    src = ins[4 + u // per_stream]
+                    size = half_fronts * mid_rows // n_pieces
+                    to = ((row // size) ^ m[at["flip"]]) * size + row % size
+                    rows = pl.ds(pl.multiple_of(to, sub), sub)
+                    src = ins[4 * n_parts + u // per_stream]
                     outs[0][rows, :] += src[pl.ds((u % per_stream) * sub, sub), :]
 
         return finish
@@ -365,62 +440,52 @@
         "mid_below", mid_below, pro_of, fwd_terms + contrib, finish_of, sign=-1.0
     )
 
-    mid_half = half_fronts * mid_rows // 2
-
     def root_pro(m, ins, extra, x2, scr):
         total = scr[0]
         total[...] = ins[0][...]
-        for w in range(2):
-            half = m[at["core"]] ^ w
-            for t in range(2):
-                src = ins[1 + 2 * w + t]
-                for k in range(mid_half // block):
-                    row = t * mid_half + k * block
-                    front = half * half_fronts + row // mid_rows
-                    slot = m[at["root"] + front * mid_width + (row % mid_rows) // block]
-                    rows = pl.ds(pl.multiple_of(slot * block, block), block)
-                    total[rows, :] += src[pl.ds(k * block, block), :]
+        for n, start in piece_starts(m, half_fronts * mid_rows):
+            src = ins[1 + n]
+            for k in range(src.shape[0] // block):
+                slot = m[at["root"] + start // block + k]
+                rows = pl.ds(pl.multiple_of(slot * block, block), block)
+                total[rows, :] += src[pl.ds(k * block, block), :]
         put(x2, 0, 0, total[...])
 
     out_rows = root_lower.shape[0] // 2
-    rows = pick_rows(out_rows, root_lower.shape[1])
-    steps = out_rows // rows
     matrix = root_lower[None]
-    h0, x2 = matmul(
-        "root_lower_0", meta, matrix, rows, width, lambda i, m: (0, i),
-        [root_rhs, *mine, *other], [out_rows], prologue=root_pro, keep_x2=True,
-        scratch=[pltpu.VMEM((root_rows, width), F32)],
-    )
-    root_fwd = list(sum_front(h0, f_masks[0]))
-    (h1,) = matmul(
-        "root_lower_1", meta, matrix, rows, width, lambda i, m: (0, steps + i), [], [out_rows], x2=x2
+    *h0, x2 = matmul(
+        "root_lower_0", meta, matrix, out_rows, 1, width, lambda g, m: (0, 0),
+        [root_rhs, *mine, *other], prologue=root_pro, keep_x2=True,
+        scratch=[pltpu.VMEM((root_rows, width), F32)], cuts=CUTS,
+    )
+    root_fwd = sum_front(h0, f_masks[0])
+    h1 = matmul(
+        "root_lower_1", meta, matrix, out_rows, 1, width, lambda g, m: (0, 1), [], x2=x2,
+        cuts=CUTS,
     )
     root_fwd += sum_front(h1, f_masks[1])
 
     def pro(m, ins, extra, x2, _):
-        for t in range(2):
-            put(x2, 0, t * out_rows, ins[2 * t][...] + ins[2 * t + 1][...])
+        for n in range(2 * CUTS):
+            put(x2, 0, n * (out_rows // CUTS), ins[2 * n][...] + ins[2 * n + 1][...])
 
     half_root = root_rows // 2
-    rows = pick_rows(half_root, root_upper.shape[1])
-    steps_up = half_root // rows
     matrix = root_upper[None]
-    row_of = lambda flip: (lambda i, m: (0, (m[at["core"]] ^ flip) * steps_up + i))
+    row_of = lambda flip: (lambda g, m: (0, m[at["core"]] ^ flip))
     send, x2 = matmul(
-        "root_upper_1", meta, matrix, rows, width, row_of(1), root_fwd, [half_root],
-        prologue=pro, keep_x2=True,
+        "root_upper_1", meta, matrix, half_root, 1, width, row_of(1), root_fwd,
+        prologue=pro, keep_x2=True, order=leave_first(1, half_root),
     )
     (keep,) = matmul(
-        "root_upper_0", meta, matrix, rows, width, row_of(0), [], [half_root], x2=x2
+        "root_upper_0", meta, matrix, half_root, 1, width, row_of(0), [], x2=x2,
+        order=leave_first(1, half_root),
     )
     mine, other = sum_subtree(send, keep)
 
     def place(m, ins, out):
-        h = ins[0].shape[0]
-        for w in range(2):
-            for t in range(2):
-                start = (m[at["core"]] ^ w) * (2 * h) + t * h
-                out[pl.ds(pl.multiple_of(start, h), h), :] = ins[2 * w + t][...]
+        for n, start in piece_starts(m, out.shape[0] // 2):
+            h = ins[n].shape[0]
+            out[pl.ds(pl.multiple_of(start, h), h), :] = ins[n][...]
 
     def pro_of(t):
         def pro(m, ins, extra, x2, _):
@@ -449,10 +514,10 @@
 
                 @pl.when((m[at["core"]] ^ flip) == t)
                 def _():
-                    for q in range(half_fronts):
-                        rows = pl.ds(q * own_rows, own_rows)
-                        a, b, c, d = (ins[j][rows, :] for j in (2 * t, 2 * t + 1, 4 + 2 * t, 5 + 2 * t))
-                        put(x2, q, 0, (a + b) - (c + d))
+                    for n in range(n_parts):
+                        k = 2 * (t * n_parts + n)
+                        a, b, c, d = (ins[j][...] for j in (k, k + 1, 4 * n_parts + k, 4 * n_parts + k + 1))
+                        put(x2, n // CUTS, n % CUTS * (own_rows // CUTS), (a + b) - (c + d))
 
         return pro
 
@@ -469,7 +534,7 @@
 
             @pl.when(m[at["ext_root"] + u] != 0)
             def _():
-                put(x2, 0, u * sub, ins[4][rows, :])
+                put(x2, 0, u * sub, ins[-1][rows, :])
 
     terms, (mid_sol,) = leaf_phase(
         "leaf_right", meta, leaf_right, [*mine, *other, root_sol], pro,
@@ -478,11 +543,11 @@
 
     def pro(m, ins, extra, x2, _):
         for t in range(2):
-            back = ins[0][pl.ds(t * half_leaf, half_leaf), :] - (ins[1 + 2 * t][...] + ins[2 + 2 * t][...])
+            back = ins[0][pl.ds(t * half_leaf, half_leaf), :] - total_of(ins, t, 1)
             put(x2, 0, t * half_leaf, live_rows(m, t, back))
 
-    terms, _ = leaf_phase("leaf_upper", meta0, leaf_upper, [leaf_fwd, *terms], pro)
-    leaf_sol = jnp.concatenate([terms[0] + terms[1], terms[2] + terms[3]], axis=0)
+    terms, _ = leaf_phase("leaf_upper", meta0, leaf_upper, [leaf_fwd, *terms[0], *terms[1]], pro)
+    leaf_sol = jnp.concatenate([sum(terms[0]), sum(terms[1])], axis=0)
     ids = jnp.arange(local, dtype=jnp.int32)[:, None]
     leaf_sol = jnp.where(ids < meta0[at["live"]], leaf_sol, 0.0)
     return leaf_sol, mid_sol.reshape(mid_rhs.shape), root_sol
@@ -524,13 +589,15 @@
     f_bits = n_front.bit_length() - 1
     masks = [1 << j for j in range(f_bits)]
     orders = [halving_order(masks), halving_order(masks[::-1])]
-    half = n_front // 2
-    table = [(o, t) for t in range(2) for o in orders[t][:half]]
-    table += [(o, t) for t in range(2) for o in orders[t][half:]]
+    table = [(o, t) for t in range(2) for o in orders[t]]
     order = (column ^ jnp.array([o for o, _ in table], jnp.int32)) * 2
     order = order + jnp.array([t for _, t in table], jnp.int32)
     own_size = lax.dynamic_slice_in_dim(leaf_sizes, group, 1)
-    head = jnp.stack([column, group, group & 1, own_size[0] - column * local])
+    top = n_sub.bit_length() - 3
+    flip = (1 << top) - 1
+    for j in range(top):
+        flip = flip ^ (((group >> (j + 1)) & 1) << (top - 1 - j))
+    head = jnp.stack([column, group, group & 1, own_size[0] - column * local, jnp.int32(flip)])
     meta0 = jnp.concatenate([head, order])
 
     columns = lax.dynamic_slice_in_dim(leaf_map, column * leaf_width, leaf_width, 1)
@@ -556,7 +623,7 @@
         ("ext_root", own_update.astype(jnp.int32)),
         ("ext_row", ext_row),
     ]
-    at = {"self": 1, "core": 2, "live": 3, "order": 4}
+    at = {"self": 1, "core": 2, "live": 3, "flip": 4, "order": 5}
     at |= {"block": block, "sub": sub, "per_stream": per_stream}
     size = meta0.shape[0]
     for key, value in parts:

time: 454 us -> 412 us (0.907)
  waiting for transfers between devices: 278 us -> 242 us
  Pallas kernels: 62.9 us -> 56.3 us
    ppermute x56 -> x88, waiting for transfers between devices: 278 us -> 242 us  [partner(): return lax.ppermute(x, axis, [(i, i ^ mask) for i in range(n)])]
    pallas_call x20, Pallas kernels: 60.7 us -> 54.1 us  [matmul(): pl.pallas_call(kernel, out_shape=out_shape, grid_spec=pltpu.PrefetchScala...]
    ppermute x56 -> x88, starting transfers between devices: 95.5 us -> 94.5 us  [partner(): return lax.ppermute(x, axis, [(i, i ^ mask) for i in range(n)])]
  transfers between devices with their start and end apart: 56 -> 88, of which waited for: 46 -> 57; matrix products, arithmetic and copies ran while one was open for 1% -> 1% of each run, Pallas kernels for 4% -> 5%
where the time goes in v2:
time: 412 us; the launch traced here: 411 us
  waiting for transfers between devices  242 us (59%)
  starting transfers between devices  94.5 us (23%)
  Pallas kernels  56.3 us (14%)
  local copies, waits for them, and re-layouts  10.7 us (3%)
  other arithmetic  5.59 us (1%)
    ppermute x88, waiting for transfers between devices, partner(): return lax.ppermute(x, axis, [(i, i ^ mask) for i in range(n)])  242 us
    ppermute x88, starting transfers between devices, partner(): return lax.ppermute(x, axis, [(i, i ^ mask) for i in range(n)])  94.5 us
    pallas_call x20, Pallas kernels, matmul(): pl.pallas_call(kernel, out_shape=out_shape, grid_spec=pltpu.PrefetchScala...  54.1 us
  transfers between devices with their start and end apart: 88, of which 57 were waited for; matrix products, arithmetic and copies ran while one was open for 1% of the time, Pallas kernels for 5%

profile of v2, /device:TPU:0, one launch (start us, length us, event | category | flops | bytes accessed | tf_op | source)
XLA Modules:
  0.0 411.2 jit_solution(9147174360339899266)
XLA Ops:
  57.8 11.6 %collective-permute-done.9.refs_1_ = f32[256,256]{1,0:T(8,128)S(1)} collective-permute-done((f32[256,256]{1,0:T(8,128)S(1)}, f32[256,256]{1,0:T(8,128)S(1)}, u32[]{:S(2)}, u32[]{:S(2)}) %collective-permute-start.9) | collective-permute-done | bytes 262176 | tf_op jit(solution)/shard_map/ppermute | solution.py:20
  74.0 5.4 %collective-permute-done.16.refs_6_ = f32[256,256]{1,0:T(8,128)} collective-permute-done((f32[256,256]{1,0:T(8,128)S(1)}, f32[256,256]{1,0:T(8,128)}, u32[]{:S(2)}, u32[]{:S(2)}) %collective-permute-start.16) | collective-permute-done | bytes 262176 | tf_op jit(solution)/shard_map/ppermute | solution.py:20
  127.9 8.3 %collective-permute-done.31 = f32[256,256]{1,0:T(8,128)S(1)} collective-permute-done((f32[256,256]{1,0:T(8,128)S(1)}, f32[256,256]{1,0:T(8,128)S(1)}, u32[]{:S(2)}, u32[]{:S(2)}) %collective-permute-start.31) | collective-permute-done | bytes 262176 | tf_op jit(solution)/shard_map/ppermute | solution.py:20
  140.0 9.4 %collective-permute-done.28 = f32[256,256]{1,0:T(8,128)S(1)} collective-permute-done((f32[256,256]{1,0:T(8,128)S(1)}, f32[256,256]{1,0:T(8,128)S(1)}, u32[]{:S(2)}, u32[]{:S(2)}) %collective-permute-start.28) | collective-permute-done | bytes 262176 | tf_op jit(solution)/shard_map/ppermute | solution.py:20
  149.6 7.4 %collective-permute-start.33 = (f32[256,256]{1,0:T(8,128)S(1)}, f32[256,256]{1,0:T(8,128)S(1)}, u32[]{:S(2)}, u32[]{:S(2)}) collective-permute-start(f32[256,256]{1,0:T(8,128)S(1)} %add.247.refs_4_), channel_id=1, source_target_pairs={{0,8},{4,12},{8,0},{12,4},{16,24},{20,28},{24,16},{28,20},{1,9},{5... | collective-permute-start | bytes 786440 | tf_op jit(solution)/shard_map/ppermute | solution.py:20
  157.1 5.4 %collective-permute-done.29 = f32[256,256]{1,0:T(8,128)S(1)} collective-permute-done((f32[256,256]{1,0:T(8,128)S(1)}, f32[256,256]{1,0:T(8,128)S(1)}, u32[]{:S(2)}, u32[]{:S(2)}) %collective-permute-start.29) | collective-permute-done | bytes 262176 | tf_op jit(solution)/shard_map/ppermute | solution.py:20
  165.2 5.6 %collective-permute-done.30.refs_3_ = f32[256,256]{1,0:T(8,128)S(1)} collective-permute-done((f32[256,256]{1,0:T(8,128)S(1)}, f32[256,256]{1,0:T(8,128)S(1)}, u32[]{:S(2)}, u32[]{:S(2)}) %collective-permute-start.30) | collective-permute-done | bytes 262176 | tf_op jit(solution)/shard_map/ppermute | solution.py:20
  172.3 6.6 %root_lower_0.1 = (f32[320,256]{1,0:T(8,128)S(1)}, f32[320,256]{1,0:T(8,128)S(1)}, bf16[1,2560,512]{2,1,0:T(8,128)(2,1)S(1)}) custom-call(s32[73]{0:T(128)S(1)} %concatenate.22.m.meta_ref, f32[1,1280,2560]{2,1,0:T(8,128)} %bitcast.32, f32[2560,256]{1,0:T(8,128)S(1)} %copy-done.12, f32[256,256]{1,0:T(8,128)S(1)} %add.243.refs_2_, ...), custom_call_target="tpu_custom_call" | custom-call | flops 2516582400 | bytes 6553600 | tf_op jit(solution)/shard_map/root_lower_0/pallas_call | solution.py:164
  178.9 5.5 %root_lower_1.1 = (f32[320,256]{1,0:T(8,128)S(1)}, f32[320,256]{1,0:T(8,128)S(1)}) custom-call(s32[73]{0:T(128)S(1)} %concatenate.22.m.meta_ref, f32[1,1280,2560]{2,1,0:T(8,128)} %bitcast.33, bf16[1,2560,512]{2,1,0:T(8,128)(2,1)S(1)} %get-tuple-element.82.refs_1_), custom_call_target="tpu_custom_call" | custom-call | flops 2516582400 | bytes 6553600 | tf_op jit(solution)/shard_map/root_lower_1/pallas_call | solution.py:164
  188.5 6.5 %collective-permute-done.42 = f32[320,256]{1,0:T(8,128)S(1)} collective-permute-done((f32[320,256]{1,0:T(8,128)S(1)}, f32[320,256]{1,0:T(8,128)S(1)}, u32[]{:S(2)}, u32[]{:S(2)}) %collective-permute-start.42) | collective-permute-done | bytes 327712 | tf_op jit(solution)/shard_map/ppermute | solution.py:20
  195.8 5.4 %collective-permute-done.44 = f32[320,256]{1,0:T(8,128)S(1)} collective-permute-done((f32[320,256]{1,0:T(8,128)S(1)}, f32[320,256]{1,0:T(8,128)S(1)}, u32[]{:S(2)}, u32[]{:S(2)}) %collective-permute-start.44) | collective-permute-done | bytes 327712 | tf_op jit(solution)/shard_map/ppermute | solution.py:20
  205.0 6.1 %collective-permute-done.43.refs_6_ = f32[320,256]{1,0:T(8,128)S(1)} collective-permute-done((f32[320,256]{1,0:T(8,128)S(1)}, f32[320,256]{1,0:T(8,128)S(1)}, u32[]{:S(2)}, u32[]{:S(2)}) %collective-permute-start.43) | collective-permute-done | bytes 327712 | tf_op jit(solution)/shard_map/ppermute | solution.py:20
  211.1 5.6 %collective-permute-done.45.refs_8_ = f32[320,256]{1,0:T(8,128)S(1)} collective-permute-done((f32[320,256]{1,0:T(8,128)S(1)}, f32[320,256]{1,0:T(8,128)S(1)}, u32[]{:S(2)}, u32[]{:S(2)}) %collective-permute-start.45) | collective-permute-done | bytes 327712 | tf_op jit(solution)/shard_map/ppermute | solution.py:20
  217.8 6.4 %root_upper_1.1 = (f32[1280,256]{1,0:T(8,128)S(1)}, bf16[1,1280,512]{2,1,0:T(8,128)(2,1)S(1)}) custom-call(s32[73]{0:T(128)S(1)} %concatenate.22.m.meta_ref, f32[1,2560,1280]{2,1,0:T(8,128)} %bitcast.34, f32[320,256]{1,0:T(8,128)S(1)} %add.248.refs_1_, f32[320,256]{1,0:T(8,128)S(1)} %collective-permute-done.39.refs_2_, f32[320,256]{1,0:T(8,128)S(1)} %add.249.refs_3_, ...), custom_call_target="tpu_custom_call" | custom-call | flops 2516582400 | bytes 6553600 | tf_op jit(solution)/shard_map/root_upper_1/pallas_call | solution.py:164
  224.2 6.3 %root_upper_0.1 = f32[1280,256]{1,0:T(8,128)S(1)} custom-call(s32[73]{0:T(128)S(1)} %concatenate.22.m.meta_ref, f32[1,2560,1280]{2,1,0:T(8,128)} %bitcast.35, bf16[1,1280,512]{2,1,0:T(8,128)(2,1)S(1)} %get-tuple-element.85.refs_1_), custom_call_target="tpu_custom_call" | custom-call | flops 2516582400 | bytes 6553600 | tf_op jit(solution)/shard_map/root_upper_0/pallas_call | solution.py:164
  231.0 9.8 %collective-permute-done.50 = f32[320,256]{1,0:T(8,128)S(1)} collective-permute-done((f32[320,256]{1,0:T(8,128)S(1)}, f32[320,256]{1,0:T(8,128)S(1)}, u32[]{:S(2)}, u32[]{:S(2)}) %collective-permute-start.50) | collective-permute-done | bytes 327712 | tf_op jit(solution)/shard_map/ppermute | solution.py:20
  244.2 13.0 %collective-permute-done.47 = f32[320,256]{1,0:T(8,128)S(1)} collective-permute-done((f32[320,256]{1,0:T(8,128)S(1)}, f32[320,256]{1,0:T(8,128)S(1)}, u32[]{:S(2)}, u32[]{:S(2)}) %collective-permute-start.47) | collective-permute-done | bytes 327712 | tf_op jit(solution)/shard_map/ppermute | solution.py:20
  257.5 6.8 %collective-permute-start.52 = (f32[320,256]{1,0:T(8,128)S(1)}, f32[320,256]{1,0:T(8,128)S(1)}, u32[]{:S(2)}, u32[]{:S(2)}) collective-permute-start(f32[320,256]{1,0:T(8,128)S(1)} %add.259.refs_3_), channel_id=1, source_target_pairs={{0,8},{4,12},{8,0},{12,4},{16,24},{20,28},{24,16},{28,20},{1,9},{5... | collective-permute-start | bytes 983048 | tf_op jit(solution)/shard_map/ppermute | solution.py:20
  264.3 8.5 %collective-permute-done.48 = f32[320,256]{1,0:T(8,128)S(1)} collective-permute-done((f32[320,256]{1,0:T(8,128)S(1)}, f32[320,256]{1,0:T(8,128)S(1)}, u32[]{:S(2)}, u32[]{:S(2)}) %collective-permute-start.48) | collective-permute-done | bytes 327712 | tf_op jit(solution)/shard_map/ppermute | solution.py:20
  275.2 7.3 %collective-permute-done.49.refs_2_ = f32[320,256]{1,0:T(8,128)S(1)} collective-permute-done((f32[320,256]{1,0:T(8,128)S(1)}, f32[320,256]{1,0:T(8,128)S(1)}, u32[]{:S(2)}, u32[]{:S(2)}) %collective-permute-start.49) | collective-permute-done | bytes 327712 | tf_op jit(solution)/shard_map/ppermute | solution.py:20
  321.8 8.0 %collective-permute-done.69 = f32[256,256]{1,0:T(8,128)S(1)} collective-permute-done((f32[256,256]{1,0:T(8,128)S(1)}, f32[256,256]{1,0:T(8,128)S(1)}, u32[]{:S(2)}, u32[]{:S(2)}) %collective-permute-start.69) | collective-permute-done | bytes 262176 | tf_op jit(solution)/shard_map/ppermute | solution.py:20
  333.7 9.4 %collective-permute-done.66 = f32[256,256]{1,0:T(8,128)S(1)} collective-permute-done((f32[256,256]{1,0:T(8,128)S(1)}, f32[256,256]{1,0:T(8,128)S(1)}, u32[]{:S(2)}, u32[]{:S(2)}) %collective-permute-start.66) | collective-permute-done | bytes 262176 | tf_op jit(solution)/shard_map/ppermute | solution.py:20
  343.3 7.7 %collective-permute-start.71 = (f32[256,256]{1,0:T(8,128)S(1)}, f32[256,256]{1,0:T(8,128)S(1)}, u32[]{:S(2)}, u32[]{:S(2)}) collective-permute-start(f32[256,256]{1,0:T(8,128)S(1)} %add.271.refs_4_), channel_id=1, source_target_pairs={{0,8},{4,12},{8,0},{12,4},{16,24},{20,28},{24,16},{28,20},{1,9},{5... | collective-permute-start | bytes 786440 | tf_op jit(solution)/shard_map/ppermute | solution.py:20
  358.9 5.6 %collective-permute-done.68.refs_3_ = f32[256,256]{1,0:T(8,128)S(1)} collective-permute-done((f32[256,256]{1,0:T(8,128)S(1)}, f32[256,256]{1,0:T(8,128)S(1)}, u32[]{:S(2)}, u32[]{:S(2)}) %collective-permute-start.68) | collective-permute-done | bytes 262176 | tf_op jit(solution)/shard_map/ppermute | solution.py:20
  (269 shorter events, 230.7 us)
Async XLA Ops:
  51.0 18.3 %collective-permute-start.9 = (f32[256,256]{1,0:T(8,128)S(1)}, f32[256,256]{1,0:T(8,128)S(1)}, u32[]{:S(2)}, u32[]{:S(2)}) collective-permute-start(f32[256,256]{1,0:T(8,128)S(1)} %add_negate_fusion.1.refs_0_.refs_9_), channel_id=1, source_target_pairs={{0,16},{4,20},{8,24},{12,28},{16,0},{20,4},{24,8},{28,12},{1,17},{... | collective-permute-start | bytes 786440 | tf_op jit(solution)/shard_map/ppermute | solution.py:20
  54.8 17.8 %collective-permute-start.15 = (f32[256,256]{1,0:T(8,128)S(1)}, f32[256,256]{1,0:T(8,128)}, u32[]{:S(2)}, u32[]{:S(2)}) collective-permute-start(f32[256,256]{1,0:T(8,128)S(1)} %add_negate_fusion.refs_4_.refs_10_), channel_id=1, source_target_pairs={{0,16},{4,20},{8,24},{12,28},{16,0},{20,4},{24,8},{28,12},{1,17},{... | collective-permute-start | bytes 786440 | tf_op jit(solution)/shard_map/ppermute | solution.py:20
  55.7 18.3 %collective-permute-start.10 = (f32[256,256]{1,0:T(8,128)S(1)}, f32[256,256]{1,0:T(8,128)}, u32[]{:S(2)}, u32[]{:S(2)}) collective-permute-start(f32[256,256]{1,0:T(8,128)S(1)} %add_negate_fusion.1.refs_0_.refs_9_), channel_id=1, source_target_pairs={{0,8},{4,12},{8,0},{12,4},{16,24},{20,28},{24,16},{28,20},{1,9},{5... | collective-permute-start | bytes 786440 | tf_op jit(solution)/shard_map/ppermute | solution.py:20
  57.3 22.0 %collective-permute-start.16 = (f32[256,256]{1,0:T(8,128)S(1)}, f32[256,256]{1,0:T(8,128)}, u32[]{:S(2)}, u32[]{:S(2)}) collective-permute-start(f32[256,256]{1,0:T(8,128)S(1)} %add_negate_fusion.refs_4_.refs_10_), channel_id=1, source_target_pairs={{0,8},{4,12},{8,0},{12,4},{16,24},{20,28},{24,16},{28,20},{1,9},{5... | collective-permute-start | bytes 786440 | tf_op jit(solution)/shard_map/ppermute | solution.py:20
  69.4 14.7 %collective-permute-start.11 = (f32[256,256]{1,0:T(8,128)S(1)}, f32[256,256]{1,0:T(8,128)}, u32[]{:S(2)}, u32[]{:S(2)}) collective-permute-start(f32[256,256]{1,0:T(8,128)S(1)} %collective-permute-done.9.refs_1_), channel_id=1, source_target_pairs={{0,8},{4,12},{8,0},{12,4},{16,24},{20,28},{24,16},{28,20},{1,9},{5... | collective-permute-start | bytes 786440 | tf_op jit(solution)/shard_map/ppermute | solution.py:20
  72.5 14.3 %collective-permute-start.17 = (f32[256,256]{1,0:T(8,128)}, f32[256,256]{1,0:T(8,128)}, u32[]{:S(2)}, u32[]{:S(2)}) collective-permute-start(f32[256,256]{1,0:T(8,128)} %collective-permute-done.15.refs_5_), channel_id=1, source_target_pairs={{0,8},{4,12},{8,0},{12,4},{16,24},{20,28},{24,16},{28,20},{1,9},{5... | collective-permute-start | bytes 786440 | tf_op jit(solution)/shard_map/ppermute | solution.py:20
  99.2 14.3 %collective-permute-start.21 = (f32[256,256]{1,0:T(8,128)S(1)}, f32[256,256]{1,0:T(8,128)S(1)}, u32[]{:S(2)}, u32[]{:S(2)}) collective-permute-start(f32[256,256]{1,0:T(8,128)S(1)} %get-tuple-element.77), channel_id=1, source_target_pairs={{0,1},{1,0},{2,3},{3,2},{4,5},{5,4},{6,7},{7,6},{8,9},{9,8},{10,11... | collective-permute-start | bytes 786440 | tf_op jit(solution)/shard_map/ppermute | solution.py:20
  104.2 14.9 %collective-permute-start.24 = (f32[256,256]{1,0:T(8,128)S(1)}, f32[256,256]{1,0:T(8,128)S(1)}, u32[]{:S(2)}, u32[]{:S(2)}) collective-permute-start(f32[256,256]{1,0:T(8,128)S(1)} %add.238.refs_5_), channel_id=1, source_target_pairs={{0,1},{1,0},{2,3},{3,2},{4,5},{5,4},{6,7},{7,6},{8,9},{9,8},{10,11... | collective-permute-start | bytes 786440 | tf_op jit(solution)/shard_map/ppermute | solution.py:20
  109.0 14.3 %collective-permute-start.26 = (f32[256,256]{1,0:T(8,128)S(1)}, f32[256,256]{1,0:T(8,128)S(1)}, u32[]{:S(2)}, u32[]{:S(2)}) collective-permute-start(f32[256,256]{1,0:T(8,128)S(1)} %add.239.refs_7_), channel_id=1, source_target_pairs={{0,1},{1,0},{2,3},{3,2},{4,5},{5,4},{6,7},{7,6},{8,9},{9,8},{10,11... | collective-permute-start | bytes 786440 | tf_op jit(solution)/shard_map/ppermute | solution.py:20
  149.6 15.5 %collective-permute-start.33 = (f32[256,256]{1,0:T(8,128)S(1)}, f32[256,256]{1,0:T(8,128)S(1)}, u32[]{:S(2)}, u32[]{:S(2)}) collective-permute-start(f32[256,256]{1,0:T(8,128)S(1)} %add.247.refs_4_), channel_id=1, source_target_pairs={{0,8},{4,12},{8,0},{12,4},{16,24},{20,28},{24,16},{28,20},{1,9},{5... | collective-permute-start | bytes 786440 | tf_op jit(solution)/shard_map/ppermute | solution.py:20
  185.3 15.9 %collective-permute-start.44 = (f32[320,256]{1,0:T(8,128)S(1)}, f32[320,256]{1,0:T(8,128)S(1)}, u32[]{:S(2)}, u32[]{:S(2)}) collective-permute-start(f32[320,256]{1,0:T(8,128)S(1)} %get-tuple-element.84), channel_id=1, source_target_pairs={{0,2},{1,3},{2,0},{3,1},{4,6},{5,7},{6,4},{7,5},{8,10},{9,11},{10,... | collective-permute-start | bytes 983048 | tf_op jit(solution)/shard_map/ppermute | solution.py:20
  186.5 15.5 %collective-permute-start.38 = (f32[320,256]{1,0:T(8,128)S(1)}, f32[320,256]{1,0:T(8,128)S(1)}, u32[]{:S(2)}, u32[]{:S(2)}) collective-permute-start(f32[320,256]{1,0:T(8,128)S(1)} %get-tuple-element.80), channel_id=1, source_target_pairs={{0,1},{1,0},{2,3},{3,2},{4,5},{5,4},{6,7},{7,6},{8,9},{9,8},{10,11... | collective-permute-start | bytes 983048 | tf_op jit(solution)/shard_map/ppermute | solution.py:20
  187.2 16.9 %collective-permute-start.40 = (f32[320,256]{1,0:T(8,128)S(1)}, f32[320,256]{1,0:T(8,128)S(1)}, u32[]{:S(2)}, u32[]{:S(2)}) collective-permute-start(f32[320,256]{1,0:T(8,128)S(1)} %get-tuple-element.81), channel_id=1, source_target_pairs={{0,1},{1,0},{2,3},{3,2},{4,5},{5,4},{6,7},{7,6},{8,9},{9,8},{10,11... | collective-permute-start | bytes 983048 | tf_op jit(solution)/shard_map/ppermute | solution.py:20
  195.1 16.0 %collective-permute-start.43 = (f32[320,256]{1,0:T(8,128)S(1)}, f32[320,256]{1,0:T(8,128)S(1)}, u32[]{:S(2)}, u32[]{:S(2)}) collective-permute-start(f32[320,256]{1,0:T(8,128)S(1)} %add.250.refs_5_), channel_id=1, source_target_pairs={{0,1},{1,0},{2,3},{3,2},{4,5},{5,4},{6,7},{7,6},{8,9},{9,8},{10,11... | collective-permute-start | bytes 983048 | tf_op jit(solution)/shard_map/ppermute | solution.py:20
  201.3 15.5 %collective-permute-start.45 = (f32[320,256]{1,0:T(8,128)S(1)}, f32[320,256]{1,0:T(8,128)S(1)}, u32[]{:S(2)}, u32[]{:S(2)}) collective-permute-start(f32[320,256]{1,0:T(8,128)S(1)} %add.251.refs_7_), channel_id=1, source_target_pairs={{0,1},{1,0},{2,3},{3,2},{4,5},{5,4},{6,7},{7,6},{8,9},{9,8},{10,11... | collective-permute-start | bytes 983048 | tf_op jit(solution)/shard_map/ppermute | solution.py:20
  202.1 14.7 %collective-permute-start.39 = (f32[320,256]{1,0:T(8,128)S(1)}, f32[320,256]{1,0:T(8,128)S(1)}, u32[]{:S(2)}, u32[]{:S(2)}) collective-permute-start(f32[320,256]{1,0:T(8,128)S(1)} %add.248.refs_1_), channel_id=1, source_target_pairs={{0,2},{1,3},{2,0},{3,1},{4,6},{5,7},{6,4},{7,5},{8,10},{9,11},{10,... | collective-permute-start | bytes 983048 | tf_op jit(solution)/shard_map/ppermute | solution.py:20
  240.9 16.3 %collective-permute-start.47 = (f32[320,256]{1,0:T(8,128)S(1)}, f32[320,256]{1,0:T(8,128)S(1)}, u32[]{:S(2)}, u32[]{:S(2)}) collective-permute-start(f32[320,256]{1,0:T(8,128)S(1)} %get-tuple-element.116), channel_id=1, source_target_pairs={{0,8},{4,12},{8,0},{12,4},{16,24},{20,28},{24,16},{28,20},{1,9},{5... | collective-permute-start | bytes 983048 | tf_op jit(solution)/shard_map/ppermute | solution.py:20
  241.3 16.1 %collective-permute-start.51 = (f32[320,256]{1,0:T(8,128)S(1)}, f32[320,256]{1,0:T(8,128)S(1)}, u32[]{:S(2)}, u32[]{:S(2)}) collective-permute-start(f32[320,256]{1,0:T(8,128)S(1)} %get-tuple-element.115), channel_id=1, source_target_pairs={{0,16},{4,20},{8,24},{12,28},{16,0},{20,4},{24,8},{28,12},{1,17},{... | collective-permute-start | bytes 983048 | tf_op jit(solution)/shard_map/ppermute | solution.py:20
  257.3 15.5 %collective-permute-start.48 = (f32[320,256]{1,0:T(8,128)S(1)}, f32[320,256]{1,0:T(8,128)S(1)}, u32[]{:S(2)}, u32[]{:S(2)}) collective-permute-start(f32[320,256]{1,0:T(8,128)S(1)} %fusion.1), channel_id=1, source_target_pairs={{0,16},{4,20},{8,24},{12,28},{16,0},{20,4},{24,8},{28,12},{1,17},{... | collective-permute-start | bytes 983048 | tf_op jit(solution)/shard_map/ppermute | solution.py:20
  257.5 17.7 %collective-permute-start.52 = (f32[320,256]{1,0:T(8,128)S(1)}, f32[320,256]{1,0:T(8,128)S(1)}, u32[]{:S(2)}, u32[]{:S(2)}) collective-permute-start(f32[320,256]{1,0:T(8,128)S(1)} %add.259.refs_3_), channel_id=1, source_target_pairs={{0,8},{4,12},{8,0},{12,4},{16,24},{20,28},{24,16},{28,20},{1,9},{5... | collective-permute-start | bytes 983048 | tf_op jit(solution)/shard_map/ppermute | solution.py:20
  296.1 16.6 %collective-permute-start.58 = (f32[256,256]{1,0:T(8,128)S(1)}, f32[256,256]{1,0:T(8,128)S(1)}, u32[]{:S(2)}, u32[]{:S(2)}) collective-permute-start(f32[256,256]{1,0:T(8,128)S(1)} %add.260.refs_9_), channel_id=1, source_target_pairs={{0,2},{1,3},{2,0},{3,1},{4,6},{5,7},{6,4},{7,5},{8,10},{9,11},{10,... | collective-permute-start | bytes 786440 | tf_op jit(solution)/shard_map/ppermute | solution.py:20
  300.9 16.1 %collective-permute-start.60 = (f32[256,256]{1,0:T(8,128)S(1)}, f32[256,256]{1,0:T(8,128)S(1)}, u32[]{:S(2)}, u32[]{:S(2)}) collective-permute-start(f32[256,256]{1,0:T(8,128)S(1)} %add.261.refs_11_), channel_id=1, source_target_pairs={{0,2},{1,3},{2,0},{3,1},{4,6},{5,7},{6,4},{7,5},{8,10},{9,11},{10,... | collective-permute-start | bytes 786440 | tf_op jit(solution)/shard_map/ppermute | solution.py:20
  302.3 14.6 %collective-permute-start.62 = (f32[256,256]{1,0:T(8,128)S(1)}, f32[256,256]{1,0:T(8,128)S(1)}, u32[]{:S(2)}, u32[]{:S(2)}) collective-permute-start(f32[256,256]{1,0:T(8,128)S(1)} %add.262.refs_13_), channel_id=1, source_target_pairs={{0,1},{1,0},{2,3},{3,2},{4,5},{5,4},{6,7},{7,6},{8,9},{9,8},{10,11... | collective-permute-start | bytes 786440 | tf_op jit(solution)/shard_map/ppermute | solution.py:20
  343.3 15.6 %collective-permute-start.71 = (f32[256,256]{1,0:T(8,128)S(1)}, f32[256,256]{1,0:T(8,128)S(1)}, u32[]{:S(2)}, u32[]{:S(2)}) collective-permute-start(f32[256,256]{1,0:T(8,128)S(1)} %add.271.refs_4_), channel_id=1, source_target_pairs={{0,8},{4,12},{8,0},{12,4},{16,24},{20,28},{24,16},{28,20},{1,9},{5... | collective-permute-start | bytes 786440 | tf_op jit(solution)/shard_map/ppermute | solution.py:20
  (83 other events, 939.9 us)

commit v3 on v2

--- a/solution.py
+++ b/solution.py
@@ -9,11 +9,11 @@
 
 F32 = jnp.float32
 BF16 = jnp.bfloat16
-CHAINS = 1
-Z_STREAMS = 2
-BLOCK_BYTES = 13 << 18
-CUTS = 2
-VMEM_LIMIT = 40 << 20
+CHAINS = 2
+Z_STREAMS = 1
+BLOCK_BYTES = 1 << 24
+CUTS = 1
+VMEM_LIMIT = 22 << 20
 
 
 def partner(x, axis, mask, n):
@@ -54,7 +54,6 @@
 
 
 def matmul(
-    name,
     meta,
     matrix,
     rows,
@@ -74,6 +73,7 @@
     blocks=1,
     cuts=1,
     order=None,
+    stay=False,
 ):
     depth = matrix.shape[2]
     chunk = pick_depth(rows * blocks, depth)
@@ -109,6 +109,7 @@
         acc = product(whole_a[0] if blocks == 1 else jnp.concatenate(whole_a, axis=0), part)
         if sign != 1.0:
             acc = -acc
+
         def write(ref, to, value, first):
             ref[to, :] = value if first else ref[to, :] + value
 
@@ -147,6 +148,8 @@
     out_shape += [jax.ShapeDtypeStruct(e, F32) for e in extra]
     out_specs = [whole(o.shape) for o in out_shape]
     scratch_shapes = list(scratch)
+    if stay:
+        matrix = pltpu.with_memory_space_constraint(matrix, pltpu.HBM)
     args = [matrix] * blocks + list(ins)
     specs = [
         pl.BlockSpec((1, rows, chunk), lambda g, k, m, q=q: (*index(q if groups == 1 else g, m), k))
@@ -179,11 +182,11 @@
             bytes_accessed=4 * groups * blocks * rows * depth,
             transcendentals=0,
         ),
-        name=name,
     )(meta, *args)
 
 
 def solve(
+    gate,
     n_sub,
     n_front,
     tables,
@@ -202,6 +205,8 @@
     root_upper,
 ):
     meta0, meta, at = tables
+    if gate:
+        leaf_rhs = lax.optimization_barrier((leaf_rhs, gate[0]))[0]
     width = leaf_rhs.shape[1]
     local = leaf_rhs.shape[0]
     fronts, mid_rows = mid_rhs.shape[0], mid_rhs.shape[1]
@@ -230,34 +235,39 @@
         terms = []
         for value in values:
             for m in masks[:-1]:
-                value = value + over_front(value, m)
+                got = over_front(value, m)
+                value = value + got
             terms += [value, over_front(value, masks[-1])]
         return terms
 
     top = z_bits - 1
     n_pieces = Z_STREAMS << top
 
-    def sum_subtree(send, keep):
-        got = over_sub(send, 1)
-        h = keep.shape[0] // Z_STREAMS
+    def sum_subtree(sends, keeps):
+        got = [over_sub(x, 1) for x in sends]
         mine, other = [], []
         for t in range(Z_STREAMS):
-            parts = [keep[t * h : (t + 1) * h], got[t * h : (t + 1) * h]]
+            if len(keeps) == Z_STREAMS:
+                parts = [keeps[t], got[t]]
+            else:
+                h = keeps[0].shape[0] // Z_STREAMS
+                parts = [x[0][t * h : (t + 1) * h] for x in (keeps, got)]
             for j in range(top):
                 n = parts[0].shape[0] // 2
                 leave = sum(x[:n] for x in parts)
-                parts = [sum(x[n:] for x in parts), over_sub(leave, z_masks[j])]
+                got_low = over_sub(leave, z_masks[j])
+                parts = [sum(x[n:] for x in parts), got_low]
             value = sum(parts)
-            value = value + over_sub(value, z_masks[top])
-            pieces = [value]
+            crossed = over_sub(value, z_masks[top])
+            pieces = [value + crossed]
             for j in reversed(range(top)):
                 pieces += [over_sub(p, z_masks[j]) for p in pieces]
             mine += pieces
             other += [over_sub(p, 1) for p in pieces]
         return mine, other
 
-    def leave_first(groups, rows):
-        per = n_pieces // groups
+    def leave_first(groups, rows, pieces=n_pieces):
+        per = pieces // groups
         size = rows // per
 
         def order(m, g):
@@ -280,7 +290,7 @@
                         start = start + ((z >> j) & 1) * (stream >> (j + 1))
                     yield (w * Z_STREAMS + t) * len(piece_bits) + n, start
 
-    def leaf_phase(name, meta_, matrix, ins, prologue, extra=()):
+    def leaf_phase(meta_, matrix, ins, prologue, extra=(), stay=False):
         early = max(n_front // 4, 1)
         spots = [[t * n_front + n for n in range(n_front)] for t in range(2)]
         calls = [spots[0][:early] + spots[1][:early], spots[0][early:] + spots[1][early:]]
@@ -291,9 +301,10 @@
                 return 0, m[at["order"] + chosen[q]]
 
             res = matmul(
-                f"{name}_{call}", meta_, matrix, half_leaf, 1, width, pick,
+                meta_, matrix, half_leaf, 1, width, pick,
                 ins if call == 0 else [], prologue=prologue, blocks=len(chosen),
                 extra=extra if call == 0 else (), keep_x2=call == 0, x2=x2,
+                stay=stay and call == 0,
             )
             made.update(zip(chosen, res))
             if call == 0:
@@ -309,12 +320,14 @@
         for t in range(2):
             put(x2, 0, t * half_leaf, live_rows(m, t, ins[0][pl.ds(t * half_leaf, half_leaf), :]))
 
-    terms, _ = leaf_phase("leaf_lower", meta0, leaf_lower, [leaf_rhs], pro)
+    terms, _ = leaf_phase(meta0, leaf_lower, [leaf_rhs], pro, stay=False)
 
     n_terms = f_bits + 1
 
     def total_of(refs, t, skip=0):
         return sum(r[...] for r in refs[skip + t * n_terms : skip + (t + 1) * n_terms])
+
+    gate.append(terms[0][-1])
 
     def pro(m, ins, extra, x2, _):
         for t in range(2):
@@ -322,7 +335,7 @@
             extra[0][pl.ds(t * half_leaf, half_leaf), :] = fwd
             put(x2, 0, t * half_leaf, fwd)
 
-    terms, (leaf_fwd,) = leaf_phase("leaf_below", meta0, leaf_below, terms[0] + terms[1], pro, [(local, width)])
+    terms, (leaf_fwd,) = leaf_phase(meta0, leaf_below, terms[0] + terms[1], pro, [(local, width)], stay=False)
     contrib = [-sum(terms[t]) for t in range(2)]
 
     pieces, offsets = [], []
@@ -333,75 +346,77 @@
         pieces += bufs
         offsets += [(t, o) for o in offs]
 
+    part = (half_fronts * mid_rows, width)
+
     def assemble(m, *refs):
-        ins, out = refs[:-1], refs[-1]
-        out[...] = jnp.zeros_like(out)
+        ins, outs = refs[:-2], refs[-2:]
+        for out in outs:
+            out[...] = jnp.zeros_like(out)
         for ref, (t, off) in zip(ins, offsets):
             leaf = m[at["self"]] ^ off
             for j in range(per_stream):
                 row = m[at["pivot"] + leaf * 2 * per_stream + t * per_stream + j]
 
-                @pl.when(row >= 0)
-                def _():
-                    rows = pl.ds(pl.multiple_of(row, sub), sub)
-                    out[rows, :] += ref[pl.ds(j * sub, sub), :]
+                for h, out in enumerate(outs):
+                    at_row = row - h * part[0]
+
+                    @pl.when((at_row >= 0) & (at_row < part[0]))
+                    def _():
+                        rows = pl.ds(pl.multiple_of(at_row, sub), sub)
+                        out[rows, :] += ref[pl.ds(j * sub, sub), :]
 
     pivot_mine = pl.pallas_call(
         assemble,
-        out_shape=jax.ShapeDtypeStruct((fronts * mid_rows, width), F32),
+        out_shape=[jax.ShapeDtypeStruct(part, F32)] * 2,
         grid_spec=pltpu.PrefetchScalarGridSpec(
             num_scalar_prefetch=1,
             grid=(1,),
             in_specs=[pl.BlockSpec(p.shape, lambda i, m: (0, 0)) for p in pieces],
-            out_specs=pl.BlockSpec((fronts * mid_rows, width), lambda i, m: (0, 0)),
+            out_specs=[pl.BlockSpec(part, lambda i, m: (0, 0))] * 2,
         ),
         compiler_params=pltpu.CompilerParams(vmem_limit_bytes=VMEM_LIMIT),
         name="pivot_rows",
     )(meta, *pieces)
-    pivot_other = over_sub(pivot_mine, 1)
+    pivot_other = [over_sub(x, 1) for x in pivot_mine]
     mid_flat = mid_rhs.reshape(fronts * mid_rows, width)
 
-    def front_products(name, matrix, prologue_of, ins_of, specs_of=None, extra_of=None):
+    def front_products(matrix, prologue, ins, extra=(), stay=False):
+        made, x2, extras = [], None, ()
+        for c in range(CUTS):
+            res = matmul(
+                meta, matrix, matrix.shape[1] // CUTS, fronts, width,
+                lambda g, m, c=c: (g, c), ins if c == 0 else [], prologue=prologue, slots=fronts,
+                extra=extra if c == 0 else (), x2=x2, keep_x2=c == 0, stay=stay and c == 0,
+            )
+            made.append(res[:fronts])
+            if c == 0:
+                extras, x2 = res[fronts:-1], res[-1]
         results = []
-        extras = None
         for t in range(2):
-            res = matmul(
-                f"{name}_{t}", meta, matrix, matrix.shape[1], half_fronts, width,
-                lambda g, m, t=t: (t * half_fronts + g, 0), ins_of(t, extras),
-                prologue=prologue_of(t), slots=half_fronts,
-                in_specs=specs_of(t) if specs_of else None,
-                extra=extra_of(t) if extra_of else (), cuts=CUTS,
-            )
-            n_parts = half_fronts * CUTS
-            if len(res) > n_parts:
-                extras = res[n_parts]
-            results.append(sum_front(res[:n_parts], f_masks[t]))
+            own = range(t * half_fronts, (t + 1) * half_fronts)
+            values = [made[c][p] for p in own for c in range(CUTS)]
+            results.append(sum_front(values, f_masks[t]))
         return results, extras
 
-    def pro_of(t):
-        def pro(m, ins, extra, x2, _):
-            for q in range(half_fronts):
-                rows = pl.ds(q * mid_rows, mid_rows)
-                put(x2, q, 0, ins[0][rows, :] + (ins[1][rows, :] + ins[2][rows, :]))
-
-        return pro
-
-    part = (half_fronts * mid_rows, width)
-    mid_fwd, _ = front_products(
-        "mid_lower", mid_lower, pro_of, lambda t, e: [mid_flat, pivot_mine, pivot_other],
-        specs_of=lambda t: [pl.BlockSpec(part, lambda g, k, m: (t, 0))] * 3,
-    )
-
-    def core_products(name, matrix, prologue_of, ins, finish_of=None, sign=1.0):
+    def pro(m, ins, extra, x2, _):
+        for p in range(fronts):
+            t, q = divmod(p, half_fronts)
+            rows = pl.ds(q * mid_rows, mid_rows)
+            value = ins[0][pl.ds(p * mid_rows, mid_rows), :] + (ins[1 + t][rows, :] + ins[3 + t][rows, :])
+            put(x2, p, 0, value)
+
+    mid_fwd, _ = front_products(mid_lower, pro, [mid_flat, *pivot_mine, *pivot_other], stay=False)
+
+    def core_products(matrix, prologue_of, ins, finish_of=None, sign=1.0):
         results = []
         for flip in (1, 0):
-            results += matmul(
-                f"{name}_{flip}", meta, matrix, matrix.shape[1], half_fronts, width,
+            results.append(matmul(
+                meta, matrix, matrix.shape[1], half_fronts, width,
                 lambda g, m, flip=flip: ((m[at["core"]] ^ flip) * half_fronts + g, 0), ins,
                 prologue=prologue_of(flip), slots=half_fronts, sign=sign,
                 finish=finish_of(flip) if finish_of else None,
                 order=leave_first(half_fronts, matrix.shape[1]),
-            )
+            ))
         return sum_subtree(*results)
 
     own_rows = mid_lower.shape[1]
@@ -436,9 +451,7 @@
         return finish
 
     fwd_terms = [*mid_fwd[0], *mid_fwd[1]]
-    mine, other = core_products(
-        "mid_below", mid_below, pro_of, fwd_terms + contrib, finish_of, sign=-1.0
-    )
+    mine, other = core_products(mid_below, pro_of, fwd_terms + contrib, finish_of, sign=-1.0)
 
     def root_pro(m, ins, extra, x2, scr):
         total = scr[0]
@@ -453,59 +466,54 @@
 
     out_rows = root_lower.shape[0] // 2
     matrix = root_lower[None]
-    *h0, x2 = matmul(
-        "root_lower_0", meta, matrix, out_rows, 1, width, lambda g, m: (0, 0),
-        [root_rhs, *mine, *other], prologue=root_pro, keep_x2=True,
-        scratch=[pltpu.VMEM((root_rows, width), F32)], cuts=CUTS,
-    )
-    root_fwd = sum_front(h0, f_masks[0])
-    h1 = matmul(
-        "root_lower_1", meta, matrix, out_rows, 1, width, lambda g, m: (0, 1), [], x2=x2,
-        cuts=CUTS,
-    )
-    root_fwd += sum_front(h1, f_masks[1])
+    made, x2 = [], None
+    for c in range(CUTS):
+        res = matmul(
+            meta, matrix, out_rows // CUTS, 1, width,
+            lambda q, m, c=c: (0, q * CUTS + c), [root_rhs, *mine, *other] if c == 0 else [],
+            prologue=root_pro, x2=x2, keep_x2=c == 0, blocks=2,
+            scratch=[pltpu.VMEM((root_rows, width), F32)] if c == 0 else [],
+        )
+        made.append(res[:2])
+        x2 = res[2] if c == 0 else x2
+    root_fwd = []
+    for t in range(2):
+        root_fwd += sum_front([made[c][t] for c in range(CUTS)], f_masks[t])
 
     def pro(m, ins, extra, x2, _):
         for n in range(2 * CUTS):
             put(x2, 0, n * (out_rows // CUTS), ins[2 * n][...] + ins[2 * n + 1][...])
 
+    matrix = root_upper[None]
     half_root = root_rows // 2
-    matrix = root_upper[None]
-    row_of = lambda flip: (lambda g, m: (0, m[at["core"]] ^ flip))
-    send, x2 = matmul(
-        "root_upper_1", meta, matrix, half_root, 1, width, row_of(1), root_fwd,
-        prologue=pro, keep_x2=True, order=leave_first(1, half_root),
-    )
-    (keep,) = matmul(
-        "root_upper_0", meta, matrix, half_root, 1, width, row_of(0), [], x2=x2,
-        order=leave_first(1, half_root),
-    )
-    mine, other = sum_subtree(send, keep)
+    up_rows = half_root // Z_STREAMS
+    sends, keeps, x2 = [], [], None
+    for t in range(Z_STREAMS):
+        for flip, into in ((1, sends), (0, keeps)):
+            res = matmul(
+                meta, matrix, up_rows, 1, width,
+                lambda g, m, t=t, flip=flip: (0, (m[at["core"]] ^ flip) * Z_STREAMS + t),
+                root_fwd if x2 is None else [], prologue=pro, x2=x2, keep_x2=x2 is None,
+                order=leave_first(1, up_rows, 1 << top),
+            )
+            into.append(res[0])
+            x2 = res[1] if x2 is None else x2
+    mine, other = sum_subtree(sends, keeps)
 
     def place(m, ins, out):
         for n, start in piece_starts(m, out.shape[0] // 2):
             h = ins[n].shape[0]
             out[pl.ds(pl.multiple_of(start, h), h), :] = ins[n][...]
 
-    def pro_of(t):
-        def pro(m, ins, extra, x2, _):
-            if t == 0:
-                place(m, ins, extra[0])
-                root = extra[0]
-            else:
-                root = ins[0]
-            for q in range(half_fronts):
-                for k in range(mid_width):
-                    slot = m[at["root"] + (t * half_fronts + q) * mid_width + k]
-                    rows = pl.ds(pl.multiple_of(slot * block, block), block)
-                    put(x2, q, k * block, root[rows, :])
-
-        return pro
-
-    mid_ext, root_sol = front_products(
-        "mid_right", mid_right, pro_of, lambda t, e: [*mine, *other] if t == 0 else [e],
-        extra_of=lambda t: [(root_rows, width)] if t == 0 else [],
-    )
+    def pro(m, ins, extra, x2, _):
+        place(m, ins, extra[0])
+        for p in range(fronts):
+            for k in range(mid_width):
+                slot = m[at["root"] + p * mid_width + k]
+                rows = pl.ds(pl.multiple_of(slot * block, block), block)
+                put(x2, p, k * block, extra[0][rows, :])
+
+    mid_ext, (root_sol,) = front_products(mid_right, pro, [*mine, *other], [(root_rows, width)])
     ext_terms = [*mid_ext[0], *mid_ext[1]]
 
     def pro_of(flip):
@@ -521,7 +529,7 @@
 
         return pro
 
-    mine, other = core_products("mid_upper", mid_upper, pro_of, fwd_terms + ext_terms)
+    mine, other = core_products(mid_upper, pro_of, fwd_terms + ext_terms)
 
     def pro(m, ins, extra, x2, _):
         place(m, ins, extra[0])
@@ -537,7 +545,7 @@
                 put(x2, 0, u * sub, ins[-1][rows, :])
 
     terms, (mid_sol,) = leaf_phase(
-        "leaf_right", meta, leaf_right, [*mine, *other, root_sol], pro,
+        meta, leaf_right, [*mine, *other, root_sol], pro,
         [(fronts * mid_rows, width)],
     )
 
@@ -546,7 +554,7 @@
             back = ins[0][pl.ds(t * half_leaf, half_leaf), :] - total_of(ins, t, 1)
             put(x2, 0, t * half_leaf, live_rows(m, t, back))
 
-    terms, _ = leaf_phase("leaf_upper", meta0, leaf_upper, [leaf_fwd, *terms[0], *terms[1]], pro)
+    terms, _ = leaf_phase(meta0, leaf_upper, [leaf_fwd, *terms[0], *terms[1]], pro)
     leaf_sol = jnp.concatenate([sum(terms[0]), sum(terms[1])], axis=0)
     ids = jnp.arange(local, dtype=jnp.int32)[:, None]
     leaf_sol = jnp.where(ids < meta0[at["live"]], leaf_sol, 0.0)
@@ -585,7 +593,6 @@
     leaf_width = local // block
     sub = min(block, local // 2)
     per_stream = (local // 2) // sub
-    leaves = leaf_map.shape[0]
     f_bits = n_front.bit_length() - 1
     masks = [1 << j for j in range(f_bits)]
     orders = [halving_order(masks), halving_order(masks[::-1])]
@@ -633,16 +640,17 @@
 
     width = scenarios // CHAINS
     results = []
+    gate = []
     for k in range(CHAINS):
         cols = slice(k * width, (k + 1) * width)
-        results.append(
-            solve(
-                n_sub, n_front, (meta0, meta, at),
-                leaf_rhs[0][:, cols], mid_rhs[:, :, cols], root_rhs[:, cols],
-                leaf_lower, leaf_below, leaf_right, leaf_upper,
-                mid_lower, mid_below, mid_right, mid_upper, root_lower, root_upper,
-            )
+        solved = solve(
+            gate,
+            n_sub, n_front, (meta0, meta, at),
+            leaf_rhs[0][:, cols], mid_rhs[:, :, cols], root_rhs[:, cols],
+            leaf_lower, leaf_below, leaf_right, leaf_upper,
+            mid_lower, mid_below, mid_right, mid_upper, root_lower, root_upper,
         )
+        results.append(solved)
     outs = [jnp.concatenate(r, axis=-1) if CHAINS > 1 else r[0] for r in zip(*results)]
     return outs[0][None], outs[1], outs[2]
 

time: 412 us -> 395 us (0.959); the launches traced: 411 us -> 387 us
  waiting for transfers between devices: 242 us -> 181 us
  starting transfers between devices: 94.5 us -> 111 us
  Pallas kernels: 56.3 us -> 69 us
  other arithmetic: 5.59 us -> 9.93 us
    ppermute x88 -> x124, waiting for transfers between devices: 242 us -> 181 us  [partner(): return lax.ppermute(x, axis, [(i, i ^ mask) for i in range(n)])]
    ppermute x88 -> x124, starting transfers between devices: 94.5 us -> 111 us  [partner(): return lax.ppermute(x, axis, [(i, i ^ mask) for i in range(n)])]
    pallas_call x20 -> x34, Pallas kernels: 54.1 us -> 67 us  [matmul(): pl.pallas_call(kernel, out_shape=out_shape, grid_spec=pltpu.PrefetchScala...]
  transfers between devices with their start and end apart: 88 -> 124, of which waited for: 57 -> 55; matrix products, arithmetic and copies ran while one was open for 1% -> 3% of each run, Pallas kernels for 5% -> 17%
where the time goes in v3:
time: 395 us; the launch traced here: 387 us
  waiting for transfers between devices  181 us (46%)
  starting transfers between devices  111 us (28%)
  Pallas kernels  69 us (17%)
  local copies, waits for them, and re-layouts  12.6 us (3%)
  other arithmetic  9.93 us (3%)
    ppermute x124, waiting for transfers between devices, partner(): return lax.ppermute(x, axis, [(i, i ^ mask) for i in range(n)])  181 us
    ppermute x124, starting transfers between devices, partner(): return lax.ppermute(x, axis, [(i, i ^ mask) for i in range(n)])  111 us
    pallas_call x34, Pallas kernels, matmul(): pl.pallas_call(kernel, out_shape=out_shape, grid_spec=pltpu.PrefetchScala...  67 us
  transfers between devices with their start and end apart: 124, of which 55 were waited for; matrix products, arithmetic and copies ran while one was open for 3% of the time, Pallas kernels for 17%

profile of v3, /device:TPU:0, one launch (start us, length us, event | category | flops | bytes accessed | tf_op | source)
XLA Modules:
  0.0 386.9 jit_solution(11193289170647508451)
XLA Ops:
  9.2 3.0 collective-permute-start
  49.4 3.1 collective-permute-done.65.refs_6_
  86.5 5.2 %collective-permute-done.77.refs_5_ = f32[256,128]{1,0:T(8,128)S(1)} collective-permute-done((f32[256,128]{1,0:T(8,128)S(1)}, f32[256,128]{1,0:T(8,128)S(1)}, u32[]{:S(2)}, u32[]{:S(2)}) %collective-permute-start.77) | collective-permute-done | bytes 131104 | tf_op jit(solution)/shard_map/ppermute | solution.py:20
  98.9 3.3 shard_map.215
  103.6 6.8 %collective-permute-done.20 = f32[512,128]{1,0:T(8,128)S(1)} collective-permute-done((f32[512,128]{1,0:T(8,128)S(1)}, f32[512,128]{1,0:T(8,128)S(1)}, u32[]{:S(2)}, u32[]{:S(2)}) %collective-permute-start.20) | collective-permute-done | bytes 262176 | tf_op jit(solution)/shard_map/ppermute | solution.py:20
  112.3 3.3 shard_map.232
  127.7 3.2 collective-permute-done.83.refs_2_
  135.7 6.6 %collective-permute-done.25 = f32[512,128]{1,0:T(8,128)S(1)} collective-permute-done((f32[512,128]{1,0:T(8,128)S(1)}, f32[512,128]{1,0:T(8,128)S(1)}, u32[]{:S(2)}, u32[]{:S(2)}) %collective-permute-start.25) | collective-permute-done | bytes 262176 | tf_op jit(solution)/shard_map/ppermute | solution.py:20
  144.6 12.1 %collective-permute-done.26 = f32[512,128]{1,0:T(8,128)S(1)} collective-permute-done((f32[512,128]{1,0:T(8,128)S(1)}, f32[512,128]{1,0:T(8,128)S(1)}, u32[]{:S(2)}, u32[]{:S(2)}) %collective-permute-start.26) | collective-permute-done | bytes 262176 | tf_op jit(solution)/shard_map/ppermute | solution.py:20
  159.1 10.2 %collective-permute-done.27.refs_4_ = f32[512,128]{1,0:T(8,128)S(1)} collective-permute-done((f32[512,128]{1,0:T(8,128)S(1)}, f32[512,128]{1,0:T(8,128)S(1)}, u32[]{:S(2)}, u32[]{:S(2)}) %collective-permute-start.27) | collective-permute-done | bytes 262176 | tf_op jit(solution)/shard_map/ppermute | solution.py:20
  171.9 5.6 %shard_map.218 = (f32[640,128]{1,0:T(8,128)S(1)}, f32[640,128]{1,0:T(8,128)S(1)}, bf16[1,2560,256]{2,1,0:T(8,128)(2,1)}) custom-call(s32[73]{0:T(128)S(1)} %concatenate.23.m.meta_ref, f32[1,1280,2560]{2,1,0:T(8,128)S(1)} %bitcast.37, f32[1,1280,2560]{2,1,0:T(8,128)S(1)} %bitcast.38, f32[2560,128]{1,0:T(8,128)S(1)} %get-tuple-element.205.refs_2_, ...), custom_call_target="tpu_custom_call" | custom-call | flops 2516582400 | bytes 13107200 | tf_op jit(solution)/shard_map/pallas_call | solution.py:167
  180.1 6.3 %collective-permute-done.30 = f32[640,128]{1,0:T(8,128)S(1)} collective-permute-done((f32[640,128]{1,0:T(8,128)S(1)}, f32[640,128]{1,0:T(8,128)S(1)}, u32[]{:S(2)}, u32[]{:S(2)}) %collective-permute-start.30) | collective-permute-done | bytes 327712 | tf_op jit(solution)/shard_map/ppermute | solution.py:20
  189.0 5.6 %shard_map.235 = (f32[640,128]{1,0:T(8,128)S(1)}, f32[640,128]{1,0:T(8,128)S(1)}, bf16[1,2560,256]{2,1,0:T(8,128)(2,1)}) custom-call(s32[73]{0:T(128)S(1)} %concatenate.23.m.meta_ref, f32[1,1280,2560]{2,1,0:T(8,128)S(1)} %bitcast.39, f32[1,1280,2560]{2,1,0:T(8,128)S(1)} %bitcast.40, f32[2560,128]{1,0:T(8,128)S(1)} %get-tuple-element.206.refs_2_, ...), custom_call_target="tpu_custom_call" | custom-call | flops 2516582400 | bytes 13107200 | tf_op jit(solution)/shard_map/pallas_call | solution.py:167
  199.4 3.7 collective-permute-done.92
  217.2 6.7 %collective-permute-done.35 = f32[640,128]{1,0:T(8,128)S(1)} collective-permute-done((f32[640,128]{1,0:T(8,128)S(1)}, f32[640,128]{1,0:T(8,128)S(1)}, u32[]{:S(2)}, u32[]{:S(2)}) %collective-permute-start.35) | collective-permute-done | bytes 327712 | tf_op jit(solution)/shard_map/ppermute | solution.py:20
  227.3 14.0 %collective-permute-done.36 = f32[640,128]{1,0:T(8,128)S(1)} collective-permute-done((f32[640,128]{1,0:T(8,128)S(1)}, f32[640,128]{1,0:T(8,128)S(1)}, u32[]{:S(2)}, u32[]{:S(2)}) %collective-permute-start.36) | collective-permute-done | bytes 327712 | tf_op jit(solution)/shard_map/ppermute | solution.py:20
  241.4 3.1 collective-permute-start.98
  244.6 12.6 %collective-permute-done.37.refs_2_ = f32[640,128]{1,0:T(8,128)S(1)} collective-permute-done((f32[640,128]{1,0:T(8,128)S(1)}, f32[640,128]{1,0:T(8,128)S(1)}, u32[]{:S(2)}, u32[]{:S(2)}) %collective-permute-start.37) | collective-permute-done | bytes 327712 | tf_op jit(solution)/shard_map/ppermute | solution.py:20
  259.6 3.3 shard_map.221
  273.4 3.3 shard_map.238
  287.8 3.4 collective-permute-done.103.refs_6_
  296.8 5.6 %collective-permute-done.45 = f32[512,128]{1,0:T(8,128)S(1)} collective-permute-done((f32[512,128]{1,0:T(8,128)S(1)}, f32[512,128]{1,0:T(8,128)S(1)}, u32[]{:S(2)}, u32[]{:S(2)}) %collective-permute-start.45) | collective-permute-done | bytes 262176 | tf_op jit(solution)/shard_map/ppermute | solution.py:20
  305.0 11.9 %collective-permute-done.46 = f32[512,128]{1,0:T(8,128)S(1)} collective-permute-done((f32[512,128]{1,0:T(8,128)S(1)}, f32[512,128]{1,0:T(8,128)S(1)}, u32[]{:S(2)}, u32[]{:S(2)}) %collective-permute-start.46) | collective-permute-done | bytes 262176 | tf_op jit(solution)/shard_map/ppermute | solution.py:20
  319.7 9.5 %collective-permute-done.47.refs_3_ = f32[512,128]{1,0:T(8,128)S(1)} collective-permute-done((f32[512,128]{1,0:T(8,128)S(1)}, f32[512,128]{1,0:T(8,128)S(1)}, u32[]{:S(2)}, u32[]{:S(2)}) %collective-permute-start.47) | collective-permute-done | bytes 262176 | tf_op jit(solution)/shard_map/ppermute | solution.py:20
  (401 shorter events, 232.3 us)
Async XLA Ops:
  43.7 15.6 %collective-permute-start.12 = (f32[256,128]{1,0:T(8,128)S(1)}, f32[256,128]{1,0:T(8,128)S(1)}, u32[]{:S(2)}, u32[]{:S(2)}) collective-permute-start(f32[256,128]{1,0:T(8,128)S(1)} %get-tuple-element.118), channel_id=1, source_target_pairs={{0,2},{1,3},{2,0},{3,1},{4,6},{5,7},{6,4},{7,5},{8,10},{9,11},{10,... | collective-permute-start | bytes 393224 | tf_op jit(solution)/shard_map/ppermute | solution.py:20
  45.8 14.1 %collective-permute-start.14 = (f32[256,128]{1,0:T(8,128)S(1)}, f32[256,128]{1,0:T(8,128)S(1)}, u32[]{:S(2)}, u32[]{:S(2)}) collective-permute-start(f32[256,128]{1,0:T(8,128)S(1)} %add.282), channel_id=1, source_target_pairs={{0,1},{1,0},{2,3},{3,2},{4,5},{5,4},{6,7},{7,6},{8,9},{9,8},{10,11... | collective-permute-start | bytes 393224 | tf_op jit(solution)/shard_map/ppermute | solution.py:20
  52.5 17.6 %collective-permute-start.9 = (f32[256,128]{1,0:T(8,128)S(1)}, f32[256,128]{1,0:T(8,128)S(1)}, u32[]{:S(2)}, u32[]{:S(2)}) collective-permute-start(f32[256,128]{1,0:T(8,128)S(1)} %add_negate_fusion.3.refs_0_.refs_5_), channel_id=1, source_target_pairs={{0,16},{4,20},{8,24},{12,28},{16,0},{20,4},{24,8},{28,12},{1,17},{... | collective-permute-start | bytes 393224 | tf_op jit(solution)/shard_map/ppermute | solution.py:20
  55.1 15.5 %collective-permute-start.10 = (f32[256,128]{1,0:T(8,128)S(1)}, f32[256,128]{1,0:T(8,128)S(1)}, u32[]{:S(2)}, u32[]{:S(2)}) collective-permute-start(f32[256,128]{1,0:T(8,128)S(1)} %add_negate_fusion.3.refs_0_.refs_5_), channel_id=1, source_target_pairs={{0,8},{4,12},{8,0},{12,4},{16,24},{20,28},{24,16},{28,20},{1,9},{5... | collective-permute-start | bytes 393224 | tf_op jit(solution)/shard_map/ppermute | solution.py:20
  81.6 17.2 %collective-permute-start.18 = (f32[1024,128]{1,0:T(8,128)S(1)}, f32[1024,128]{1,0:T(8,128)S(1)}, u32[]{:S(2)}, u32[]{:S(2)}) collective-permute-start(f32[1024,128]{1,0:T(8,128)S(1)} %get-tuple-element.121.refs_2_), channel_id=1, source_target_pairs={{0,4},{4,0},{8,12},{12,8},{16,20},{20,16},{24,28},{28,24},{1,5},{5... | collective-permute-start | bytes 1572872 | tf_op jit(solution)/shard_map/ppermute | solution.py:20
  81.7 17.1 %collective-permute-start.19 = (f32[1024,128]{1,0:T(8,128)S(1)}, f32[1024,128]{1,0:T(8,128)S(1)}, u32[]{:S(2)}, u32[]{:S(2)}) collective-permute-start(f32[1024,128]{1,0:T(8,128)S(1)} %get-tuple-element.122.refs_3_), channel_id=1, source_target_pairs={{0,4},{4,0},{8,12},{12,8},{16,20},{20,16},{24,28},{28,24},{1,5},{5... | collective-permute-start | bytes 1572872 | tf_op jit(solution)/shard_map/ppermute | solution.py:20
  98.3 14.0 %collective-permute-start.80 = (f32[1024,128]{1,0:T(8,128)S(1)}, f32[1024,128]{1,0:T(8,128)S(1)}, u32[]{:S(2)}, u32[]{:S(2)}) collective-permute-start(f32[1024,128]{1,0:T(8,128)S(1)} %get-tuple-element.170.refs_2_), channel_id=1, source_target_pairs={{0,4},{4,0},{8,12},{12,8},{16,20},{20,16},{24,28},{28,24},{1,5},{5... | collective-permute-start | bytes 1572872 | tf_op jit(solution)/shard_map/ppermute | solution.py:20
  98.3 13.9 %collective-permute-start.81 = (f32[1024,128]{1,0:T(8,128)S(1)}, f32[1024,128]{1,0:T(8,128)S(1)}, u32[]{:S(2)}, u32[]{:S(2)}) collective-permute-start(f32[1024,128]{1,0:T(8,128)S(1)} %get-tuple-element.171.refs_3_), channel_id=1, source_target_pairs={{0,4},{4,0},{8,12},{12,8},{16,20},{20,16},{24,28},{28,24},{1,5},{5... | collective-permute-start | bytes 1572872 | tf_op jit(solution)/shard_map/ppermute | solution.py:20
  142.3 14.4 %collective-permute-start.26 = (f32[512,128]{1,0:T(8,128)S(1)}, f32[512,128]{1,0:T(8,128)S(1)}, u32[]{:S(2)}, u32[]{:S(2)}) collective-permute-start(f32[512,128]{1,0:T(8,128)S(1)} %fusion.5), channel_id=1, source_target_pairs={{0,16},{4,20},{8,24},{12,28},{16,0},{20,4},{24,8},{28,12},{1,17},{... | collective-permute-start | bytes 786440 | tf_op jit(solution)/shard_map/ppermute | solution.py:20
  143.3 13.5 %collective-permute-start.87 = (f32[512,128]{1,0:T(8,128)S(1)}, f32[512,128]{1,0:T(8,128)S(1)}, u32[]{:S(2)}, u32[]{:S(2)}) collective-permute-start(f32[512,128]{1,0:T(8,128)S(1)} %slice_add_fusion.6), channel_id=1, source_target_pairs={{0,8},{4,12},{8,0},{12,4},{16,24},{20,28},{24,16},{28,20},{1,9},{5... | collective-permute-start | bytes 786440 | tf_op jit(solution)/shard_map/ppermute | solution.py:20
  156.9 14.9 %collective-permute-start.88 = (f32[512,128]{1,0:T(8,128)S(1)}, f32[512,128]{1,0:T(8,128)S(1)}, u32[]{:S(2)}, u32[]{:S(2)}) collective-permute-start(f32[512,128]{1,0:T(8,128)S(1)} %fusion.3), channel_id=1, source_target_pairs={{0,16},{4,20},{8,24},{12,28},{16,0},{20,4},{24,8},{28,12},{1,17},{... | collective-permute-start | bytes 786440 | tf_op jit(solution)/shard_map/ppermute | solution.py:20
  199.4 14.3 %collective-permute-start.34 = (f32[1280,128]{1,0:T(8,128)S(1)}, f32[1280,128]{1,0:T(8,128)S(1)}, u32[]{:S(2)}, u32[]{:S(2)}) collective-permute-start(f32[1280,128]{1,0:T(8,128)S(1)} %get-tuple-element.128), channel_id=1, source_target_pairs={{0,4},{4,0},{8,12},{12,8},{16,20},{20,16},{24,28},{28,24},{1,5},{5... | collective-permute-start | bytes 1966088 | tf_op jit(solution)/shard_map/ppermute | solution.py:20
  223.9 17.3 %collective-permute-start.36 = (f32[640,128]{1,0:T(8,128)S(1)}, f32[640,128]{1,0:T(8,128)S(1)}, u32[]{:S(2)}, u32[]{:S(2)}) collective-permute-start(f32[640,128]{1,0:T(8,128)S(1)} %fusion.1), channel_id=1, source_target_pairs={{0,16},{4,20},{8,24},{12,28},{16,0},{20,4},{24,8},{28,12},{1,17},{... | collective-permute-start | bytes 983048 | tf_op jit(solution)/shard_map/ppermute | solution.py:20
  225.5 15.9 %collective-permute-start.97 = (f32[640,128]{1,0:T(8,128)S(1)}, f32[640,128]{1,0:T(8,128)S(1)}, u32[]{:S(2)}, u32[]{:S(2)}) collective-permute-start(f32[640,128]{1,0:T(8,128)S(1)} %slice_add_fusion), channel_id=1, source_target_pairs={{0,8},{4,12},{8,0},{12,4},{16,24},{20,28},{24,16},{28,20},{1,9},{5... | collective-permute-start | bytes 983048 | tf_op jit(solution)/shard_map/ppermute | solution.py:20
  241.3 15.9 %collective-permute-start.37 = (f32[640,128]{1,0:T(8,128)S(1)}, f32[640,128]{1,0:T(8,128)S(1)}, u32[]{:S(2)}, u32[]{:S(2)}) collective-permute-start(f32[640,128]{1,0:T(8,128)S(1)} %add.295.refs_1_), channel_id=1, source_target_pairs={{0,8},{4,12},{8,0},{12,4},{16,24},{20,28},{24,16},{28,20},{1,9},{5... | collective-permute-start | bytes 983048 | tf_op jit(solution)/shard_map/ppermute | solution.py:20
  241.4 17.8 %collective-permute-start.98 = (f32[640,128]{1,0:T(8,128)S(1)}, f32[640,128]{1,0:T(8,128)S(1)}, u32[]{:S(2)}, u32[]{:S(2)}) collective-permute-start(f32[640,128]{1,0:T(8,128)S(1)} %fusion), channel_id=1, source_target_pairs={{0,16},{4,20},{8,24},{12,28},{16,0},{20,4},{24,8},{28,12},{1,17},{... | collective-permute-start | bytes 983048 | tf_op jit(solution)/shard_map/ppermute | solution.py:20
  244.6 15.0 %collective-permute-start.38 = (f32[640,128]{1,0:T(8,128)S(1)}, f32[640,128]{1,0:T(8,128)S(1)}, u32[]{:S(2)}, u32[]{:S(2)}) collective-permute-start(f32[640,128]{1,0:T(8,128)S(1)} %add.295.refs_1_), channel_id=1, source_target_pairs={{0,4},{4,0},{8,12},{12,8},{16,20},{20,16},{24,28},{28,24},{1,5},{5... | collective-permute-start | bytes 983048 | tf_op jit(solution)/shard_map/ppermute | solution.py:20
  302.5 14.4 %collective-permute-start.46 = (f32[512,128]{1,0:T(8,128)S(1)}, f32[512,128]{1,0:T(8,128)S(1)}, u32[]{:S(2)}, u32[]{:S(2)}) collective-permute-start(f32[512,128]{1,0:T(8,128)S(1)} %fusion.4), channel_id=1, source_target_pairs={{0,16},{4,20},{8,24},{12,28},{16,0},{20,4},{24,8},{28,12},{1,17},{... | collective-permute-start | bytes 786440 | tf_op jit(solution)/shard_map/ppermute | solution.py:20
  317.1 13.9 %collective-permute-start.108 = (f32[512,128]{1,0:T(8,128)S(1)}, f32[512,128]{1,0:T(8,128)S(1)}, u32[]{:S(2)}, u32[]{:S(2)}) collective-permute-start(f32[512,128]{1,0:T(8,128)S(1)} %fusion.2), channel_id=1, source_target_pairs={{0,16},{4,20},{8,24},{12,28},{16,0},{20,4},{24,8},{28,12},{1,17},{... | collective-permute-start | bytes 786440 | tf_op jit(solution)/shard_map/ppermute | solution.py:20
  337.6 13.8 %collective-permute-start.110 = (f32[512,128]{1,0:T(8,128)S(1)}, f32[512,128]{1,0:T(8,128)S(1)}, u32[]{:S(2)}, u32[]{:S(2)}) collective-permute-start(f32[512,128]{1,0:T(8,128)S(1)} %add.335.refs_2_), channel_id=1, source_target_pairs={{0,4},{4,0},{8,12},{12,8},{16,20},{20,16},{24,28},{28,24},{1,5},{5... | collective-permute-start | bytes 786440 | tf_op jit(solution)/shard_map/ppermute | solution.py:20
  338.1 13.4 %collective-permute-start.111 = (f32[512,128]{1,0:T(8,128)S(1)}, f32[512,128]{1,0:T(8,128)S(1)}, u32[]{:S(2)}, u32[]{:S(2)}) collective-permute-start(f32[512,128]{1,0:T(8,128)S(1)} %collective-permute-done.109.refs_3_), channel_id=1, source_target_pairs={{0,4},{4,0},{8,12},{12,8},{16,20},{20,16},{24,28},{28,24},{1,5},{5... | collective-permute-start | bytes 786440 | tf_op jit(solution)/shard_map/ppermute | solution.py:20
  349.3 13.5 %collective-permute-start.57 = (f32[256,128]{1,0:T(8,128)S(1)}, f32[256,128]{1,0:T(8,128)S(1)}, u32[]{:S(2)}, u32[]{:S(2)}) collective-permute-start(f32[256,128]{1,0:T(8,128)S(1)} %get-tuple-element.145), channel_id=1, source_target_pairs={{0,1},{1,0},{2,3},{3,2},{4,5},{5,4},{6,7},{7,6},{8,9},{9,8},{10,11... | collective-permute-start | bytes 393224 | tf_op jit(solution)/shard_map/ppermute | solution.py:20
  359.8 14.6 %collective-permute-start.59 = (f32[256,128]{1,0:T(8,128)S(1)}, f32[256,128]{1,0:T(8,128)S(1)}, u32[]{:S(2)}, u32[]{:S(2)}) collective-permute-start(f32[256,128]{1,0:T(8,128)S(1)} %get-tuple-element.147), channel_id=1, source_target_pairs={{0,2},{1,3},{2,0},{3,1},{4,6},{5,7},{6,4},{7,5},{8,10},{9,11},{10,... | collective-permute-start | bytes 393224 | tf_op jit(solution)/shard_map/ppermute | solution.py:20
  362.0 13.6 %collective-permute-start.61 = (f32[256,128]{1,0:T(8,128)S(1)}, f32[256,128]{1,0:T(8,128)S(1)}, u32[]{:S(2)}, u32[]{:S(2)}) collective-permute-start(f32[256,128]{1,0:T(8,128)S(1)} %add.308), channel_id=1, source_target_pairs={{0,1},{1,0},{2,3},{3,2},{4,5},{5,4},{6,7},{7,6},{8,9},{9,8},{10,11... | collective-permute-start | bytes 393224 | tf_op jit(solution)/shard_map/ppermute | solution.py:20
  (130 other events, 1288.0 us)

commit v4 on v3

--- a/solution.py
+++ b/solution.py
@@ -7,13 +7,14 @@
 from jax.experimental.pallas import tpu as pltpu
 from jax.sharding import PartitionSpec as P
 
+
 F32 = jnp.float32
 BF16 = jnp.bfloat16
-CHAINS = 2
-Z_STREAMS = 1
-BLOCK_BYTES = 1 << 24
-CUTS = 1
-VMEM_LIMIT = 22 << 20
+CHAINS = 1
+Z_STREAMS = 2
+BLOCK_BYTES = 13 << 18
+CUTS = 2
+VMEM_LIMIT = 40 << 20
 
 
 def partner(x, axis, mask, n):
@@ -186,7 +187,6 @@
 
 
 def solve(
-    gate,
     n_sub,
     n_front,
     tables,
@@ -205,8 +205,6 @@
     root_upper,
 ):
     meta0, meta, at = tables
-    if gate:
-        leaf_rhs = lax.optimization_barrier((leaf_rhs, gate[0]))[0]
     width = leaf_rhs.shape[1]
     local = leaf_rhs.shape[0]
     fronts, mid_rows = mid_rhs.shape[0], mid_rhs.shape[1]
@@ -320,14 +318,12 @@
         for t in range(2):
             put(x2, 0, t * half_leaf, live_rows(m, t, ins[0][pl.ds(t * half_leaf, half_leaf), :]))
 
-    terms, _ = leaf_phase(meta0, leaf_lower, [leaf_rhs], pro, stay=False)
+    terms, _ = leaf_phase(meta0, leaf_lower, [leaf_rhs], pro, stay=True)
 
     n_terms = f_bits + 1
 
     def total_of(refs, t, skip=0):
         return sum(r[...] for r in refs[skip + t * n_terms : skip + (t + 1) * n_terms])
-
-    gate.append(terms[0][-1])
 
     def pro(m, ins, extra, x2, _):
         for t in range(2):
@@ -335,7 +331,7 @@
             extra[0][pl.ds(t * half_leaf, half_leaf), :] = fwd
             put(x2, 0, t * half_leaf, fwd)
 
-    terms, (leaf_fwd,) = leaf_phase(meta0, leaf_below, terms[0] + terms[1], pro, [(local, width)], stay=False)
+    terms, (leaf_fwd,) = leaf_phase(meta0, leaf_below, terms[0] + terms[1], pro, [(local, width)], stay=True)
     contrib = [-sum(terms[t]) for t in range(2)]
 
     pieces, offsets = [], []
@@ -405,7 +401,7 @@
             value = ins[0][pl.ds(p * mid_rows, mid_rows), :] + (ins[1 + t][rows, :] + ins[3 + t][rows, :])
             put(x2, p, 0, value)
 
-    mid_fwd, _ = front_products(mid_lower, pro, [mid_flat, *pivot_mine, *pivot_other], stay=False)
+    mid_fwd, _ = front_products(mid_lower, pro, [mid_flat, *pivot_mine, *pivot_other], stay=True)
 
     def core_products(matrix, prologue_of, ins, finish_of=None, sign=1.0):
         results = []
@@ -640,11 +636,9 @@
 
     width = scenarios // CHAINS
     results = []
-    gate = []
     for k in range(CHAINS):
         cols = slice(k * width, (k + 1) * width)
         solved = solve(
-            gate,
             n_sub, n_front, (meta0, meta, at),
             leaf_rhs[0][:, cols], mid_rhs[:, :, cols], root_rhs[:, cols],
             leaf_lower, leaf_below, leaf_right, leaf_upper,

time: 395 us -> 410 us (1.038); the launches traced: 387 us -> 410 us
  waiting for transfers between devices: 181 us -> 245 us
  starting transfers between devices: 111 us -> 85.2 us
  local copies, waits for them, and re-layouts: 12.6 us -> 3.91 us
    ppermute x124 -> x90, waiting for transfers between devices: 181 us -> 245 us  [partner(): return lax.ppermute(x, axis, [(i, i ^ mask) for i in range(n)])]
    ppermute x124 -> x90, starting transfers between devices: 111 us -> 85.2 us  [partner(): return lax.ppermute(x, axis, [(i, i ^ mask) for i in range(n)])]
    unnamed x60 -> x32, local copies, waits for them, and re-layouts: 5.89 us -> 1.11 us
    pallas_call x34 -> x22, Pallas kernels: 67 us -> 63.2 us  [matmul(): pl.pallas_call(kernel, out_shape=out_shape, grid_spec=pltpu.PrefetchScala...]
  transfers between devices with their start and end apart: 124 -> 90, of which waited for: 55 -> 55; matrix products, arithmetic and copies ran while one was open for 3% -> 2% of each run, Pallas kernels for 17% -> 5%
where the time goes in v4:
time: 410 us
  waiting for transfers between devices  245 us (60%)
  starting transfers between devices  85.2 us (21%)
  Pallas kernels  65.5 us (16%)
  other arithmetic  7.13 us (2%)
    ppermute x90, waiting for transfers between devices, partner(): return lax.ppermute(x, axis, [(i, i ^ mask) for i in range(n)])  245 us
    ppermute x90, starting transfers between devices, partner(): return lax.ppermute(x, axis, [(i, i ^ mask) for i in range(n)])  85.2 us
    pallas_call x22, Pallas kernels, matmul(): pl.pallas_call(kernel, out_shape=out_shape, grid_spec=pltpu.PrefetchScala...  63.2 us
  transfers between devices with their start and end apart: 90, of which 55 were waited for; matrix products, arithmetic and copies ran while one was open for 2% of the time, Pallas kernels for 5%

profile of v4, /device:TPU:0, one launch (start us, length us, event | category | flops | bytes accessed | tf_op | source)
XLA Modules:
  0.0 409.6 jit_solution(16227042113407808736)
XLA Ops:
  57.2 10.0 %collective-permute-done.9.refs_1_ = f32[256,256]{1,0:T(8,128)S(1)} collective-permute-done((f32[256,256]{1,0:T(8,128)S(1)}, f32[256,256]{1,0:T(8,128)S(1)}, u32[]{:S(2)}, u32[]{:S(2)}) %collective-permute-start.9) | collective-permute-done | bytes 262176 | tf_op jit(solution)/shard_map/ppermute | solution.py:21
  72.1 5.6 %collective-permute-done.16.refs_6_ = f32[256,256]{1,0:T(8,128)} collective-permute-done((f32[256,256]{1,0:T(8,128)S(1)}, f32[256,256]{1,0:T(8,128)}, u32[]{:S(2)}, u32[]{:S(2)}) %collective-permute-start.16) | collective-permute-done | bytes 262176 | tf_op jit(solution)/shard_map/ppermute | solution.py:21
  101.1 5.1 %collective-permute-done.22 = f32[256,256]{1,0:T(8,128)S(1)} collective-permute-done((f32[256,256]{1,0:T(8,128)S(1)}, f32[256,256]{1,0:T(8,128)S(1)}, u32[]{:S(2)}, u32[]{:S(2)}) %collective-permute-start.22) | collective-permute-done | bytes 262176 | tf_op jit(solution)/shard_map/ppermute | solution.py:21
  114.0 4.6 %collective-permute-done.23.refs_4_ = f32[256,256]{1,0:T(8,128)S(1)} collective-permute-done((f32[256,256]{1,0:T(8,128)S(1)}, f32[256,256]{1,0:T(8,128)S(1)}, u32[]{:S(2)}, u32[]{:S(2)}) %collective-permute-start.23) | collective-permute-done | bytes 262176 | tf_op jit(solution)/shard_map/ppermute | solution.py:21
  128.3 7.7 %collective-permute-done.32 = f32[256,256]{1,0:T(8,128)S(1)} collective-permute-done((f32[256,256]{1,0:T(8,128)S(1)}, f32[256,256]{1,0:T(8,128)S(1)}, u32[]{:S(2)}, u32[]{:S(2)}) %collective-permute-start.32) | collective-permute-done | bytes 262176 | tf_op jit(solution)/shard_map/ppermute | solution.py:21
  139.7 9.5 %collective-permute-done.29 = f32[256,256]{1,0:T(8,128)S(1)} collective-permute-done((f32[256,256]{1,0:T(8,128)S(1)}, f32[256,256]{1,0:T(8,128)S(1)}, u32[]{:S(2)}, u32[]{:S(2)}) %collective-permute-start.29) | collective-permute-done | bytes 262176 | tf_op jit(solution)/shard_map/ppermute | solution.py:21
  149.4 7.0 %collective-permute-start.34 = (f32[256,256]{1,0:T(8,128)S(1)}, f32[256,256]{1,0:T(8,128)S(1)}, u32[]{:S(2)}, u32[]{:S(2)}) collective-permute-start(f32[256,256]{1,0:T(8,128)S(1)} %add.247.refs_5_), channel_id=1, source_target_pairs={{0,8},{4,12},{8,0},{12,4},{16,24},{20,28},{24,16},{28,20},{1,9},{5... | collective-permute-start | bytes 786440 | tf_op jit(solution)/shard_map/ppermute | solution.py:21
  156.4 5.7 %collective-permute-done.30 = f32[256,256]{1,0:T(8,128)S(1)} collective-permute-done((f32[256,256]{1,0:T(8,128)S(1)}, f32[256,256]{1,0:T(8,128)S(1)}, u32[]{:S(2)}, u32[]{:S(2)}) %collective-permute-start.30) | collective-permute-done | bytes 262176 | tf_op jit(solution)/shard_map/ppermute | solution.py:21
  164.7 5.8 %collective-permute-done.31.refs_4_ = f32[256,256]{1,0:T(8,128)S(1)} collective-permute-done((f32[256,256]{1,0:T(8,128)S(1)}, f32[256,256]{1,0:T(8,128)S(1)}, u32[]{:S(2)}, u32[]{:S(2)}) %collective-permute-start.31) | collective-permute-done | bytes 262176 | tf_op jit(solution)/shard_map/ppermute | solution.py:21
  172.0 6.7 %shard_map.219 = (f32[320,256]{1,0:T(8,128)S(1)}, f32[320,256]{1,0:T(8,128)S(1)}, bf16[1,2560,512]{2,1,0:T(8,128)(2,1)S(1)}) custom-call(s32[73]{0:T(128)S(1)} %concatenate.22.m.meta_ref, f32[1,1280,2560]{2,1,0:T(8,128)} %bitcast.35, f32[1,1280,2560]{2,1,0:T(8,128)} %bitcast.36, f32[2560,256]{1,0:T(8,128)S(1)} %copy-done.8, f32[256,256]{1,0:T(8,128)S(1)} %add.243.refs_3_, ...), custom_call_target="tpu_custom_call" | custom-call | flops 2516582400 | bytes 6553600 | tf_op jit(solution)/shard_map/pallas_call | solution.py:168
  178.8 5.5 %shard_map.220 = (f32[320,256]{1,0:T(8,128)S(1)}, f32[320,256]{1,0:T(8,128)S(1)}) custom-call(s32[73]{0:T(128)S(1)} %concatenate.22.m.meta_ref, f32[1,1280,2560]{2,1,0:T(8,128)} %bitcast.37, f32[1,1280,2560]{2,1,0:T(8,128)} %bitcast.38, bf16[1,2560,512]{2,1,0:T(8,128)(2,1)S(1)} %get-tuple-element.88.refs_2_), custom_call_target="tpu_custom_call" | custom-call | flops 2516582400 | bytes 6553600 | tf_op jit(solution)/shard_map/pallas_call | solution.py:168
  188.4 6.5 %collective-permute-done.41 = f32[320,256]{1,0:T(8,128)S(1)} collective-permute-done((f32[320,256]{1,0:T(8,128)S(1)}, f32[320,256]{1,0:T(8,128)S(1)}, u32[]{:S(2)}, u32[]{:S(2)}) %collective-permute-start.41) | collective-permute-done | bytes 327712 | tf_op jit(solution)/shard_map/ppermute | solution.py:21
  204.6 5.3 %collective-permute-done.42.refs_4_ = f32[320,256]{1,0:T(8,128)S(1)} collective-permute-done((f32[320,256]{1,0:T(8,128)S(1)}, f32[320,256]{1,0:T(8,128)S(1)}, u32[]{:S(2)}, u32[]{:S(2)}) %collective-permute-start.42) | collective-permute-done | bytes 327712 | tf_op jit(solution)/shard_map/ppermute | solution.py:21
  209.9 5.9 %collective-permute-done.40.refs_2_ = f32[320,256]{1,0:T(8,128)S(1)} collective-permute-done((f32[320,256]{1,0:T(8,128)S(1)}, f32[320,256]{1,0:T(8,128)S(1)}, u32[]{:S(2)}, u32[]{:S(2)}) %collective-permute-start.40) | collective-permute-done | bytes 327712 | tf_op jit(solution)/shard_map/ppermute | solution.py:21
  240.2 9.9 %collective-permute-done.48 = f32[320,256]{1,0:T(8,128)S(1)} collective-permute-done((f32[320,256]{1,0:T(8,128)S(1)}, f32[320,256]{1,0:T(8,128)S(1)}, u32[]{:S(2)}, u32[]{:S(2)}) %collective-permute-start.48) | collective-permute-done | bytes 327712 | tf_op jit(solution)/shard_map/ppermute | solution.py:21
  250.3 13.6 %collective-permute-done.53 = f32[320,256]{1,0:T(8,128)S(1)} collective-permute-done((f32[320,256]{1,0:T(8,128)S(1)}, f32[320,256]{1,0:T(8,128)S(1)}, u32[]{:S(2)}, u32[]{:S(2)}) %collective-permute-start.53) | collective-permute-done | bytes 327712 | tf_op jit(solution)/shard_map/ppermute | solution.py:21
  269.8 6.3 %collective-permute-done.54.refs_4_ = f32[320,256]{1,0:T(8,128)S(1)} collective-permute-done((f32[320,256]{1,0:T(8,128)S(1)}, f32[320,256]{1,0:T(8,128)S(1)}, u32[]{:S(2)}, u32[]{:S(2)}) %collective-permute-start.54) | collective-permute-done | bytes 327712 | tf_op jit(solution)/shard_map/ppermute | solution.py:21
  276.1 6.9 %collective-permute-done.50.refs_2_ = f32[320,256]{1,0:T(8,128)S(1)} collective-permute-done((f32[320,256]{1,0:T(8,128)S(1)}, f32[320,256]{1,0:T(8,128)S(1)}, u32[]{:S(2)}, u32[]{:S(2)}) %collective-permute-start.50) | collective-permute-done | bytes 327712 | tf_op jit(solution)/shard_map/ppermute | solution.py:21
  294.5 5.1 %collective-permute-done.61 = f32[256,256]{1,0:T(8,128)S(1)} collective-permute-done((f32[256,256]{1,0:T(8,128)S(1)}, f32[256,256]{1,0:T(8,128)S(1)}, u32[]{:S(2)}, u32[]{:S(2)}) %collective-permute-start.61) | collective-permute-done | bytes 262176 | tf_op jit(solution)/shard_map/ppermute | solution.py:21
  307.4 4.6 %collective-permute-done.62.refs_12_ = f32[256,256]{1,0:T(8,128)S(1)} collective-permute-done((f32[256,256]{1,0:T(8,128)S(1)}, f32[256,256]{1,0:T(8,128)S(1)}, u32[]{:S(2)}, u32[]{:S(2)}) %collective-permute-start.62) | collective-permute-done | bytes 262176 | tf_op jit(solution)/shard_map/ppermute | solution.py:21
  321.0 8.3 %collective-permute-done.71 = f32[256,256]{1,0:T(8,128)S(1)} collective-permute-done((f32[256,256]{1,0:T(8,128)S(1)}, f32[256,256]{1,0:T(8,128)S(1)}, u32[]{:S(2)}, u32[]{:S(2)}) %collective-permute-start.71) | collective-permute-done | bytes 262176 | tf_op jit(solution)/shard_map/ppermute | solution.py:21
  332.7 9.9 %collective-permute-done.68 = f32[256,256]{1,0:T(8,128)S(1)} collective-permute-done((f32[256,256]{1,0:T(8,128)S(1)}, f32[256,256]{1,0:T(8,128)S(1)}, u32[]{:S(2)}, u32[]{:S(2)}) %collective-permute-start.68) | collective-permute-done | bytes 262176 | tf_op jit(solution)/shard_map/ppermute | solution.py:21
  344.6 10.7 %collective-permute-done.69 = f32[256,256]{1,0:T(8,128)S(1)} collective-permute-done((f32[256,256]{1,0:T(8,128)S(1)}, f32[256,256]{1,0:T(8,128)S(1)}, u32[]{:S(2)}, u32[]{:S(2)}) %collective-permute-start.69) | collective-permute-done | bytes 262176 | tf_op jit(solution)/shard_map/ppermute | solution.py:21
  356.1 7.5 %collective-permute-done.70.refs_3_ = f32[256,256]{1,0:T(8,128)S(1)} collective-permute-done((f32[256,256]{1,0:T(8,128)S(1)}, f32[256,256]{1,0:T(8,128)S(1)}, u32[]{:S(2)}, u32[]{:S(2)}) %collective-permute-start.70) | collective-permute-done | bytes 262176 | tf_op jit(solution)/shard_map/ppermute | solution.py:21
  (270 shorter events, 232.8 us)
Async XLA Ops:
  49.8 17.4 %collective-permute-start.9 = (f32[256,256]{1,0:T(8,128)S(1)}, f32[256,256]{1,0:T(8,128)S(1)}, u32[]{:S(2)}, u32[]{:S(2)}) collective-permute-start(f32[256,256]{1,0:T(8,128)S(1)} %add_negate_fusion.1.refs_0_.refs_9_), channel_id=1, source_target_pairs={{0,16},{4,20},{8,24},{12,28},{16,0},{20,4},{24,8},{28,12},{1,17},{... | collective-permute-start | bytes 786440 | tf_op jit(solution)/shard_map/ppermute | solution.py:21
  53.5 17.0 %collective-permute-start.15 = (f32[256,256]{1,0:T(8,128)S(1)}, f32[256,256]{1,0:T(8,128)}, u32[]{:S(2)}, u32[]{:S(2)}) collective-permute-start(f32[256,256]{1,0:T(8,128)S(1)} %add_negate_fusion.refs_4_.refs_10_), channel_id=1, source_target_pairs={{0,16},{4,20},{8,24},{12,28},{16,0},{20,4},{24,8},{28,12},{1,17},{... | collective-permute-start | bytes 786440 | tf_op jit(solution)/shard_map/ppermute | solution.py:21
  55.1 17.0 %collective-permute-start.10 = (f32[256,256]{1,0:T(8,128)S(1)}, f32[256,256]{1,0:T(8,128)}, u32[]{:S(2)}, u32[]{:S(2)}) collective-permute-start(f32[256,256]{1,0:T(8,128)S(1)} %add_negate_fusion.1.refs_0_.refs_9_), channel_id=1, source_target_pairs={{0,8},{4,12},{8,0},{12,4},{16,24},{20,28},{24,16},{28,20},{1,9},{5... | collective-permute-start | bytes 786440 | tf_op jit(solution)/shard_map/ppermute | solution.py:21
  56.7 21.0 %collective-permute-start.16 = (f32[256,256]{1,0:T(8,128)S(1)}, f32[256,256]{1,0:T(8,128)}, u32[]{:S(2)}, u32[]{:S(2)}) collective-permute-start(f32[256,256]{1,0:T(8,128)S(1)} %add_negate_fusion.refs_4_.refs_10_), channel_id=1, source_target_pairs={{0,8},{4,12},{8,0},{12,4},{16,24},{20,28},{24,16},{28,20},{1,9},{5... | collective-permute-start | bytes 786440 | tf_op jit(solution)/shard_map/ppermute | solution.py:21
  67.2 14.9 %collective-permute-start.11 = (f32[256,256]{1,0:T(8,128)S(1)}, f32[256,256]{1,0:T(8,128)}, u32[]{:S(2)}, u32[]{:S(2)}) collective-permute-start(f32[256,256]{1,0:T(8,128)S(1)} %collective-permute-done.9.refs_1_), channel_id=1, source_target_pairs={{0,8},{4,12},{8,0},{12,4},{16,24},{20,28},{24,16},{28,20},{1,9},{5... | collective-permute-start | bytes 786440 | tf_op jit(solution)/shard_map/ppermute | solution.py:21
  70.5 14.3 %collective-permute-start.17 = (f32[256,256]{1,0:T(8,128)}, f32[256,256]{1,0:T(8,128)}, u32[]{:S(2)}, u32[]{:S(2)}) collective-permute-start(f32[256,256]{1,0:T(8,128)} %collective-permute-done.15.refs_5_), channel_id=1, source_target_pairs={{0,8},{4,12},{8,0},{12,4},{16,24},{20,28},{24,16},{28,20},{1,9},{5... | collective-permute-start | bytes 786440 | tf_op jit(solution)/shard_map/ppermute | solution.py:21
  136.1 13.2 %collective-permute-start.29 = (f32[256,256]{1,0:T(8,128)S(1)}, f32[256,256]{1,0:T(8,128)S(1)}, u32[]{:S(2)}, u32[]{:S(2)}) collective-permute-start(f32[256,256]{1,0:T(8,128)S(1)} %get-tuple-element.126), channel_id=1, source_target_pairs={{0,8},{4,12},{8,0},{12,4},{16,24},{20,28},{24,16},{28,20},{1,9},{5... | collective-permute-start | bytes 786440 | tf_op jit(solution)/shard_map/ppermute | solution.py:21
  149.3 12.9 %collective-permute-start.30 = (f32[256,256]{1,0:T(8,128)S(1)}, f32[256,256]{1,0:T(8,128)S(1)}, u32[]{:S(2)}, u32[]{:S(2)}) collective-permute-start(f32[256,256]{1,0:T(8,128)S(1)} %fusion.5), channel_id=1, source_target_pairs={{0,16},{4,20},{8,24},{12,28},{16,0},{20,4},{24,8},{28,12},{1,17},{... | collective-permute-start | bytes 786440 | tf_op jit(solution)/shard_map/ppermute | solution.py:21
  149.4 15.2 %collective-permute-start.34 = (f32[256,256]{1,0:T(8,128)S(1)}, f32[256,256]{1,0:T(8,128)S(1)}, u32[]{:S(2)}, u32[]{:S(2)}) collective-permute-start(f32[256,256]{1,0:T(8,128)S(1)} %add.247.refs_5_), channel_id=1, source_target_pairs={{0,8},{4,12},{8,0},{12,4},{16,24},{20,28},{24,16},{28,20},{1,9},{5... | collective-permute-start | bytes 786440 | tf_op jit(solution)/shard_map/ppermute | solution.py:21
  186.8 15.2 %collective-permute-start.39 = (f32[320,256]{1,0:T(8,128)S(1)}, f32[320,256]{1,0:T(8,128)S(1)}, u32[]{:S(2)}, u32[]{:S(2)}) collective-permute-start(f32[320,256]{1,0:T(8,128)S(1)} %get-tuple-element.87), channel_id=1, source_target_pairs={{0,1},{1,0},{2,3},{3,2},{4,5},{5,4},{6,7},{7,6},{8,9},{9,8},{10,11... | collective-permute-start | bytes 983048 | tf_op jit(solution)/shard_map/ppermute | solution.py:21
  187.2 15.7 %collective-permute-start.43 = (f32[320,256]{1,0:T(8,128)S(1)}, f32[320,256]{1,0:T(8,128)S(1)}, u32[]{:S(2)}, u32[]{:S(2)}) collective-permute-start(f32[320,256]{1,0:T(8,128)S(1)} %get-tuple-element.90), channel_id=1, source_target_pairs={{0,2},{1,3},{2,0},{3,1},{4,6},{5,7},{6,4},{7,5},{8,10},{9,11},{10,... | collective-permute-start | bytes 983048 | tf_op jit(solution)/shard_map/ppermute | solution.py:21
  195.0 14.9 %collective-permute-start.42 = (f32[320,256]{1,0:T(8,128)S(1)}, f32[320,256]{1,0:T(8,128)S(1)}, u32[]{:S(2)}, u32[]{:S(2)}) collective-permute-start(f32[320,256]{1,0:T(8,128)S(1)} %add.249.refs_3_), channel_id=1, source_target_pairs={{0,2},{1,3},{2,0},{3,1},{4,6},{5,7},{6,4},{7,5},{8,10},{9,11},{10,... | collective-permute-start | bytes 983048 | tf_op jit(solution)/shard_map/ppermute | solution.py:21
  196.0 13.9 %collective-permute-start.46 = (f32[320,256]{1,0:T(8,128)S(1)}, f32[320,256]{1,0:T(8,128)S(1)}, u32[]{:S(2)}, u32[]{:S(2)}) collective-permute-start(f32[320,256]{1,0:T(8,128)S(1)} %add.251.refs_7_), channel_id=1, source_target_pairs={{0,1},{1,0},{2,3},{3,2},{4,5},{5,4},{6,7},{7,6},{8,9},{9,8},{10,11... | collective-permute-start | bytes 983048 | tf_op jit(solution)/shard_map/ppermute | solution.py:21
  202.0 13.8 %collective-permute-start.40 = (f32[320,256]{1,0:T(8,128)S(1)}, f32[320,256]{1,0:T(8,128)S(1)}, u32[]{:S(2)}, u32[]{:S(2)}) collective-permute-start(f32[320,256]{1,0:T(8,128)S(1)} %add.248.refs_1_), channel_id=1, source_target_pairs={{0,2},{1,3},{2,0},{3,1},{4,6},{5,7},{6,4},{7,5},{8,10},{9,11},{10,... | collective-permute-start | bytes 983048 | tf_op jit(solution)/shard_map/ppermute | solution.py:21
  232.6 17.6 %collective-permute-start.48 = (f32[320,256]{1,0:T(8,128)S(1)}, f32[320,256]{1,0:T(8,128)S(1)}, u32[]{:S(2)}, u32[]{:S(2)}) collective-permute-start(f32[320,256]{1,0:T(8,128)S(1)} %slice_add_fusion.2), channel_id=1, source_target_pairs={{0,8},{4,12},{8,0},{12,4},{16,24},{20,28},{24,16},{28,20},{1,9},{5... | collective-permute-start | bytes 983048 | tf_op jit(solution)/shard_map/ppermute | solution.py:21
  239.0 25.0 %collective-permute-start.53 = (f32[320,256]{1,0:T(8,128)S(1)}, f32[320,256]{1,0:T(8,128)S(1)}, u32[]{:S(2)}, u32[]{:S(2)}) collective-permute-start(f32[320,256]{1,0:T(8,128)S(1)} %fusion), channel_id=1, source_target_pairs={{0,16},{4,20},{8,24},{12,28},{16,0},{20,4},{24,8},{28,12},{1,17},{... | collective-permute-start | bytes 983048 | tf_op jit(solution)/shard_map/ppermute | solution.py:21
  250.2 18.8 %collective-permute-start.49 = (f32[320,256]{1,0:T(8,128)S(1)}, f32[320,256]{1,0:T(8,128)S(1)}, u32[]{:S(2)}, u32[]{:S(2)}) collective-permute-start(f32[320,256]{1,0:T(8,128)S(1)} %fusion.1), channel_id=1, source_target_pairs={{0,16},{4,20},{8,24},{12,28},{16,0},{20,4},{24,8},{28,12},{1,17},{... | collective-permute-start | bytes 983048 | tf_op jit(solution)/shard_map/ppermute | solution.py:21
  269.1 13.9 %collective-permute-start.50 = (f32[320,256]{1,0:T(8,128)S(1)}, f32[320,256]{1,0:T(8,128)S(1)}, u32[]{:S(2)}, u32[]{:S(2)}) collective-permute-start(f32[320,256]{1,0:T(8,128)S(1)} %add.255.refs_1_), channel_id=1, source_target_pairs={{0,8},{4,12},{8,0},{12,4},{16,24},{20,28},{24,16},{28,20},{1,9},{5... | collective-permute-start | bytes 983048 | tf_op jit(solution)/shard_map/ppermute | solution.py:21
  269.2 13.8 %collective-permute-start.57 = (f32[320,256]{1,0:T(8,128)S(1)}, f32[320,256]{1,0:T(8,128)S(1)}, u32[]{:S(2)}, u32[]{:S(2)}) collective-permute-start(f32[320,256]{1,0:T(8,128)S(1)} %add.259.refs_3_), channel_id=1, source_target_pairs={{0,4},{4,0},{8,12},{12,8},{16,20},{20,16},{24,28},{28,24},{1,5},{5... | collective-permute-start | bytes 983048 | tf_op jit(solution)/shard_map/ppermute | solution.py:21
  269.3 13.8 %collective-permute-start.55 = (f32[320,256]{1,0:T(8,128)S(1)}, f32[320,256]{1,0:T(8,128)S(1)}, u32[]{:S(2)}, u32[]{:S(2)}) collective-permute-start(f32[320,256]{1,0:T(8,128)S(1)} %add.255.refs_1_), channel_id=1, source_target_pairs={{0,4},{4,0},{8,12},{12,8},{16,20},{20,16},{24,28},{28,24},{1,5},{5... | collective-permute-start | bytes 983048 | tf_op jit(solution)/shard_map/ppermute | solution.py:21
  294.0 12.9 %collective-permute-start.63 = (f32[256,256]{1,0:T(8,128)S(1)}, f32[256,256]{1,0:T(8,128)S(1)}, u32[]{:S(2)}, u32[]{:S(2)}) collective-permute-start(f32[256,256]{1,0:T(8,128)S(1)} %get-tuple-element.97), channel_id=1, source_target_pairs={{0,2},{1,3},{2,0},{3,1},{4,6},{5,7},{6,4},{7,5},{8,10},{9,11},{10,... | collective-permute-start | bytes 786440 | tf_op jit(solution)/shard_map/ppermute | solution.py:21
  329.4 13.2 %collective-permute-start.68 = (f32[256,256]{1,0:T(8,128)S(1)}, f32[256,256]{1,0:T(8,128)S(1)}, u32[]{:S(2)}, u32[]{:S(2)}) collective-permute-start(f32[256,256]{1,0:T(8,128)S(1)} %get-tuple-element.124), channel_id=1, source_target_pairs={{0,8},{4,12},{8,0},{12,4},{16,24},{20,28},{24,16},{28,20},{1,9},{5... | collective-permute-start | bytes 786440 | tf_op jit(solution)/shard_map/ppermute | solution.py:21
  329.7 13.0 %collective-permute-start.72 = (f32[256,256]{1,0:T(8,128)S(1)}, f32[256,256]{1,0:T(8,128)S(1)}, u32[]{:S(2)}, u32[]{:S(2)}) collective-permute-start(f32[256,256]{1,0:T(8,128)S(1)} %get-tuple-element.123), channel_id=1, source_target_pairs={{0,16},{4,20},{8,24},{12,28},{16,0},{20,4},{24,8},{28,12},{1,17},{... | collective-permute-start | bytes 786440 | tf_op jit(solution)/shard_map/ppermute | solution.py:21
  342.8 13.3 %collective-permute-start.73 = (f32[256,256]{1,0:T(8,128)S(1)}, f32[256,256]{1,0:T(8,128)S(1)}, u32[]{:S(2)}, u32[]{:S(2)}) collective-permute-start(f32[256,256]{1,0:T(8,128)S(1)} %add.271.refs_4_), channel_id=1, source_target_pairs={{0,8},{4,12},{8,0},{12,4},{16,24},{20,28},{24,16},{28,20},{1,9},{5... | collective-permute-start | bytes 786440 | tf_op jit(solution)/shard_map/ppermute | solution.py:21
  (82 other events, 956.0 us)
